TPU v7x, 256 devices: a whole 4x4x8 slice. The times are simulated.
256 devices in a mesh: dp: 32 (over x, z), ctx: 8 (over y, core).
Axes of the slice: x: 4, y: 4, z: 8, core: 2. Of those that a mesh axis runs over, the one named last changes fastest.
Arguments:
- layer_input: bfloat16 [32, 1024, 4096], P('dp', 'ctx'), may hold values from -6 to 6
- queries: bfloat16 [32, 1024, 4096], P('dp', 'ctx'), may hold values from -4.5 to 4.5
- keys_saved: bfloat16 [32, 1024, 1024], P('dp', 'ctx'), may hold values from -4.5 to 4.5
- values_saved: bfloat16 [32, 1024, 1024], P('dp', 'ctx'), may hold values from -6 to 6
- out_grad: bfloat16 [32, 1024, 4096], P('dp', 'ctx'), may hold values from -6 to 6
- master_weight: float32 [4096, 6144], P('dp', 'ctx'), may hold values from -2 to 2
- first_moment: float32 [4096, 6144], P('dp', 'ctx'), may hold values from -100 to 100
- second_moment: float32 [4096, 6144], P('dp', 'ctx'), may hold values from 10 to 3000
Outputs:
- first_new: float32 [4096, 6144], P('dp', 'ctx')
- second_new: float32 [4096, 6144], P('dp', 'ctx')
- lamb_update: float32 [4096, 6144], P('dp', 'ctx')
- new_weights: bfloat16 [4096, 6144], P(None, 'ctx')
All inputs are finite; a program needn't handle non-finite values.
Results may differ from a plain program's by a relative error of at most 0.0095.
Values may be sent and summed in bfloat16 or wider, within the bound.
No kernel may reach another device: no remote copies, remote signals or barrier semaphores. Data moves between devices by JAX's collectives and lax.ppermute only.
A program may use at most 128 MiB of HBM per device.

v0:
```python
import jax
import jax.numpy as jnp
from jax import lax
from jax.sharding import PartitionSpec as P

HEAD_DIM = 128
STEP = 100


beta_first = 0.9
beta_second = 0.999
adam_epsilon = 1e-06
decay_rate = 0.01
learn_rate = 0.01
masked_score = -1e30


def head_grads(query_local, key_local, value_local, grad_local):
    length = query_local.shape[0]
    kv_local = key_local.shape[1] // HEAD_DIM
    group_size = query_local.shape[1] // key_local.shape[1]
    block_rows = min(512, length)
    block_count = length // block_rows
    score_scale = HEAD_DIM ** (-0.5)
    query_blocks = query_local.reshape(block_count, block_rows, kv_local, group_size, HEAD_DIM)
    grad_blocks = grad_local.reshape(block_count, block_rows, kv_local, group_size, HEAD_DIM)
    key_rows = key_local.reshape(length, kv_local, HEAD_DIM)
    value_rows = value_local.reshape(length, kv_local, HEAD_DIM)
    positions = jnp.arange(length)

    def one_block(accums, block_items):
        key_acc, value_acc = accums
        query_blk, grad_blk, block_start = block_items
        scores = (
            jnp.einsum("qgrd,kgd->grqk", query_blk, key_rows, preferred_element_type=jnp.float32)
            * score_scale
        )
        query_pos = block_start + jnp.arange(block_rows)
        allowed = positions[None, :] <= query_pos[:, None]
        scores = jnp.where(allowed, scores, masked_score)
        row_max = jnp.max(scores, axis=-1, keepdims=True)
        weights = jnp.exp(scores - row_max)
        probabilities = weights / jnp.sum(weights, axis=-1, keepdims=True)
        probs_b = probabilities.astype(jnp.bfloat16)
        attended = jnp.einsum(
            "grqk,kgd->qgrd", probs_b, value_rows, preferred_element_type=jnp.float32
        )
        row_delta = jnp.sum(grad_blk.astype(jnp.float32) * attended, axis=-1)
        prob_grad = jnp.einsum(
            "qgrd,kgd->grqk", grad_blk, value_rows, preferred_element_type=jnp.float32
        )
        dscore = (
            probabilities * (prob_grad - jnp.transpose(row_delta, (1, 2, 0))[..., None])
        ).astype(jnp.bfloat16)
        query_grad = (
            jnp.einsum("grqk,kgd->qgrd", dscore, key_rows, preferred_element_type=jnp.float32)
            * score_scale
        ).astype(jnp.bfloat16)
        key_acc = key_acc + jnp.einsum(
            "grqk,qgrd->kgd", dscore, query_blk, preferred_element_type=jnp.float32
        )
        value_acc = value_acc + jnp.einsum(
            "grqk,qgrd->kgd", probs_b, grad_blk, preferred_element_type=jnp.float32
        )
        return ((key_acc, value_acc), query_grad)

    starts = jnp.arange(block_count) * block_rows
    empty_acc = jnp.zeros((length, kv_local, HEAD_DIM), jnp.float32)
    (key_acc, value_acc), query_grads = lax.scan(
        one_block, (empty_acc, empty_acc), (query_blocks, grad_blocks, starts)
    )
    query_grad = query_grads.reshape(length, kv_local, group_size * HEAD_DIM)
    key_grad = (key_acc * score_scale).astype(jnp.bfloat16)
    value_grad = value_acc.astype(jnp.bfloat16)
    return jnp.concatenate([query_grad, key_grad, value_grad], axis=2).reshape(length, -1)


def body(
    layer_input,
    queries,
    keys_saved,
    values_saved,
    out_grad,
    master_weight,
    first_moment,
    second_moment,
):
    weight_sq = jnp.sum(master_weight * master_weight)
    query_heads, key_heads, value_heads, grad_heads = (
        lax.all_to_all(queries, "ctx", split_axis=2, concat_axis=1, tiled=True),
        lax.all_to_all(keys_saved, "ctx", split_axis=2, concat_axis=1, tiled=True),
        lax.all_to_all(values_saved, "ctx", split_axis=2, concat_axis=1, tiled=True),
        lax.all_to_all(out_grad, "ctx", split_axis=2, concat_axis=1, tiled=True),
    )
    grouped = head_grads(query_heads[0], key_heads[0], value_heads[0], grad_heads[0])
    partial_value = lax.dot_general(
        lax.all_gather(layer_input, "ctx", axis=1, tiled=True)[0],
        grouped,
        (((0,), (0,)), ((), ())),
        preferred_element_type=jnp.float32,
    )
    gradient = lax.psum_scatter(
        partial_value.astype(jnp.bfloat16), "dp", scatter_dimension=0, tiled=True
    ).astype(jnp.float32)
    first_new = beta_first * first_moment + (1.0 - beta_first) * gradient
    second_new = beta_second * second_moment + (1.0 - beta_second) * gradient * gradient
    corr_first = 1.0 - beta_first**STEP
    corr_second = 1.0 - beta_second**STEP
    direction = (
        first_new / corr_first / (jnp.sqrt(second_new / corr_second) + adam_epsilon)
        + decay_rate * master_weight
    )
    update_sq = jnp.sum(direction * direction)
    weight_total, update_total = lax.psum((weight_sq, update_sq), ("dp", "ctx"))
    trust_ratio = jnp.sqrt(weight_total) / jnp.sqrt(update_total)
    lamb_update = trust_ratio * direction
    new_local = (master_weight - learn_rate * lamb_update).astype(jnp.bfloat16)
    new_weights = lax.all_gather(new_local, "dp", axis=0, tiled=True)
    return (first_new, second_new, lamb_update, new_weights)


def solution(mesh):
    in_specs = (
        P("dp", "ctx", None),
        P("dp", "ctx", None),
        P("dp", "ctx", None),
        P("dp", "ctx", None),
        P("dp", "ctx", None),
        P("dp", "ctx"),
        P("dp", "ctx"),
        P("dp", "ctx"),
    )
    out_specs = (P("dp", "ctx"), P("dp", "ctx"), P("dp", "ctx"), P(None, "ctx"))
    return jax.shard_map(body, mesh=mesh, in_specs=in_specs, out_specs=out_specs, check_vma=False)
```

profile of v0, /device:TPU:1, one launch (start us, length us, event | category | flops | bytes accessed | tf_op | source)
XLA Modules:
  0.0 621.5 jit_solution(10160004014047542531)
XLA Ops:
  9.0 2.2 reduce.6
  11.9 6.6 %all-to-all-start.3 = ((bf16[8,2,8192]{2,1,0:T(2,128)(2,1)}), bf16[8,2,8192]{2,1,0:T(2,128)(2,1)S(1)}, u32[]{:S(2)}, u32[]{:S(2)}) async-start(bf16[8,2,8192]{2,1,0:T(2,128)(2,1)} %reshape.113), calls=%async_computation.3 | async-start | bytes 524288 | tf_op jit(solution)/shard_map/all_to_all | solution.py:92
  19.8 2.2 reduce.4
  22.7 2.3 all-to-all-done.3
  25.0 5.0 all-to-all-start.1
  30.0 5.0 copy.102
  35.0 22.4 %reduce.3 = bf16[4096,128]{1,0:T(8,128)(2,1)S(1)} reduce(bf16[4096,1,128]{2,1,0:T(2,128)(2,1)S(1)} %bitcast.220, bf16[]{:T(256)} %broadcast.70), dimensions={1}, to_apply=%bitcast.150.reduce_sub_computation | reduce | bytes 2097154
  58.5 4.8 all-to-all-start
  63.3 5.0 copy.106
  68.4 23.4 %reduce.5 = bf16[4096,128]{1,0:T(8,128)(2,1)} reduce(bf16[4096,1,128]{2,1,0:T(2,128)(2,1)S(1)} %bitcast.219, bf16[]{:T(256)} %broadcast.70), dimensions={1}, to_apply=%bitcast.154.reduce_sub_computation | reduce | bytes 2097154
  91.7 2.2 reshape.111
  94.0 4.8 all-to-all-start.2
  102.4 4.3 reshape.108
  109.6 4.4 all-to-all-done.2
  114.0 5.9 reshape.112
  125.1 66.4 %while.15 = (s32[]{:T(128)}, f32[1024,1,128]{0,2,1:T(8,128)S(1)}, f32[1024,1,128]{0,2,1:T(8,128)}, bf16[2,512,1,4,128]{4,3,1,0,2:T(4,128)(2,1)}, bf16[2,512,1,4,...) while((s32[]{:T(128)}, f32[1024,1,128]{0,2,1:T(8,128)S(1)}, ...), condition=%wide.region_4.5_spmd.clone, body=%wide.region_0.4_spmd.clone.sunk | while | flops 3273910784 | bytes 178353008 | solution.py:69
  130.1 3.2 copy-done
  133.3 2.5 fusion.83
  136.1 5.3 fusion.84
  142.3 3.5 fusion.85
  150.4 7.3 %fusion.87 = f32[1024,1,128]{0,2,1:T(8,128)} fusion(bf16[1,512,1,4,128]{4,3,1,0,2:T(4,128)(2,1)S(1)} %get-tuple-element.238, f32[1024,1,128]{0,2,1:T(8,128)} %get-tuple-element.255, pred[]{:T(512)S(6)} %compare.3, f32[4,512]{1,0:T(4,128)S(1)} %fusion.83, f32[4,512]{1,0:T(4,128)S(1)} %get-tuple-element.241, f32[512,4,1024]{2,0,1:T(8,128)} %copy-done, ...), kind=kOutput, calls=%fused_computation.23.clone.1 | convolution fusion | flops 547618816 | bytes 10502145 | tf_op jit(solution)/shard_map/while/body/eval_jaxpr/grqk,qgrd->kgd/dot_general | solution.py:62
  163.5 3.2 copy-done
  166.7 2.5 fusion.83
  169.5 5.3 fusion.84
  175.4 3.5 fusion.85
  183.4 7.2 %fusion.87 = f32[1024,1,128]{0,2,1:T(8,128)} fusion(bf16[1,512,1,4,128]{4,3,1,0,2:T(4,128)(2,1)S(1)} %get-tuple-element.238, f32[1024,1,128]{0,2,1:T(8,128)} %get-tuple-element.255, pred[]{:T(512)S(6)} %compare.3, f32[4,512]{1,0:T(4,128)S(1)} %fusion.83, f32[4,512]{1,0:T(4,128)S(1)} %get-tuple-element.241, f32[512,4,1024]{2,0,1:T(8,128)} %copy-done, ...), kind=kOutput, calls=%fused_computation.23.clone.1 | convolution fusion | flops 547618816 | bytes 10502145 | tf_op jit(solution)/shard_map/while/body/eval_jaxpr/grqk,qgrd->kgd/dot_general | solution.py:62
  194.7 12.3 %fusion.45 = bf16[4096,768]{0,1:T(8,128)(2,1)} fusion(bf16[1,1024,4096]{2,1,0:T(8,128)(2,1)} %all-gather.3.cloned.1.call-done, bf16[1024,1,128]{2,0,1:T(8,128)(2,1)S(1)} %copy.115, bf16[1024,1,128]{2,0,1:T(8,128)(2,1)S(1)} %multiply_convert_fusion, bf16[1024,1,512]{2,0,1:T(8,128)(2,1)S(1)} %reshape.90), kind=kOutput, calls=%fused_computation.42 | convolution fusion | flops 6450315264 | bytes 16252928 | tf_op jit(solution)/shard_map/dot_general | solution.py:96
  207.0 8.7 %copy.129 = bf16[4096,768]{1,0:T(8,128)(2,1)} copy(bf16[4096,768]{0,1:T(8,128)(2,1)} %fusion.45) | data formatting | bytes 12582912
  217.0 219.6 %reduce-scatter.4.cloned.1.call-done = bf16[128,768]{1,0:T(8,128)(2,1)} async-done(((bf16[4096,768]{1,0:T(8,128)(2,1)}), bf16[128,768]{1,0:T(8,128)(2,1)}) %reduce-scatter.4.cloned.1.call-update) | async-done | bytes 196624
  438.6 78.8 %all-reduce = (f32[]{:T(128)}, f32[]{:T(128)}) all-reduce(f32[]{:T(128)} %multiply_reduce_fusion.1, f32[]{:T(128)} %get-tuple-element.171), channel_id=1, replica_groups=mesh['dp'=32,'ctx'=8] {'dp','ctx'}, use_global_device_ids=true, to_apply=%region_7.8 | all-reduce | flops 2 | bytes 16 | tf_op jit(solution)/shard_map/psum | solution.py:114
  522.3 84.1 %all-gather.5.cloned.1.call-done = bf16[4096,768]{0,1:T(8,128)(2,1)} async-done(((bf16[128,768]{0,1:T(8,128)(2,1)}), bf16[4096,768]{0,1:T(8,128)(2,1)}) %all-gather.5.cloned.1.call-update) | async-done | bytes 6291472 | tf_op jit(solution)/shard_map/all_gather | solution.py:118
  606.4 8.6 %copy.122 = bf16[4096,768]{1,0:T(8,128)(2,1)} copy(bf16[4096,768]{0,1:T(8,128)(2,1)} %all-gather.5.cloned.1.call-done) | data formatting | bytes 12582912
  (98 shorter events, 49.8 us)
Async XLA Ops:
  11.9 13.1 %all-to-all-start.3 = ((bf16[8,2,8192]{2,1,0:T(2,128)(2,1)}), bf16[8,2,8192]{2,1,0:T(2,128)(2,1)S(1)}, u32[]{:S(2)}, u32[]{:S(2)}) async-start(bf16[8,2,8192]{2,1,0:T(2,128)(2,1)} %reshape.113), calls=%async_computation.3 | async-start | bytes 524288 | tf_op jit(solution)/shard_map/all_to_all | solution.py:92
  25.0 33.5 %all-to-all-start.1 = ((bf16[8,2,8192]{2,1,0:T(2,128)(2,1)}), bf16[8,2,8192]{2,1,0:T(2,128)(2,1)}, u32[]{:S(2)}, u32[]{:S(2)}) async-start(bf16[8,2,8192]{2,1,0:T(2,128)(2,1)} %reshape.109), calls=%async_computation.1 | async-start | bytes 524288 | tf_op jit(solution)/shard_map/all_to_all | solution.py:91
  58.5 35.4 %all-to-all-start = ((bf16[8,2,32768]{2,1,0:T(2,128)(2,1)}), bf16[8,2,32768]{2,1,0:T(2,128)(2,1)S(1)}, u32[]{:S(2)}, u32[]{:S(2)}) async-start(bf16[8,2,32768]{2,1,0:T(2,128)(2,1)} %reshape.107), calls=%async_computation | async-start | bytes 2097152 | tf_op jit(solution)/shard_map/all_to_all | solution.py:90
  94.0 8.2 %copy-start.6 = (bf16[8,2,32768]{2,1,0:T(2,128)(2,1)}, bf16[8,2,32768]{2,1,0:T(2,128)(2,1)S(1)}, u32[]{:S(2)}) copy-start(bf16[8,2,32768]{2,1,0:T(2,128)(2,1)S(1)} %all-to-all-done) | copy-start | bytes 3145732
  94.0 20.0 %all-to-all-start.2 = ((bf16[8,2,32768]{2,1,0:T(2,128)(2,1)}), bf16[8,2,32768]{2,1,0:T(2,128)(2,1)}, u32[]{:S(2)}, u32[]{:S(2)}) async-start(bf16[8,2,32768]{2,1,0:T(2,128)(2,1)} %reshape.111), calls=%async_computation.2 | async-start | bytes 2097152 | tf_op jit(solution)/shard_map/all_to_all | solution.py:93
  98.8 95.9 %all-gather.3.cloned.1.call-start = ((), (), s32[]{:S(2)}) async-start(), calls=%async_computation.5 | async-start | bytes 9437184 | tf_op jit(solution)/shard_map/all_gather | solution.py:97
  99.5 337.1 %reduce-scatter.4.cloned.1.call-start = ((), (), s32[]{:S(2)}) async-start(), calls=%async_computation.7 | async-start | bytes 6488064
  125.1 10.7 %copy-start.4 = (bf16[2,512,1,4,128]{4,3,1,0,2:T(4,128)(2,1)}, bf16[2,512,1,4,128]{4,3,1,0,2:T(4,128)(2,1)S(1)}, u32[]{:S(2)}) copy-start(bf16[2,512,1,4,128]{4,3,1,0,2:T(4,128)(2,1)S(1)} %get-tuple-element.268) | copy-start | bytes 3145732 | tf_op jit(solution)/shard_map/while
  130.1 3.2 copy-start
  136.1 6.2 %copy-start.1 = (f32[512,4,1024]{2,0,1:T(8,128)S(1)}, f32[512,4,1024]{2,0,1:T(8,128)}, u32[]{:S(2)}) copy-start(f32[512,4,1024]{2,0,1:T(8,128)} %copy-done) | copy-start | bytes 25165828 | tf_op jit(solution)/shard_map/while
  136.1 6.2 %copy-start.10 = (bf16[1024,1,128]{0,2,1:T(8,128)(2,1)S(1)}, bf16[1024,1,128]{0,2,1:T(8,128)(2,1)}, u32[]{:S(2)}) copy-start(bf16[1024,1,128]{0,2,1:T(8,128)(2,1)} %get-tuple-element.272) | copy-start | bytes 786436 | tf_op jit(solution)/shard_map/while
  145.9 2.0 copy-start.2
  150.4 7.3 %copy-start.3 = (bf16[4,512,1024]{2,1,0:T(8,128)(2,1)S(1)}, bf16[4,512,1024]{2,1,0:T(8,128)(2,1)}, u32[]{:S(2)}) copy-start(bf16[4,512,1024]{2,1,0:T(8,128)(2,1)} %copy-done.2) | copy-start | bytes 12582916 | tf_op jit(solution)/shard_map/while
  150.4 8.1 %copy-start.5 = (bf16[2,512,1,4,128]{4,3,1,0,2:T(4,128)(2,1)S(1)}, bf16[2,512,1,4,128]{4,3,1,0,2:T(4,128)(2,1)}, u32[]{:S(2)}) copy-start(bf16[2,512,1,4,128]{4,3,1,0,2:T(4,128)(2,1)} %copy-done.4) | copy-start | bytes 3145732 | tf_op jit(solution)/shard_map/while
  158.5 10.7 %copy-start.4 = (bf16[2,512,1,4,128]{4,3,1,0,2:T(4,128)(2,1)}, bf16[2,512,1,4,128]{4,3,1,0,2:T(4,128)(2,1)S(1)}, u32[]{:S(2)}) copy-start(bf16[2,512,1,4,128]{4,3,1,0,2:T(4,128)(2,1)S(1)} %get-tuple-element.268) | copy-start | bytes 3145732 | tf_op jit(solution)/shard_map/while
  163.5 3.2 copy-start
  169.5 5.9 copy-start.1
  169.5 5.9 copy-start.10
  178.9 2.0 copy-start.2
  183.4 7.3 %copy-start.3 = (bf16[4,512,1024]{2,1,0:T(8,128)(2,1)S(1)}, bf16[4,512,1024]{2,1,0:T(8,128)(2,1)}, u32[]{:S(2)}) copy-start(bf16[4,512,1024]{2,1,0:T(8,128)(2,1)} %copy-done.2) | copy-start | bytes 12582916 | tf_op jit(solution)/shard_map/while
  183.4 8.1 %copy-start.5 = (bf16[2,512,1,4,128]{4,3,1,0,2:T(4,128)(2,1)S(1)}, bf16[2,512,1,4,128]{4,3,1,0,2:T(4,128)(2,1)}, u32[]{:S(2)}) copy-start(bf16[2,512,1,4,128]{4,3,1,0,2:T(4,128)(2,1)} %copy-done.4) | copy-start | bytes 3145732 | tf_op jit(solution)/shard_map/while
  207.0 8.8 %copy-start.7 = (f32[128,768]{1,0:T(8,128)S(1)}, f32[128,768]{1,0:T(8,128)}, u32[]{:S(2)}) copy-start(f32[128,768]{1,0:T(8,128)} %param.15) | copy-start | bytes 1179652
  207.0 9.0 %copy-start.8 = (f32[128,768]{1,0:T(8,128)S(1)}, f32[128,768]{1,0:T(8,128)}, u32[]{:S(2)}) copy-start(f32[128,768]{1,0:T(8,128)} %param.16) | copy-start | bytes 1179652
  207.0 9.2 %copy-start.9 = (f32[128,768]{1,0:T(8,128)S(1)}, f32[128,768]{1,0:T(8,128)}, u32[]{:S(2)}) copy-start(f32[128,768]{1,0:T(8,128)} %param.17) | copy-start | bytes 1179652
  215.8 390.6 %all-gather.5.cloned.1.call-start = ((), (), s32[]{:S(2)}) async-start(), calls=%async_computation.6 | async-start | bytes 6488064 | tf_op jit(solution)/shard_map/all_gather | solution.py:118
Sparse Core Ops, SparseCore 0:
  101.5 54.7 all-gather.2
  215.9 220.6 reduce-scatter.3
  519.7 86.6 all-gather.4
where the time goes:
time: 626 us; the launch traced here: 622 us
  waiting for transfers between devices  311 us (50%)
  local copies, waits for them, and re-layouts  83 us (13%)
  blocking collectives  78.8 us (13%)
  other arithmetic  59.6 us (10%)
  matrix products  52.3 us (8%)
  starting transfers between devices  21.2 us (3%)
  between operations  15.4 us (2%)
    unnamed x4, waiting for transfers between devices  220 us
    all_gather x1, waiting for transfers between devices, body(): new_weights = lax.all_gather(new_local, 'dp', axis=0, tiled=True)  84.1 us
    psum x1, blocking collectives, body(): weight_total, update_total = lax.psum((weight_sq, update_sq), ('dp', 'ctx'))  78.8 us
    unnamed x35, local copies, waits for them, and re-layouts  55 us
    unnamed x6, other arithmetic  50.2 us
    dot_general x2, matrix products, one_block(): jnp.einsum('grqk,qgrd->kgd', probs_b, grad_blk, preferred_element_type=jn...  14.5 us
  transfers between devices with their start and end apart: 7, of which 4 were waited for; matrix products, arithmetic and copies ran while one was open for 23% of the time, Pallas kernels for 0%

commit v1 on v0

v1 whole, which is shorter than its diff:
```python
import jax
import jax.numpy as jnp
from jax import lax
from jax.experimental import pallas as pl
from jax.experimental.pallas import tpu as pltpu
from jax.sharding import Mesh
from jax.sharding import PartitionSpec as P

HEAD_DIM = 128
STEP = 100
GROUP = 4
NX, NZ, NY, NCORE = 4, 8, 4, 2
LENGTH = 1024
COLS = 768
WIDTH = 4096
ROWS = 128
PACKED = 1280
BLOCK = 256

beta_first = 0.9
beta_second = 0.999
adam_epsilon = 1e-06
decay_rate = 0.01
learn_rate = 0.01
masked_score = -1e30
score_scale = HEAD_DIM ** (-0.5)
LOG2E = 1.4426950408889634

f32 = jnp.float32
bf16 = jnp.bfloat16


def dot(a, b, ca, cb):
    return lax.dot_general(a, b, (((ca,), (cb,)), ((), ())), preferred_element_type=f32)


def pack_kernel(q_ref, k_ref, v_ref, g_ref, out_ref):
    out_ref[0, :, 0:512] = q_ref[...]
    out_ref[0, :, 512:640] = k_ref[...]
    out_ref[0, :, 640:768] = v_ref[...]
    out_ref[0, :, 768:1280] = g_ref[...]


def pack(q, k, v, g):
    rows = q.shape[0]
    return pl.pallas_call(
        pack_kernel,
        grid=(8,),
        in_specs=[
            pl.BlockSpec((rows, 512), lambda c: (0, c)),
            pl.BlockSpec((rows, 128), lambda c: (0, c)),
            pl.BlockSpec((rows, 128), lambda c: (0, c)),
            pl.BlockSpec((rows, 512), lambda c: (0, c)),
        ],
        out_specs=pl.BlockSpec((1, rows, PACKED), lambda c: (c, 0, 0)),
        out_shape=jax.ShapeDtypeStruct((8, rows, PACKED), bf16),
        cost_estimate=pl.CostEstimate(flops=0, bytes_accessed=5 << 20, transcendentals=0),
        name="pack",
    )(q, k, v, g)


def attention_kernel(q_ref, k_ref, v_ref, g_ref, dq_ref, dkv_ref, kt_ref, dk_acc, dv_acc):
    head = pl.program_id(0)

    @pl.when(head == 0)
    def _():
        kt_ref[...] = k_ref[...].T
        dk_acc[...] = jnp.zeros_like(dk_acc)
        dv_acc[...] = jnp.zeros_like(dv_acc)

    key_pos = lax.broadcasted_iota(jnp.int32, (BLOCK, BLOCK), 0)
    query_pos = lax.broadcasted_iota(jnp.int32, (BLOCK, BLOCK), 1)
    allowed = key_pos <= query_pos
    for i in range(LENGTH // BLOCK):
        lo, hi = i * BLOCK, (i + 1) * BLOCK
        q = q_ref[lo:hi, :]
        g = g_ref[lo:hi, :]
        scores = dot(k_ref[:hi, :], q, 1, 1)
        diag = jnp.where(allowed, scores[lo:hi, :], masked_score)
        scores = diag if i == 0 else jnp.concatenate([scores[:lo, :], diag], axis=0)
        top = jnp.max(scores, axis=0, keepdims=True)
        weights = jnp.exp2((scores - top) * (score_scale * LOG2E))
        probs = weights * (1.0 / jnp.sum(weights, axis=0, keepdims=True))
        probs_b = probs.astype(bf16)
        prob_grad = dot(v_ref[:hi, :], g, 1, 1)
        row_delta = jnp.sum(probs_b.astype(f32) * prob_grad, axis=0, keepdims=True)
        dscore = (probs * (prob_grad - row_delta)).astype(bf16)
        dq_t = dot(kt_ref[:, :hi], dscore, 1, 0) * score_scale
        dq_ref[:, lo:hi] = dq_t.astype(bf16)
        dk_acc[:hi, :] += dot(dscore, q, 1, 0)
        dv_acc[:hi, :] += dot(probs_b, g, 1, 0)

    @pl.when(head == GROUP - 1)
    def _():
        dkv_ref[0:128, :] = (dk_acc[...] * score_scale).astype(bf16).T
        dkv_ref[128:256, :] = dv_acc[...].astype(bf16).T


def attention(packed):
    return pl.pallas_call(
        attention_kernel,
        grid=(GROUP,),
        in_specs=[
            pl.BlockSpec((LENGTH, 128), lambda h: (0, h)),
            pl.BlockSpec((LENGTH, 128), lambda h: (0, 4)),
            pl.BlockSpec((LENGTH, 128), lambda h: (0, 5)),
            pl.BlockSpec((LENGTH, 128), lambda h: (0, 6 + h)),
        ],
        out_specs=[
            pl.BlockSpec((128, LENGTH), lambda h: (h, 0)),
            pl.BlockSpec((256, LENGTH), lambda h: (0, 0)),
        ],
        out_shape=[
            jax.ShapeDtypeStruct((512, LENGTH), bf16),
            jax.ShapeDtypeStruct((256, LENGTH), bf16),
        ],
        scratch_shapes=[
            pltpu.VMEM((128, LENGTH), bf16),
            pltpu.VMEM((LENGTH, 128), f32),
            pltpu.VMEM((LENGTH, 128), f32),
        ],
        compiler_params=pltpu.CompilerParams(vmem_limit_bytes=48 << 20),
        cost_estimate=pl.CostEstimate(
            flops=4 << 30, bytes_accessed=5 << 20, transcendentals=4 << 20
        ),
        name="attention_backward",
    )(packed, packed, packed, packed)


def project_kernel(dq_ref, dkv_ref, x0, x1, x2, x3, out_ref):
    for i, x_ref in enumerate((x0, x1, x2, x3)):
        out_ref[0, i, 0:512, :] = dot(dq_ref[...], x_ref[...], 1, 0).astype(bf16)
        out_ref[0, i, 512:768, :] = dot(dkv_ref[...], x_ref[...], 1, 0).astype(bf16)


def project(dq, dkv, x):
    def x_spec(i):
        return pl.BlockSpec((LENGTH, ROWS), lambda z: (0, i * NZ + z))

    return pl.pallas_call(
        project_kernel,
        grid=(NZ,),
        in_specs=[
            pl.BlockSpec((512, LENGTH), lambda z: (0, 0)),
            pl.BlockSpec((256, LENGTH), lambda z: (0, 0)),
            *[x_spec(i) for i in range(NX)],
        ],
        out_specs=pl.BlockSpec((1, NX, COLS, ROWS), lambda z: (z, 0, 0, 0)),
        out_shape=jax.ShapeDtypeStruct((NZ, NX, COLS, ROWS), bf16),
        compiler_params=pltpu.CompilerParams(vmem_limit_bytes=48 << 20),
        cost_estimate=pl.CostEstimate(flops=6 << 30, bytes_accessed=16 << 20, transcendentals=0),
        name="project",
    )(dq, dkv, x, x, x, x)


def optimizer_kernel(grad_ref, w_ref, m_ref, v_ref, m_out, v_out, dir_out, sums_out):
    gradient = grad_ref[...].astype(f32).T
    weight = w_ref[...]
    first_new = beta_first * m_ref[...] + (1.0 - beta_first) * gradient
    second_new = beta_second * v_ref[...] + (1.0 - beta_second) * gradient * gradient
    corr_first = 1.0 - beta_first**STEP
    corr_second = 1.0 - beta_second**STEP
    direction = (
        first_new / corr_first / (jnp.sqrt(second_new / corr_second) + adam_epsilon)
        + decay_rate * weight
    )
    m_out[...] = first_new
    v_out[...] = second_new
    dir_out[...] = direction
    weight_sq = jnp.sum(weight * weight)
    update_sq = jnp.sum(direction * direction)
    row = lax.broadcasted_iota(jnp.int32, (8, 128), 0)
    sums_out[...] = jnp.where(row == 0, weight_sq, update_sq)


def optimizer(grad, w, m, v):
    shape = jax.ShapeDtypeStruct((ROWS, COLS), f32)
    return pl.pallas_call(
        optimizer_kernel,
        out_shape=[shape, shape, shape, jax.ShapeDtypeStruct((8, 128), f32)],
        compiler_params=pltpu.CompilerParams(vmem_limit_bytes=32 << 20),
        name="optimizer",
    )(grad, w, m, v)


def all_sum(sums, axes, size):
    spread = jnp.broadcast_to(sums[None], (size,) + sums.shape)
    return jnp.sum(lax.all_to_all(spread, axes, 0, 0, tiled=True), axis=0)


def body(x, q, k, v, g, w, m, s):
    packed = pack(q[0], k[0], v[0], g[0])
    heads = lax.all_to_all(packed, ("y", "core"), 0, 0, tiled=True).reshape(LENGTH, PACKED)
    x_full = lax.all_gather(x[0], ("y", "core"), axis=0, tiled=True)
    dq, dkv = attention(heads)
    partial = project(dq, dkv, x_full)
    partial = lax.psum_scatter(partial, "z", scatter_dimension=0, tiled=True)[0]
    grad = lax.psum_scatter(partial, "x", scatter_dimension=0, tiled=True)[0]
    first_new, second_new, direction, sums = optimizer(grad, w, m, s)
    sums = all_sum(all_sum(sums, ("y", "core"), 8), ("x", "z"), 32)
    trust_ratio = jnp.sqrt(sums[0, 0]) / jnp.sqrt(sums[1, 0])
    lamb_update = trust_ratio * direction
    new_local = (w - learn_rate * lamb_update).astype(bf16)
    new_weights = lax.all_gather(new_local, ("x", "z"), axis=0, tiled=True)
    return first_new, second_new, lamb_update, new_weights


def solution(mesh):
    fine = Mesh(mesh.devices.reshape(NX, NZ, NY, NCORE), ("x", "z", "y", "core"))
    dp, ctx = ("x", "z"), ("y", "core")
    seq = P(dp, ctx, None)
    mat = P(dp, ctx)
    return jax.shard_map(
        body,
        mesh=fine,
        in_specs=(seq, seq, seq, seq, seq, mat, mat, mat),
        out_specs=(mat, mat, mat, P(None, ctx)),
        check_vma=False,
    )
```

time: 626 us -> 335 us (0.54)
  waiting for transfers between devices: 311 us -> 186 us
  local copies, waits for them, and re-layouts: 83 us -> 7.36 us
  other arithmetic: 59.6 us -> 0.9 us
  matrix products: 52.3 us -> 0 us
  Pallas kernels: 0 us -> 37.7 us
  starting transfers between devices: 21.2 us -> 0.16 us
  blocking collectives: 78.8 us -> 88.1 us
    unnamed x4, waiting for transfers between devices: 220 us -> 0.73 us
    reduce_scatter x0 -> x2, waiting for transfers between devices: none -> 101 us  [the longest x1 76.3 us: body(): partial = lax.psum_scatter(partial, 'z', scatter_dimension=0, tiled=True)[0]]
    all_to_all x0 -> x3, blocking collectives: none -> 88.1 us  [the longest x1 60.6 us: body(): lax.all_to_all(packed, ('y', 'core'), 0, 0, tiled=True)]
    psum x1 -> x0, blocking collectives: 78.8 us -> none  [body(): weight_total, update_total = lax.psum((weight_sq, update_sq), ('dp', 'ctx'))]
    dot_general x13 -> x0, matrix products: 52.3 us -> none  [the longest x2 14.5 us: one_block(): jnp.einsum('grqk,qgrd->kgd', probs_b, grad_blk, preferred_element_type=jn...]
    unnamed x6 -> x0, other arithmetic: 50.2 us -> none
    unnamed x35 -> x9, local copies, waits for them, and re-layouts: 55 us -> 6.83 us
    pallas_call x0 -> x4, Pallas kernels: none -> 37.7 us  [the longest x1 16.7 us: project(): pl.pallas_call(project_kernel, grid=(NZ,), in_specs=[pl.BlockSpec((512, L...]
  transfers between devices with their start and end apart: 7 -> 4, of which waited for: 4 -> 4; matrix products, arithmetic and copies ran while one was open for 23% -> 0% of each run, Pallas kernels for 0% -> 6%
where the time goes in v1:
time: 335 us
  waiting for transfers between devices  186 us (56%)
  blocking collectives  88.1 us (26%)
  Pallas kernels  37.7 us (11%)
  between operations  15.2 us (5%)
  local copies, waits for them, and re-layouts  7.36 us (2%)
    all_gather x1, waiting for transfers between devices, body(): new_weights = lax.all_gather(new_local, ('x', 'z'), axis=0, tiled=True)  83.3 us
    reduce_scatter x1, waiting for transfers between devices, body(): partial = lax.psum_scatter(partial, 'z', scatter_dimension=0, tiled=True)[0]  76.3 us
    all_to_all x1, blocking collectives, body(): lax.all_to_all(packed, ('y', 'core'), 0, 0, tiled=True)  60.6 us
    all_to_all x2, blocking collectives, all_sum(): return jnp.sum(lax.all_to_all(spread, axes, 0, 0, tiled=True), axis=0)  27.5 us
    reduce_scatter x1, waiting for transfers between devices, body(): grad = lax.psum_scatter(partial, 'x', scatter_dimension=0, tiled=True)[0]  25 us
    pallas_call x1, Pallas kernels, project(): pl.pallas_call(project_kernel, grid=(NZ,), in_specs=[pl.BlockSpec((512, L...  16.7 us
    pallas_call x1, Pallas kernels, attention(): pl.pallas_call(attention_kernel, grid=(GROUP,), in_specs=[pl.BlockSpec((L...  13.6 us
    unnamed x9, local copies, waits for them, and re-layouts  6.83 us
  transfers between devices with their start and end apart: 4, of which 4 were waited for; matrix products, arithmetic and copies ran while one was open for 0% of the time, Pallas kernels for 6%

profile of v1, /device:TPU:1, one launch (start us, length us, event | category | flops | bytes accessed | tf_op | source)
XLA Modules:
  0.0 335.0 jit_solution(11439109407742691029)
XLA Ops:
  7.2 0.0 all-gather.6.cloned.1.call-start
  7.2 0.7 all-gather.6.cloned.1.call-update
  7.9 0.0 reduce-scatter.3.cloned.1.call-start
  7.9 6.1 %pack.1 = bf16[8,128,1280]{2,1,0:T(8,128)(2,1)} custom-call(bf16[128,4096]{1,0:T(8,128)(2,1)} %bitcast.18, bf16[128,1024]{1,0:T(8,128)(2,1)} %bitcast.21, bf16[128,1024]{1,0:T(8,128)(2,1)} %bitcast.22, bf16[128,4096]{1,0:T(8,128)(2,1)} %bitcast.19), custom_call_target="tpu_custom_call" | custom-call | bytes 5242880 | tf_op jit(solution)/shard_map/pack/pallas_call | solution.py:46
  14.0 60.6 %all_to_all.15 = bf16[8,128,1280]{2,1,0:T(8,128)(2,1)S(1)} all-to-all(bf16[8,128,1280]{2,1,0:T(8,128)(2,1)} %pack.1), channel_id=1, replica_groups=mesh['x'=4,'z'=8,'y'=4,'core'=2] {'y','core'}, dimensions={0} | all-to-all | bytes 5242880 | tf_op jit(solution)/shard_map/all_to_all | solution.py:193
  74.6 13.6 %attention_backward.1 = (bf16[512,1024]{1,0:T(8,128)(2,1)S(1)}, bf16[256,1024]{1,0:T(8,128)(2,1)S(1)}) custom-call(bf16[1024,1280]{1,0:T(8,128)(2,1)S(1)} %bitcast.9, bf16[1024,1280]{1,0:T(8,128)(2,1)S(1)} %bitcast.10, bf16[1024,1280]{1,0:T(8,128)(2,1)S(1)} %bitcast.11, bf16[1024,1280]{1,0:T(8,128)(2,1)S(1)} %bitcast.12), custom_call_target="tpu_custom_call" | custom-call | flops 4294967296 | bytes 5242880 | tf_op jit(solution)/shard_map/attention_backward/pallas_call | solution.py:100
  88.3 0.3 all-gather.6.cloned.1.call-done
  88.6 16.7 %project.1 = bf16[8,4,768,128]{3,2,1,0:T(8,128)(2,1)} custom-call(bf16[512,1024]{1,0:T(8,128)(2,1)S(1)} %get-tuple-element.10.dq_ref, bf16[256,1024]{1,0:T(8,128)(2,1)S(1)} %get-tuple-element.11.dkv_ref, bf16[1024,4096]{1,0:T(8,128)(2,1)} %bitcast.14, bf16[1024,4096]{1,0:T(8,128)(2,1)} %bitcast.15, bf16[1024,4096]{1,0:T(8,128)(2,1)} %bitcast.16, ...), custom_call_target="tpu_custom_call" | custom-call | flops 6442450944 | bytes 16777216 | tf_op jit(solution)/shard_map/project/pallas_call | solution.py:140
  105.3 0.0 copy-start
  105.3 0.0 copy-start.1
  105.3 0.0 copy-start.2
  105.3 0.0 reduce-scatter.3.cloned.1.call-update
  105.3 0.0 reduce-scatter.5.cloned.1.call-start
  105.4 76.3 %reduce-scatter.3.cloned.1.call-done = bf16[1,4,768,128]{3,2,1,0:T(8,128)(2,1)} async-done(((bf16[8,4,768,128]{3,2,1,0:T(8,128)(2,1)}), bf16[1,4,768,128]{3,2,1,0:T(8,128)(2,1)}) %reduce-scatter.3.cloned.1.call-update) | async-done | bytes 786448 | tf_op jit(solution)/shard_map/reduce_scatter | solution.py:197
  181.7 0.0 reduce-scatter.5.cloned.1.call-update
  181.7 0.0 all-gather.4.cloned.1.call-start
  181.7 25.0 %reduce-scatter.5.cloned.1.call-done = bf16[1,768,128]{2,1,0:T(8,128)(2,1)} async-done(((bf16[4,768,128]{2,1,0:T(8,128)(2,1)}), bf16[1,768,128]{2,1,0:T(8,128)(2,1)}) %reduce-scatter.5.cloned.1.call-update) | async-done | bytes 196624 | tf_op jit(solution)/shard_map/reduce_scatter | solution.py:198
  206.7 0.0 copy-done
  206.7 0.0 copy-done.1
  206.7 0.0 copy-done.2
  206.7 0.0 copy-start.3
  206.8 0.9 copy-done.3
  207.7 1.3 optimizer.1
  208.9 10.5 %all_to_all.16 = f32[8,8,128]{2,1,0:T(8,128)S(1)} all-to-all(f32[8,8,128]{2,1,0:T(8,128)S(1)} %broadcast_in_dim.4), channel_id=1, replica_groups=mesh['x'=4,'z'=8,'y'=4,'core'=2] {'y','core'}, dimensions={0} | all-to-all | bytes 65536 | tf_op jit(solution)/shard_map/all_to_all | solution.py:188
  219.5 17.0 %all_to_all.17 = f32[32,8,128]{2,1,0:T(8,128)S(1)} all-to-all(f32[32,8,128]{2,1,0:T(8,128)S(1)} %broadcast_in_dim.5), channel_id=1, replica_groups=mesh['x'=4,'z'=8,'y'=4,'core'=2] {'x','z'}, dimensions={0} | all-to-all | bytes 262144 | tf_op jit(solution)/shard_map/all_to_all | solution.py:188
  236.5 0.5 fusion
  238.4 0.9 subtract_convert_fusion
  239.3 0.0 all-gather.4.cloned.1.call-update
  239.3 83.3 %all-gather.4.cloned.1.call-done = bf16[4096,768]{1,0:T(8,128)(2,1)} async-done(((bf16[128,768]{1,0:T(8,128)(2,1)}), bf16[4096,768]{1,0:T(8,128)(2,1)}) %all-gather.4.cloned.1.call-update) | async-done | bytes 6291472 | tf_op jit(solution)/shard_map/all_gather | solution.py:204
  322.6 5.9 %copy.13 = bf16[4096,768]{1,0:T(8,128)(2,1)} copy(bf16[4096,768]{1,0:T(8,128)(2,1)} %all-gather.4.cloned.1.call-done) | data formatting | bytes 12582912
  (4 shorter events, 0.1 us)
Async XLA Ops:
  7.2 81.4 %all-gather.6.cloned.1.call-start = ((), (), s32[]{:S(2)}) async-start(), calls=%async_computation.8 | async-start | bytes 9437184 | tf_op jit(solution)/shard_map/all_gather | solution.py:194
  7.9 173.8 %reduce-scatter.3.cloned.1.call-start = ((), (), s32[]{:S(2)}) async-start(), calls=%async_computation.5 | async-start | bytes 7077888 | tf_op jit(solution)/shard_map/reduce_scatter | solution.py:197
  105.3 101.4 %copy-start = (f32[128,768]{1,0:T(8,128)S(1)}, f32[128,768]{1,0:T(8,128)}, u32[]{:S(2)}) copy-start(f32[128,768]{1,0:T(8,128)} %w_ref.1) | copy-start | bytes 1179652
  105.3 101.4 %copy-start.1 = (f32[128,768]{1,0:T(8,128)S(1)}, f32[128,768]{1,0:T(8,128)}, u32[]{:S(2)}) copy-start(f32[128,768]{1,0:T(8,128)} %m_ref.1) | copy-start | bytes 1179652
  105.3 101.4 %copy-start.2 = (f32[128,768]{1,0:T(8,128)S(1)}, f32[128,768]{1,0:T(8,128)}, u32[]{:S(2)}) copy-start(f32[128,768]{1,0:T(8,128)} %v_ref.1) | copy-start | bytes 1179652
  105.3 101.4 %reduce-scatter.5.cloned.1.call-start = ((), (), s32[]{:S(2)}) async-start(), calls=%async_computation.6 | async-start | bytes 983040 | tf_op jit(solution)/shard_map/reduce_scatter | solution.py:198
  181.7 140.9 %all-gather.4.cloned.1.call-start = ((), (), s32[]{:S(2)}) async-start(), calls=%async_computation.7 | async-start | bytes 6488064 | tf_op jit(solution)/shard_map/all_gather | solution.py:204
  206.7 0.9 copy-start.3
Sparse Core Ops, SparseCore 0:
  9.9 78.6 all-gather.5
  105.5 76.1 reduce-scatter.2
  184.2 22.4 reduce-scatter.4
  239.4 83.1 all-gather.3

commit v2 on v1

v2 whole, which is shorter than its diff:
```python
import jax
import jax.numpy as jnp
from jax import lax
from jax.experimental import pallas as pl
from jax.experimental.pallas import tpu as pltpu
from jax.sharding import Mesh
from jax.sharding import PartitionSpec as P

HEAD_DIM = 128
STEP = 100
GROUP = 4
NX, NZ, NY, NCORE = 4, 8, 4, 2
LENGTH = 1024
COLS = 768
WIDTH = 4096
ROWS = 128
PACKED = 1280
BLOCK = 256
COLS_A = 448
COLS_B = COLS - COLS_A
ROWS_A = 64
ROWS_B = ROWS - ROWS_A

beta_first = 0.9
beta_second = 0.999
adam_epsilon = 1e-06
decay_rate = 0.01
learn_rate = 0.01
masked_score = -1e30
score_scale = HEAD_DIM ** (-0.5)
LOG2E = 1.4426950408889634

f32 = jnp.float32
bf16 = jnp.bfloat16


def dot(a, b, ca, cb):
    return lax.dot_general(a, b, (((ca,), (cb,)), ((), ())), preferred_element_type=f32)


def pack_kernel(q_ref, k_ref, v_ref, g_ref, out_ref):
    for c in range(out_ref.shape[0]):
        out_ref[c, :, 0:512] = q_ref[:, c * 512 : (c + 1) * 512]
        out_ref[c, :, 512:640] = k_ref[:, c * 128 : (c + 1) * 128]
        out_ref[c, :, 640:768] = v_ref[:, c * 128 : (c + 1) * 128]
        out_ref[c, :, 768:1280] = g_ref[:, c * 512 : (c + 1) * 512]


def pack(q, k, v, g):
    rows = q.shape[0]
    each = 4
    return pl.pallas_call(
        pack_kernel,
        grid=(8 // each,),
        in_specs=[
            pl.BlockSpec((rows, 512 * each), lambda c: (0, c)),
            pl.BlockSpec((rows, 128 * each), lambda c: (0, c)),
            pl.BlockSpec((rows, 128 * each), lambda c: (0, c)),
            pl.BlockSpec((rows, 512 * each), lambda c: (0, c)),
        ],
        out_specs=pl.BlockSpec((each, rows, PACKED), lambda c: (c, 0, 0)),
        out_shape=jax.ShapeDtypeStruct((8, rows, PACKED), bf16),
        cost_estimate=pl.CostEstimate(flops=0, bytes_accessed=5 << 20, transcendentals=0),
        name="pack",
    )(q, k, v, g)


def attention_kernel(q_ref, k_ref, v_ref, g_ref, out_ref, kt_ref, dk_acc, dv_acc):
    head = pl.program_id(0)

    @pl.when(head == 0)
    def _():
        kt_ref[...] = k_ref[...].T
        dk_acc[...] = jnp.zeros_like(dk_acc)
        dv_acc[...] = jnp.zeros_like(dv_acc)

    key_pos = lax.broadcasted_iota(jnp.int32, (BLOCK, BLOCK), 0)
    query_pos = lax.broadcasted_iota(jnp.int32, (BLOCK, BLOCK), 1)
    allowed = key_pos <= query_pos
    for i in range(LENGTH // BLOCK):
        lo, hi = i * BLOCK, (i + 1) * BLOCK
        q = q_ref[lo:hi, :]
        g = g_ref[lo:hi, :]
        scores = dot(k_ref[:hi, :], q, 1, 1)
        diag = jnp.where(allowed, scores[lo:hi, :], masked_score)
        scores = diag if i == 0 else jnp.concatenate([scores[:lo, :], diag], axis=0)
        top = jnp.max(scores, axis=0, keepdims=True)
        weights = jnp.exp2((scores - top) * (score_scale * LOG2E))
        probs = weights * (1.0 / jnp.sum(weights, axis=0, keepdims=True))
        probs_b = probs.astype(bf16)
        prob_grad = dot(v_ref[:hi, :], g, 1, 1)
        row_delta = jnp.sum(probs_b.astype(f32) * prob_grad, axis=0, keepdims=True)
        dscore = (probs * (prob_grad - row_delta)).astype(bf16)
        dq_t = dot(kt_ref[:, :hi], dscore, 1, 0) * score_scale
        out_ref[pl.ds(pl.multiple_of(head * 128, 128), 128), lo:hi] = dq_t.astype(bf16)
        dk_acc[:hi, :] += dot(dscore, q, 1, 0)
        dv_acc[:hi, :] += dot(probs_b, g, 1, 0)

    @pl.when(head == GROUP - 1)
    def _():
        out_ref[512:640, :] = (dk_acc[...] * score_scale).astype(bf16).T
        out_ref[640:768, :] = dv_acc[...].astype(bf16).T


def attention(packed):
    return pl.pallas_call(
        attention_kernel,
        grid=(GROUP,),
        in_specs=[
            pl.BlockSpec((LENGTH, 128), lambda h: (0, h)),
            pl.BlockSpec((LENGTH, 128), lambda h: (0, 4)),
            pl.BlockSpec((LENGTH, 128), lambda h: (0, 5)),
            pl.BlockSpec((LENGTH, 128), lambda h: (0, 6 + h)),
        ],
        out_specs=pl.BlockSpec((COLS, LENGTH), lambda h: (0, 0)),
        out_shape=jax.ShapeDtypeStruct((COLS, LENGTH), bf16),
        scratch_shapes=[
            pltpu.VMEM((128, LENGTH), bf16),
            pltpu.VMEM((LENGTH, 128), f32),
            pltpu.VMEM((LENGTH, 128), f32),
        ],
        compiler_params=pltpu.CompilerParams(vmem_limit_bytes=48 << 20),
        cost_estimate=pl.CostEstimate(
            flops=4 << 30, bytes_accessed=5 << 20, transcendentals=4 << 20
        ),
        name="attention_backward",
    )(packed, packed, packed, packed)


def project(grouped, x, lo, hi, z_major):
    cols = hi - lo
    tile = 4

    def kernel(grouped_ref, x_ref, out_ref):
        res = dot(grouped_ref[lo:hi, :], x_ref[...], 1, 0).astype(bf16)
        for i in range(tile):
            piece = res[:, i * ROWS : (i + 1) * ROWS]
            if z_major:
                out_ref[i, 0] = piece
            else:
                out_ref[0, i] = piece

    if z_major:
        shape, block = (NZ, NX, cols, ROWS), (tile, 1, cols, ROWS)
        place = lambda x, z: (z, x, 0, 0)
    else:
        shape, block = (NX, NZ, cols, ROWS), (1, tile, cols, ROWS)
        place = lambda x, z: (x, z, 0, 0)
    return pl.pallas_call(
        kernel,
        grid=(NX, NZ // tile),
        in_specs=[
            pl.BlockSpec((COLS, LENGTH), lambda x, z: (0, 0)),
            pl.BlockSpec((LENGTH, ROWS * tile), lambda x, z: (0, x * (NZ // tile) + z)),
        ],
        out_specs=pl.BlockSpec(block, place),
        out_shape=jax.ShapeDtypeStruct(shape, bf16),
        compiler_params=pltpu.CompilerParams(vmem_limit_bytes=48 << 20),
        cost_estimate=pl.CostEstimate(
            flops=2 * cols * LENGTH * WIDTH,
            bytes_accessed=(10 << 20) + 2 * cols * WIDTH,
            transcendentals=0,
        ),
        name="project_z" if z_major else "project_x",
    )(grouped, x)


def optimizer_kernel(ga_ref, gb_ref, w_ref, m_ref, v_ref, m_out, v_out, dir_out, a_out, b_out, sums_out):
    grad_a = jnp.sum(ga_ref[...].astype(f32), axis=0)
    grad_b = jnp.sum(gb_ref[...].astype(f32), axis=0)
    gradient = jnp.concatenate([grad_a, grad_b], axis=0).T
    weight = w_ref[...]
    first_new = beta_first * m_ref[...] + (1.0 - beta_first) * gradient
    second_new = beta_second * v_ref[...] + (1.0 - beta_second) * gradient * gradient
    corr_first = 1.0 - beta_first**STEP
    corr_second = 1.0 - beta_second**STEP
    direction = (
        first_new / corr_first / (jnp.sqrt(second_new / corr_second) + adam_epsilon)
        + decay_rate * weight
    )
    m_out[...] = first_new
    v_out[...] = second_new
    dir_out[...] = direction
    a_out[0] = direction[:ROWS_A].astype(bf16)
    a_out[1] = weight[:ROWS_A].astype(bf16)
    b_out[0] = direction[ROWS_A:].astype(bf16)
    b_out[1] = weight[ROWS_A:].astype(bf16)
    weight_sq = jnp.sum(weight * weight)
    update_sq = jnp.sum(direction * direction)
    row = lax.broadcasted_iota(jnp.int32, (8, 128), 0)
    sums_out[...] = jnp.where(row == 0, weight_sq, update_sq)


def optimizer(ga, gb, w, m, v):
    shape = jax.ShapeDtypeStruct((ROWS, COLS), f32)
    return pl.pallas_call(
        optimizer_kernel,
        out_shape=[
            shape,
            shape,
            shape,
            jax.ShapeDtypeStruct((2, ROWS_A, COLS), bf16),
            jax.ShapeDtypeStruct((2, ROWS_B, COLS), bf16),
            jax.ShapeDtypeStruct((8, 128), f32),
        ],
        compiler_params=pltpu.CompilerParams(vmem_limit_bytes=32 << 20),
        name="optimizer",
    )(ga, gb, w, m, v)


def apply_kernel(place_ref, sums_ref, a0, a1, a2, a3, b_ref, a_out, b_out):
    sums = jnp.sum(sums_ref[...], axis=0)
    rate = learn_rate * (jnp.sqrt(sums[0:1, 0:1]) / jnp.sqrt(sums[1:2, 0:1]))
    for k, ref in enumerate((a0, a1, a2, a3)):
        new = ref[1].astype(f32) - rate * ref[0].astype(f32)
        a_out[place_ref[k]] = new.astype(bf16)
    for z in range(NZ):
        new = b_ref[z, 1].astype(f32) - rate * b_ref[z, 0].astype(f32)
        b_out[z] = new.astype(bf16)


def apply_step(place, sums, pieces, gathered):
    vmem = pl.BlockSpec(memory_space=pltpu.VMEM)
    return pl.pallas_call(
        apply_kernel,
        in_specs=[pl.BlockSpec(memory_space=pltpu.SMEM)] + [vmem] * 6,
        out_specs=[vmem, vmem],
        out_shape=[
            jax.ShapeDtypeStruct((NX, ROWS_A, COLS), bf16),
            jax.ShapeDtypeStruct((NZ, ROWS_B, COLS), bf16),
        ],
        compiler_params=pltpu.CompilerParams(vmem_limit_bytes=32 << 20),
        name="apply",
    )(place, sums, *pieces, gathered)


def join_kernel(place_ref, a_ref, b0, b1, b2, b3, b4, out_ref):
    step, half = pl.program_id(0), pl.program_id(1)
    for z in range(a_ref.shape[0]):
        out_ref[0, z, 0:ROWS_A, :] = a_ref[z, 0]
    for k, ref in enumerate((b0, b1, b2)):

        @pl.when(step == k)
        def _(ref=ref):
            out_ref[0, :, ROWS_A:ROWS, :] = ref[...]

    for k, ref in enumerate((b3, b4)):

        @pl.when((step == 3) & (half == k))
        def _(ref=ref):
            out_ref[0, :, ROWS_A:ROWS, :] = ref[...]


def join(place, a_full, own, before, after, far_lo, far_hi):
    half = NZ // 2

    def b_spec(k):
        return pl.BlockSpec(
            (half, ROWS_B, COLS),
            lambda o, h, place: (jnp.where(o < k, 0, jnp.where(o > k, 1, h)), 0, 0),
        )

    whole = pl.BlockSpec((half, ROWS_B, COLS), lambda o, h, place: (0, 0, 0))
    return pl.pallas_call(
        join_kernel,
        grid_spec=pltpu.PrefetchScalarGridSpec(
            num_scalar_prefetch=1,
            grid=(NX, 2),
            in_specs=[
                pl.BlockSpec((half, 1, ROWS_A, COLS), lambda o, h, place: (h, place[o], 0, 0)),
                b_spec(0),
                b_spec(1),
                b_spec(2),
                whole,
                whole,
            ],
            out_specs=pl.BlockSpec(
                (1, half, ROWS, COLS), lambda o, h, place: (place[o], h, 0, 0)
            ),
        ),
        out_shape=jax.ShapeDtypeStruct((NX, NZ, ROWS, COLS), bf16),
        compiler_params=pltpu.CompilerParams(vmem_limit_bytes=48 << 20),
        cost_estimate=pl.CostEstimate(flops=0, bytes_accessed=13 << 20, transcendentals=0),
        name="join",
    )(place, a_full, own, before, after, far_lo, far_hi)


def shift(value, axis, size, by):
    return lax.ppermute(value, axis, [(i, (i + by) % size) for i in range(size)])


def spread(sums, axes, size):
    wide = jnp.broadcast_to(sums[None], (size,) + sums.shape)
    return lax.all_to_all(wide, axes, 0, 0, tiled=True)


def body(x, q, k, v, g, w, m, s):
    packed = pack(q[0], k[0], v[0], g[0])
    heads = lax.all_to_all(packed, ("y", "core"), 0, 0, tiled=True).reshape(LENGTH, PACKED)
    x_full = lax.all_gather(x[0], ("y", "core"), axis=0, tiled=True)
    grouped = attention(heads)

    part_a = project(grouped, x_full, 0, COLS_A, True)
    part_b = project(grouped, x_full, COLS_A, COLS, False)
    part_a = lax.psum_scatter(part_a, "z", scatter_dimension=0, tiled=True)[0]
    part_b = lax.all_to_all(part_b, "x", 0, 0, tiled=True)
    part_b = jnp.sum(part_b.astype(f32), axis=0).astype(bf16)
    part_b = lax.all_to_all(part_b, "z", 0, 0, tiled=True)
    part_a = lax.all_to_all(part_a, "x", 0, 0, tiled=True)

    first_new, second_new, direction, mine_a, mine_b, sums = optimizer(part_a, part_b, w, m, s)
    at_x = lax.axis_index("x")
    place = jnp.stack([at_x, (at_x + 3) % NX, (at_x + 1) % NX, (at_x + 2) % NX]).astype(jnp.int32)
    pieces = (
        mine_a,
        shift(mine_a, "x", NX, 1),
        shift(mine_a, "x", NX, -1),
        shift(mine_a, "x", NX, 2),
    )
    gathered_b = lax.all_gather(mine_b, "z", axis=0, tiled=False)
    sums = spread(jnp.sum(spread(sums, ("y", "core"), 8), axis=0), ("x", "z"), 32)
    new_a, new_b = apply_step(place, sums, pieces, gathered_b)
    full_a = lax.all_gather(new_a, "z", axis=0, tiled=False)
    before, after = shift(new_b, "x", NX, 1), shift(new_b, "x", NX, -1)
    far_lo = shift(before[: NZ // 2], "x", NX, 1)
    far_hi = shift(after[NZ // 2 :], "x", NX, -1)
    new_weights = join(place, full_a, new_b, before, after, far_lo, far_hi)

    total = jnp.sum(sums, axis=0)
    lamb_update = (jnp.sqrt(total[0, 0]) / jnp.sqrt(total[1, 0])) * direction
    return first_new, second_new, lamb_update, new_weights.reshape(WIDTH, COLS)


def solution(mesh):
    fine = Mesh(mesh.devices.reshape(NX, NZ, NY, NCORE), ("x", "z", "y", "core"))
    dp, ctx = ("x", "z"), ("y", "core")
    seq = P(dp, ctx, None)
    mat = P(dp, ctx)
    return jax.shard_map(
        body,
        mesh=fine,
        in_specs=(seq, seq, seq, seq, seq, mat, mat, mat),
        out_specs=(mat, mat, mat, P(None, ctx)),
        check_vma=False,
    )
```

time: 335 us -> 279 us (0.83)
  waiting for transfers between devices: 186 us -> 55.9 us
  blocking collectives: 88.1 us -> 140 us
  starting transfers between devices: 0.16 us -> 13.7 us
  Pallas kernels: 37.7 us -> 43 us
  other arithmetic: 0.9 us -> 4.25 us
    reduce_scatter x2 -> x1, waiting for transfers between devices: 101 us -> 0.01 us  [body(): part_a = lax.psum_scatter(part_a, 'z', scatter_dimension=0, tiled=True)[0]]
    all_gather x1 -> x2, waiting for transfers between devices: 83.3 us -> 27.3 us  [the longest x1 21.5 us: body(): full_a = lax.all_gather(new_a, 'z', axis=0, tiled=False)]
    all_to_all x2 -> x4, blocking collectives: 27.5 us -> 82.2 us  [the longest x1 35 us: body(): part_b = lax.all_to_all(part_b, 'x', 0, 0, tiled=True)]
    ppermute x0 -> x7, waiting for transfers between devices: none -> 24.5 us  [shift(): lax.ppermute(value, axis, [(i, (i + by) % size) for i in range(size)])]
    ppermute x0 -> x7, starting transfers between devices: none -> 9.7 us  [shift(): lax.ppermute(value, axis, [(i, (i + by) % size) for i in range(size)])]
    pallas_call x2 -> x5, Pallas kernels: 22.8 us -> 28 us  [the longest x2 16.3 us: project(): pl.pallas_call(kernel, grid=(NX, NZ // tile), in_specs=[pl.BlockSpec((COL...]
    all_to_all x0 -> x1, starting transfers between devices: none -> 3.85 us  [spread(): return lax.all_to_all(wide, axes, 0, 0, tiled=True)]
    unnamed x9 -> x12, local copies, waits for them, and re-layouts: 6.83 us -> 3.99 us
  transfers between devices with their start and end apart: 4 -> 12, of which waited for: 4 -> 7; matrix products, arithmetic and copies ran while one was open for 0% -> 3% of each run, Pallas kernels for 6% -> 9%
where the time goes in v2:
time: 279 us; the launch traced here: 278 us
  blocking collectives  140 us (50%)
  waiting for transfers between devices  55.9 us (20%)
  Pallas kernels  43 us (15%)
  between operations  15 us (5%)
  starting transfers between devices  13.7 us (5%)
  local copies, waits for them, and re-layouts  6.75 us (2%)
  other arithmetic  4.25 us (2%)
    all_to_all x1, blocking collectives, body(): lax.all_to_all(packed, ('y', 'core'), 0, 0, tiled=True)  57.6 us
    all_to_all x1, blocking collectives, body(): part_b = lax.all_to_all(part_b, 'x', 0, 0, tiled=True)  35 us
    all_to_all x1, blocking collectives, body(): part_b = lax.all_to_all(part_b, 'z', 0, 0, tiled=True)  25.8 us
    ppermute x7, waiting for transfers between devices, shift(): lax.ppermute(value, axis, [(i, (i + by) % size) for i in range(size)])  24.5 us
    all_gather x1, waiting for transfers between devices, body(): full_a = lax.all_gather(new_a, 'z', axis=0, tiled=False)  21.5 us
    pallas_call x2, Pallas kernels, project(): pl.pallas_call(kernel, grid=(NX, NZ // tile), in_specs=[pl.BlockSpec((COL...  16.3 us
    pallas_call x1, Pallas kernels, attention(): pl.pallas_call(attention_kernel, grid=(GROUP,), in_specs=[pl.BlockSpec((L...  13.6 us
    all_to_all x1, blocking collectives, spread(): return lax.all_to_all(wide, axes, 0, 0, tiled=True)  11.4 us
  transfers between devices with their start and end apart: 12, of which 7 were waited for; matrix products, arithmetic and copies ran while one was open for 3% of the time, Pallas kernels for 9%

profile of v2, /device:TPU:1, one launch (start us, length us, event | category | flops | bytes accessed | tf_op | source)
XLA Modules:
  0.0 278.5 jit_solution(880951137772115418)
XLA Ops:
  7.9 2.9 %pack.1 = bf16[8,128,1280]{2,1,0:T(8,128)(2,1)} custom-call(bf16[128,4096]{1,0:T(8,128)(2,1)} %bitcast.24, bf16[128,1024]{1,0:T(8,128)(2,1)} %bitcast.27, bf16[128,1024]{1,0:T(8,128)(2,1)} %bitcast.28, bf16[128,4096]{1,0:T(8,128)(2,1)} %bitcast.25), custom_call_target="tpu_custom_call" | custom-call | bytes 5242880 | tf_op jit(solution)/shard_map/pack/pallas_call | solution.py:52
  10.9 57.6 %all_to_all.30 = bf16[8,128,1280]{2,1,0:T(8,128)(2,1)S(1)} all-to-all(bf16[8,128,1280]{2,1,0:T(8,128)(2,1)} %pack.1), channel_id=1, replica_groups=mesh['x'=4,'z'=8,'y'=4,'core'=2] {'y','core'}, dimensions={0} | all-to-all | bytes 5242880 | tf_op jit(solution)/shard_map/all_to_all | solution.py:299
  68.5 13.6 %attention_backward.1.grouped_ref = bf16[768,1024]{1,0:T(8,128)(2,1)S(1)} custom-call(bf16[1024,1280]{1,0:T(8,128)(2,1)S(1)} %bitcast.15, bf16[1024,1280]{1,0:T(8,128)(2,1)S(1)} %bitcast.16, bf16[1024,1280]{1,0:T(8,128)(2,1)S(1)} %bitcast.17, bf16[1024,1280]{1,0:T(8,128)(2,1)S(1)} %bitcast.18), custom_call_target="tpu_custom_call" | custom-call | flops 4294967296 | bytes 5242880 | tf_op jit(solution)/shard_map/attention_backward/pallas_call | solution.py:106
  82.1 3.4 %all-gather.7.cloned.1.call-done = bf16[1,1024,4096]{2,1,0:T(8,128)(2,1)} async-done(((bf16[1,128,4096]{2,1,0:T(8,128)(2,1)}), bf16[1,1024,4096]{2,1,0:T(8,128)(2,1)}) %all-gather.7.cloned.1.call-update) | async-done | bytes 8388624 | tf_op jit(solution)/shard_map/all_gather | solution.py:300
  85.5 8.5 %project_z.1 = bf16[8,4,448,128]{3,2,1,0:T(8,128)(2,1)S(1)} custom-call(bf16[768,1024]{1,0:T(8,128)(2,1)S(1)} %attention_backward.1.grouped_ref, bf16[1024,4096]{1,0:T(8,128)(2,1)} %bitcast.20), custom_call_target="tpu_custom_call" | custom-call | flops 3758096384 | bytes 14155776 | tf_op jit(solution)/shard_map/project_z/pallas_call | solution.py:149
  94.0 1.8 copy-done
  95.9 7.7 %project_x.1 = bf16[4,8,320,128]{3,2,1,0:T(8,128)(2,1)S(1)} custom-call(bf16[768,1024]{1,0:T(8,128)(2,1)S(1)} %attention_backward.1.grouped_ref, bf16[1024,4096]{1,0:T(8,128)(2,1)} %bitcast.21), custom_call_target="tpu_custom_call" | custom-call | flops 2684354560 | bytes 13107200 | tf_op jit(solution)/shard_map/project_x/pallas_call | solution.py:149
  103.7 35.0 %all_to_all.31 = bf16[4,8,320,128]{3,2,1,0:T(8,128)(2,1)} all-to-all(bf16[4,8,320,128]{3,2,1,0:T(8,128)(2,1)S(1)} %project_x.1), channel_id=1, replica_groups=mesh['x'=4,'z'=8,'y'=4,'core'=2] {'x'}, dimensions={0} | all-to-all | bytes 5242880 | tf_op jit(solution)/shard_map/all_to_all | solution.py:306
  138.7 2.4 reduce_sum.30
  141.0 25.8 %all_to_all.32.gb_ref = bf16[8,320,128]{2,1,0:T(8,128)(2,1)S(1)} all-to-all(bf16[8,320,128]{2,1,0:T(8,128)(2,1)S(1)} %reduce_sum.30), channel_id=1, replica_groups=mesh['x'=4,'z'=8,'y'=4,'core'=2] {'z'}, dimensions={0} | all-to-all | bytes 1310720 | tf_op jit(solution)/shard_map/all_to_all | solution.py:308
  166.9 10.0 %all_to_all.33.ga_ref = bf16[4,448,128]{2,1,0:T(8,128)(2,1)S(1)} all-to-all(bf16[4,448,128]{2,1,0:T(8,128)(2,1)} %bitcast.26), channel_id=1, replica_groups=mesh['x'=4,'z'=8,'y'=4,'core'=2] {'x'}, dimensions={0} | all-to-all | bytes 917504 | tf_op jit(solution)/shard_map/all_to_all | solution.py:309
  176.9 1.4 optimizer.1
  179.1 11.4 %all_to_all.34 = f32[8,8,128]{2,1,0:T(8,128)S(1)} all-to-all(f32[8,8,128]{2,1,0:T(8,128)S(1)} %broadcast_in_dim.4), channel_id=1, replica_groups=mesh['x'=4,'z'=8,'y'=4,'core'=2] {'y','core'}, dimensions={0} | all-to-all | bytes 65536 | tf_op jit(solution)/shard_map/all_to_all | solution.py:294
  191.1 3.8 %all-to-all-start.5 = ((f32[32,8,128]{2,1,0:T(8,128)}), f32[32,8,128]{2,1,0:T(8,128)S(1)}, u32[]{:S(2)}, u32[]{:S(2)}) async-start(f32[32,8,128]{2,1,0:T(8,128)} %broadcast_in_dim.5), calls=%async_computation.6 | async-start | bytes 262144 | tf_op jit(solution)/shard_map/all_to_all | solution.py:294
  195.0 1.2 collective-permute-start
  196.3 1.5 collective-permute-start.1
  197.8 1.5 collective-permute-start.2
  199.4 3.4 %collective-permute-done.a1 = bf16[2,64,768]{2,1,0:T(8,128)(2,1)S(1)} collective-permute-done((bf16[2,64,768]{2,1,0:T(8,128)(2,1)S(1)}, bf16[2,64,768]{2,1,0:T(8,128)(2,1)S(1)}, u32[]{:S(2)}, u32[]{:S(2)}) %collective-permute-start) | collective-permute-done | bytes 196640 | tf_op jit(solution)/shard_map/ppermute | solution.py:289
  202.8 5.7 %collective-permute-done.2.a3 = bf16[2,64,768]{2,1,0:T(8,128)(2,1)S(1)} collective-permute-done((bf16[2,64,768]{2,1,0:T(8,128)(2,1)S(1)}, bf16[2,64,768]{2,1,0:T(8,128)(2,1)S(1)}, u32[]{:S(2)}, u32[]{:S(2)}) %collective-permute-start.2) | collective-permute-done | bytes 196640 | tf_op jit(solution)/shard_map/ppermute | solution.py:289
  208.5 5.8 %all-gather.9.cloned.1.call-done = bf16[16,64,768]{2,1,0:T(8,128)(2,1)} async-done(((bf16[2,64,768]{2,1,0:T(8,128)(2,1)}), bf16[16,64,768]{2,1,0:T(8,128)(2,1)}) %all-gather.9.cloned.1.call-update) | async-done | bytes 1572880 | tf_op jit(solution)/shard_map/all_gather | solution.py:320
  214.3 1.4 copy-done.1
  215.7 1.5 apply.1
  217.2 1.3 collective-permute-start.3
  218.5 1.4 collective-permute-start.4
  220.0 13.8 %collective-permute-done.3.b1 = bf16[8,64,768]{2,1,0:T(8,128)(2,1)S(1)} collective-permute-done((bf16[8,64,768]{2,1,0:T(8,128)(2,1)S(1)}, bf16[8,64,768]{2,1,0:T(8,128)(2,1)S(1)}, u32[]{:S(2)}, u32[]{:S(2)}) %collective-permute-start.3) | collective-permute-done | bytes 786464 | tf_op jit(solution)/shard_map/ppermute | solution.py:289
  233.8 0.8 slice.16
  234.7 0.8 slice.17
  235.5 2.6 collective-permute-start.6
  239.8 1.8 broadcast_multiply_fusion
  241.6 1.5 collective-permute-done.5.b3
  243.1 21.5 %all-gather.11.cloned.1.call-done = bf16[32,64,768]{2,1,0:T(8,128)(2,1)} async-done(((bf16[4,64,768]{2,1,0:T(8,128)(2,1)}), bf16[32,64,768]{2,1,0:T(8,128)(2,1)}) %all-gather.11.cloned.1.call-update) | async-done | bytes 3145744 | tf_op jit(solution)/shard_map/all_gather | solution.py:323
  264.6 7.3 %join.1 = bf16[4,8,128,768]{3,2,1,0:T(8,128)(2,1)} custom-call(s32[4]{0:T(128)S(1)} %pad_add_fusion.place_ref, bf16[8,4,64,768]{3,2,1,0:T(8,128)(2,1)} %bitcast.23, bf16[8,64,768]{2,1,0:T(8,128)(2,1)S(1)} %get-tuple-element.19.b0, bf16[8,64,768]{2,1,0:T(8,128)(2,1)S(1)} %collective-permute-done.3.b1, bf16[8,64,768]{2,1,0:T(8,128)(2,1)S(1)} %collective-permute-done.4.b2, ...), custom_call_target="tpu_custom_call" | custom-call | bytes 13631488 | tf_op jit(solution)/shard_map/join/pallas_call | solution.py:264
  (30 shorter events, 3.1 us)
Async XLA Ops:
  7.2 78.3 %all-gather.7.cloned.1.call-start = ((), (), s32[]{:S(2)}) async-start(), calls=%async_computation.8 | async-start | bytes 9437184 | tf_op jit(solution)/shard_map/all_gather | solution.py:300
  7.9 158.9 %reduce-scatter.2.cloned.1.call-start = ((), (), s32[]{:S(2)}) async-start(), calls=%async_computation.7 | async-start | bytes 4128768 | tf_op jit(solution)/shard_map/reduce_scatter | solution.py:305
  94.0 1.8 copy-start
  95.9 118.4 %all-gather.9.cloned.1.call-start = ((), (), s32[]{:S(2)}) async-start(), calls=%async_computation.9 | async-start | bytes 1769472 | tf_op jit(solution)/shard_map/all_gather | solution.py:320
  138.6 38.2 %copy-start.2 = (f32[128,768]{1,0:T(8,128)S(1)}, f32[128,768]{1,0:T(8,128)}, u32[]{:S(2)}) copy-start(f32[128,768]{1,0:T(8,128)} %w_ref.1) | copy-start | bytes 1179652
  138.6 38.2 %copy-start.3 = (f32[128,768]{1,0:T(8,128)S(1)}, f32[128,768]{1,0:T(8,128)}, u32[]{:S(2)}) copy-start(f32[128,768]{1,0:T(8,128)} %m_ref.1) | copy-start | bytes 1179652
  138.7 38.2 %copy-start.4 = (f32[128,768]{1,0:T(8,128)S(1)}, f32[128,768]{1,0:T(8,128)}, u32[]{:S(2)}) copy-start(f32[128,768]{1,0:T(8,128)} %v_ref.1) | copy-start | bytes 1179652
  178.3 0.7 copy-start.5
  191.1 17.4 %all-to-all-start.5 = ((f32[32,8,128]{2,1,0:T(8,128)}), f32[32,8,128]{2,1,0:T(8,128)S(1)}, u32[]{:S(2)}, u32[]{:S(2)}) async-start(f32[32,8,128]{2,1,0:T(8,128)} %broadcast_in_dim.5), calls=%async_computation.6 | async-start | bytes 262144 | tf_op jit(solution)/shard_map/all_to_all | solution.py:294
  195.0 69.7 %all-gather.11.cloned.1.call-start = ((), (), s32[]{:S(2)}) async-start(), calls=%async_computation.10 | async-start | bytes 3538944 | tf_op jit(solution)/shard_map/all_gather | solution.py:323
  195.0 7.8 %collective-permute-start = (bf16[2,64,768]{2,1,0:T(8,128)(2,1)S(1)}, bf16[2,64,768]{2,1,0:T(8,128)(2,1)S(1)}, u32[]{:S(2)}, u32[]{:S(2)}) collective-permute-start(bf16[2,64,768]{2,1,0:T(8,128)(2,1)S(1)} %get-tuple-element.16.a0), channel_id=1, source_target_pairs={{0,64},{64,128},{128,192},{192,0},{1,65},{65,129},{129,193},{193,1... | collective-permute-start | bytes 589832 | tf_op jit(solution)/shard_map/ppermute | solution.py:289
  196.3 6.5 %collective-permute-start.1 = (bf16[2,64,768]{2,1,0:T(8,128)(2,1)S(1)}, bf16[2,64,768]{2,1,0:T(8,128)(2,1)S(1)}, u32[]{:S(2)}, u32[]{:S(2)}) collective-permute-start(bf16[2,64,768]{2,1,0:T(8,128)(2,1)S(1)} %get-tuple-element.16.a0), channel_id=1, source_target_pairs={{0,192},{64,0},{128,64},{192,128},{1,193},{65,1},{129,65},{193,129... | collective-permute-start | bytes 589832 | tf_op jit(solution)/shard_map/ppermute | solution.py:289
  197.8 10.7 %collective-permute-start.2 = (bf16[2,64,768]{2,1,0:T(8,128)(2,1)S(1)}, bf16[2,64,768]{2,1,0:T(8,128)(2,1)S(1)}, u32[]{:S(2)}, u32[]{:S(2)}) collective-permute-start(bf16[2,64,768]{2,1,0:T(8,128)(2,1)S(1)} %get-tuple-element.16.a0), channel_id=1, source_target_pairs={{0,128},{64,192},{128,0},{192,64},{1,129},{65,193},{129,1},{193,65... | collective-permute-start | bytes 589832 | tf_op jit(solution)/shard_map/ppermute | solution.py:289
  214.3 1.4 copy-start.1
  217.2 16.6 %collective-permute-start.3 = (bf16[8,64,768]{2,1,0:T(8,128)(2,1)S(1)}, bf16[8,64,768]{2,1,0:T(8,128)(2,1)S(1)}, u32[]{:S(2)}, u32[]{:S(2)}) collective-permute-start(bf16[8,64,768]{2,1,0:T(8,128)(2,1)S(1)} %get-tuple-element.19.b0), channel_id=1, source_target_pairs={{0,64},{64,128},{128,192},{192,0},{1,65},{65,129},{129,193},{193,1... | collective-permute-start | bytes 2359304 | tf_op jit(solution)/shard_map/ppermute | solution.py:289
  218.5 16.1 %collective-permute-start.4 = (bf16[8,64,768]{2,1,0:T(8,128)(2,1)S(1)}, bf16[8,64,768]{2,1,0:T(8,128)(2,1)S(1)}, u32[]{:S(2)}, u32[]{:S(2)}) collective-permute-start(bf16[8,64,768]{2,1,0:T(8,128)(2,1)S(1)} %get-tuple-element.19.b0), channel_id=1, source_target_pairs={{0,192},{64,0},{128,64},{192,128},{1,193},{65,1},{129,65},{193,129... | collective-permute-start | bytes 2359304 | tf_op jit(solution)/shard_map/ppermute | solution.py:289
  234.6 8.4 %collective-permute-start.5 = (bf16[4,64,768]{2,1,0:T(8,128)(2,1)}, bf16[4,64,768]{2,1,0:T(8,128)(2,1)S(1)}, u32[]{:S(2)}, u32[]{:S(2)}) collective-permute-start(bf16[4,64,768]{2,1,0:T(8,128)(2,1)} %slice.16), channel_id=1, source_target_pairs={{0,64},{64,128},{128,192},{192,0},{1,65},{65,129},{129,193},{193,1... | collective-permute-start | bytes 1179656 | tf_op jit(solution)/shard_map/ppermute | solution.py:289
  235.5 7.6 %collective-permute-start.6 = (bf16[4,64,768]{2,1,0:T(8,128)(2,1)}, bf16[4,64,768]{2,1,0:T(8,128)(2,1)S(1)}, u32[]{:S(2)}, u32[]{:S(2)}) collective-permute-start(bf16[4,64,768]{2,1,0:T(8,128)(2,1)} %slice.17), channel_id=1, source_target_pairs={{0,192},{64,0},{128,64},{192,128},{1,193},{65,1},{129,65},{193,129... | collective-permute-start | bytes 1179656 | tf_op jit(solution)/shard_map/ppermute | solution.py:289
Sparse Core Ops, SparseCore 0:
  9.9 75.5 all-gather.6
  96.0 50.3 reduce-scatter.1
  179.2 35.0 all-gather.8
  217.3 47.2 all-gather.10

commit v3 on v2

--- a/solution.py
+++ b/solution.py
@@ -16,7 +16,7 @@
 ROWS = 128
 PACKED = 1280
 BLOCK = 256
-COLS_A = 448
+COLS_A = 480
 COLS_B = COLS - COLS_A
 ROWS_A = 64
 ROWS_B = ROWS - ROWS_A
@@ -127,41 +127,33 @@
     )(packed, packed, packed, packed)
 
 
-def project(grouped, x, lo, hi, z_major):
-    cols = hi - lo
+def project_kernel(grouped_ref, x_ref, a_ref, b_ref):
+    res = dot(grouped_ref[...], x_ref[...], 1, 0).astype(bf16)
+    for i in range(a_ref.shape[0]):
+        a_ref[i, 0] = res[:COLS_A, i * ROWS : (i + 1) * ROWS]
+        b_ref[0, i] = res[COLS_A:, i * ROWS : (i + 1) * ROWS]
+
+
+def project(grouped, x):
     tile = 4
-
-    def kernel(grouped_ref, x_ref, out_ref):
-        res = dot(grouped_ref[lo:hi, :], x_ref[...], 1, 0).astype(bf16)
-        for i in range(tile):
-            piece = res[:, i * ROWS : (i + 1) * ROWS]
-            if z_major:
-                out_ref[i, 0] = piece
-            else:
-                out_ref[0, i] = piece
-
-    if z_major:
-        shape, block = (NZ, NX, cols, ROWS), (tile, 1, cols, ROWS)
-        place = lambda x, z: (z, x, 0, 0)
-    else:
-        shape, block = (NX, NZ, cols, ROWS), (1, tile, cols, ROWS)
-        place = lambda x, z: (x, z, 0, 0)
-    return pl.pallas_call(
-        kernel,
+    return pl.pallas_call(
+        project_kernel,
         grid=(NX, NZ // tile),
         in_specs=[
             pl.BlockSpec((COLS, LENGTH), lambda x, z: (0, 0)),
             pl.BlockSpec((LENGTH, ROWS * tile), lambda x, z: (0, x * (NZ // tile) + z)),
         ],
-        out_specs=pl.BlockSpec(block, place),
-        out_shape=jax.ShapeDtypeStruct(shape, bf16),
-        compiler_params=pltpu.CompilerParams(vmem_limit_bytes=48 << 20),
-        cost_estimate=pl.CostEstimate(
-            flops=2 * cols * LENGTH * WIDTH,
-            bytes_accessed=(10 << 20) + 2 * cols * WIDTH,
-            transcendentals=0,
-        ),
-        name="project_z" if z_major else "project_x",
+        out_specs=[
+            pl.BlockSpec((tile, 1, COLS_A, ROWS), lambda x, z: (z, x, 0, 0)),
+            pl.BlockSpec((1, tile, COLS_B, ROWS), lambda x, z: (x, z, 0, 0)),
+        ],
+        out_shape=[
+            jax.ShapeDtypeStruct((NZ, NX, COLS_A, ROWS), bf16),
+            jax.ShapeDtypeStruct((NX, NZ, COLS_B, ROWS), bf16),
+        ],
+        compiler_params=pltpu.CompilerParams(vmem_limit_bytes=60 << 20),
+        cost_estimate=pl.CostEstimate(flops=6 << 30, bytes_accessed=16 << 20, transcendentals=0),
+        name="project",
     )(grouped, x)
 
 
@@ -234,24 +226,25 @@
     )(place, sums, *pieces, gathered)
 
 
-def join_kernel(place_ref, a_ref, b0, b1, b2, b3, b4, out_ref):
+FULL = (NX, NZ, ROWS, COLS)
+
+
+def join_x_kernel(place_ref, b0, b1, b2, b3, b4, out_ref):
     step, half = pl.program_id(0), pl.program_id(1)
-    for z in range(a_ref.shape[0]):
-        out_ref[0, z, 0:ROWS_A, :] = a_ref[z, 0]
     for k, ref in enumerate((b0, b1, b2)):
 
         @pl.when(step == k)
         def _(ref=ref):
-            out_ref[0, :, ROWS_A:ROWS, :] = ref[...]
+            out_ref[0] = ref[...]
 
     for k, ref in enumerate((b3, b4)):
 
         @pl.when((step == 3) & (half == k))
         def _(ref=ref):
-            out_ref[0, :, ROWS_A:ROWS, :] = ref[...]
-
-
-def join(place, a_full, own, before, after, far_lo, far_hi):
+            out_ref[0] = ref[...]
+
+
+def join_x(place, own, before, after, far_lo, far_hi):
     half = NZ // 2
 
     def b_spec(k):
@@ -262,27 +255,42 @@
 
     whole = pl.BlockSpec((half, ROWS_B, COLS), lambda o, h, place: (0, 0, 0))
     return pl.pallas_call(
-        join_kernel,
+        join_x_kernel,
         grid_spec=pltpu.PrefetchScalarGridSpec(
             num_scalar_prefetch=1,
             grid=(NX, 2),
-            in_specs=[
-                pl.BlockSpec((half, 1, ROWS_A, COLS), lambda o, h, place: (h, place[o], 0, 0)),
-                b_spec(0),
-                b_spec(1),
-                b_spec(2),
-                whole,
-                whole,
-            ],
+            in_specs=[b_spec(0), b_spec(1), b_spec(2), whole, whole],
             out_specs=pl.BlockSpec(
-                (1, half, ROWS, COLS), lambda o, h, place: (place[o], h, 0, 0)
+                (1, half, ROWS_B, COLS),
+                lambda o, h, place: (place[o], h, ROWS_A // ROWS_B, 0),
             ),
         ),
-        out_shape=jax.ShapeDtypeStruct((NX, NZ, ROWS, COLS), bf16),
+        out_shape=jax.ShapeDtypeStruct(FULL, bf16),
         compiler_params=pltpu.CompilerParams(vmem_limit_bytes=48 << 20),
-        cost_estimate=pl.CostEstimate(flops=0, bytes_accessed=13 << 20, transcendentals=0),
-        name="join",
-    )(place, a_full, own, before, after, far_lo, far_hi)
+        cost_estimate=pl.CostEstimate(flops=0, bytes_accessed=7 << 20, transcendentals=0),
+        name="join_x",
+    )(place, own, before, after, far_lo, far_hi)
+
+
+def join_sc_kernel(base_ref, a_ref, out_ref):
+    out_ref[0] = a_ref[:, 0]
+
+
+def join_sc(base, full):
+    return pl.pallas_call(
+        join_sc_kernel,
+        grid=(NX,),
+        in_specs=[
+            pl.BlockSpec(memory_space=pl.ANY),
+            pl.BlockSpec((NZ, 1, ROWS_A, COLS), lambda x: (0, x, 0, 0)),
+        ],
+        out_specs=pl.BlockSpec((1, NZ, ROWS_A, COLS), lambda x: (x, 0, 0, 0)),
+        out_shape=jax.ShapeDtypeStruct(FULL, bf16),
+        input_output_aliases={0: 0},
+        compiler_params=pltpu.CompilerParams(vmem_limit_bytes=48 << 20),
+        cost_estimate=pl.CostEstimate(flops=0, bytes_accessed=4 << 20, transcendentals=0),
+        name="join_sc",
+    )(base, full)
 
 
 def shift(value, axis, size, by):
@@ -300,8 +308,7 @@
     x_full = lax.all_gather(x[0], ("y", "core"), axis=0, tiled=True)
     grouped = attention(heads)
 
-    part_a = project(grouped, x_full, 0, COLS_A, True)
-    part_b = project(grouped, x_full, COLS_A, COLS, False)
+    part_a, part_b = project(grouped, x_full)
     part_a = lax.psum_scatter(part_a, "z", scatter_dimension=0, tiled=True)[0]
     part_b = lax.all_to_all(part_b, "x", 0, 0, tiled=True)
     part_b = jnp.sum(part_b.astype(f32), axis=0).astype(bf16)
@@ -324,7 +331,8 @@
     before, after = shift(new_b, "x", NX, 1), shift(new_b, "x", NX, -1)
     far_lo = shift(before[: NZ // 2], "x", NX, 1)
     far_hi = shift(after[NZ // 2 :], "x", NX, -1)
-    new_weights = join(place, full_a, new_b, before, after, far_lo, far_hi)
+    new_weights = join_x(place, new_b, before, after, far_lo, far_hi)
+    new_weights = join_sc(new_weights, full_a)
 
     total = jnp.sum(sums, axis=0)
     lamb_update = (jnp.sqrt(total[0, 0]) / jnp.sqrt(total[1, 0])) * direction

time: 279 us -> 276 us (0.989)
  Pallas kernels: 43 us -> 38 us
  waiting for transfers between devices: 55.9 us -> 50.9 us
  local copies, waits for them, and re-layouts: 6.75 us -> 9.57 us
    all_gather x1, waiting for transfers between devices: 21.5 us -> 14.7 us  [body(): full_a = lax.all_gather(new_a, 'z', axis=0, tiled=False)]
    pallas_call x3, Pallas kernels: 23.6 us -> 18.5 us  [the longest x1 12.4 us: project(): pl.pallas_call(project_kernel, grid=(NX, NZ // tile), in_specs=[pl.BlockS...]
    all_to_all x1, blocking collectives: 25.8 us -> 30 us  [body(): part_b = lax.all_to_all(part_b, 'z', 0, 0, tiled=True)]
    all_to_all x1, blocking collectives: 35 us -> 32.1 us  [body(): part_b = lax.all_to_all(part_b, 'x', 0, 0, tiled=True)]
    unnamed x12 -> x16, local copies, waits for them, and re-layouts: 3.99 us -> 6.79 us
  transfers between devices with their start and end apart: 12 -> 12, of which waited for: 7 -> 9; matrix products, arithmetic and copies ran while one was open for 3% -> 2% of each run, Pallas kernels for 9% -> 7%
where the time goes in v3:
time: 276 us; the launch traced here: 275 us
  blocking collectives  142 us (51%)
  waiting for transfers between devices  50.9 us (18%)
  Pallas kernels  38 us (14%)
  starting transfers between devices  15.3 us (6%)
  between operations  15.1 us (5%)
  local copies, waits for them, and re-layouts  9.57 us (3%)
  other arithmetic  4.1 us (1%)
    all_to_all x1, blocking collectives, body(): lax.all_to_all(packed, ('y', 'core'), 0, 0, tiled=True)  57.6 us
    all_to_all x1, blocking collectives, body(): part_b = lax.all_to_all(part_b, 'x', 0, 0, tiled=True)  32.1 us
    all_to_all x1, blocking collectives, body(): part_b = lax.all_to_all(part_b, 'z', 0, 0, tiled=True)  30 us
    ppermute x7, waiting for transfers between devices, shift(): lax.ppermute(value, axis, [(i, (i + by) % size) for i in range(size)])  26.7 us
    all_gather x1, waiting for transfers between devices, body(): full_a = lax.all_gather(new_a, 'z', axis=0, tiled=False)  14.7 us
    pallas_call x1, Pallas kernels, attention(): pl.pallas_call(attention_kernel, grid=(GROUP,), in_specs=[pl.BlockSpec((L...  13.6 us
    pallas_call x1, Pallas kernels, project(): pl.pallas_call(project_kernel, grid=(NX, NZ // tile), in_specs=[pl.BlockS...  12.4 us
    all_to_all x1, blocking collectives, body(): part_a = lax.all_to_all(part_a, 'x', 0, 0, tiled=True)  11.5 us
  transfers between devices with their start and end apart: 12, of which 9 were waited for; matrix products, arithmetic and copies ran while one was open for 2% of the time, Pallas kernels for 7%

profile of v3, /device:TPU:1, one launch (start us, length us, event | category | flops | bytes accessed | tf_op | source)
XLA Modules:
  0.0 275.3 jit_solution(15126314633540249037)
XLA Ops:
  7.9 2.9 %pack.1 = bf16[8,128,1280]{2,1,0:T(8,128)(2,1)} custom-call(bf16[128,4096]{1,0:T(8,128)(2,1)} %bitcast.22, bf16[128,1024]{1,0:T(8,128)(2,1)} %bitcast.25, bf16[128,1024]{1,0:T(8,128)(2,1)} %bitcast.26, bf16[128,4096]{1,0:T(8,128)(2,1)} %bitcast.23), custom_call_target="tpu_custom_call" | custom-call | bytes 5242880 | tf_op jit(solution)/shard_map/pack/pallas_call | solution.py:52
  10.9 57.6 %all_to_all.30 = bf16[8,128,1280]{2,1,0:T(8,128)(2,1)S(1)} all-to-all(bf16[8,128,1280]{2,1,0:T(8,128)(2,1)} %pack.1), channel_id=1, replica_groups=mesh['x'=4,'z'=8,'y'=4,'core'=2] {'y','core'}, dimensions={0} | all-to-all | bytes 5242880 | tf_op jit(solution)/shard_map/all_to_all | solution.py:307
  68.5 13.6 %attention_backward.1.grouped_ref = bf16[768,1024]{1,0:T(8,128)(2,1)S(1)} custom-call(bf16[1024,1280]{1,0:T(8,128)(2,1)S(1)} %bitcast.16, bf16[1024,1280]{1,0:T(8,128)(2,1)S(1)} %bitcast.17, bf16[1024,1280]{1,0:T(8,128)(2,1)S(1)} %bitcast.18, bf16[1024,1280]{1,0:T(8,128)(2,1)S(1)} %bitcast.19), custom_call_target="tpu_custom_call" | custom-call | flops 4294967296 | bytes 5242880 | tf_op jit(solution)/shard_map/attention_backward/pallas_call | solution.py:106
  82.1 1.1 copy-done.6
  83.2 2.3 all-gather.7.cloned.1.call-done
  85.5 12.4 %project.1 = (bf16[8,4,480,128]{3,2,1,0:T(8,128)(2,1)}, bf16[4,8,288,128]{3,2,1,0:T(8,128)(2,1)}) custom-call(bf16[768,1024]{1,0:T(8,128)(2,1)} %copy-done.6, bf16[1024,4096]{1,0:T(8,128)(2,1)} %bitcast.27), custom_call_target="tpu_custom_call" | custom-call | flops 6442450944 | bytes 16777216 | tf_op jit(solution)/shard_map/project/pallas_call | solution.py:139
  97.9 1.6 copy-done.7
  99.5 32.1 %all_to_all.31 = bf16[4,8,288,128]{3,2,1,0:T(8,128)(2,1)} all-to-all(bf16[4,8,288,128]{3,2,1,0:T(8,128)(2,1)S(1)} %copy-done.7), channel_id=1, replica_groups=mesh['x'=4,'z'=8,'y'=4,'core'=2] {'x'}, dimensions={0} | all-to-all | bytes 4718592 | tf_op jit(solution)/shard_map/all_to_all | solution.py:313
  131.6 2.2 reduce_sum.30
  133.9 30.0 %all_to_all.32.gb_ref = bf16[8,288,128]{2,1,0:T(8,128)(2,1)S(1)} all-to-all(bf16[8,288,128]{2,1,0:T(8,128)(2,1)S(1)} %reduce_sum.30), channel_id=1, replica_groups=mesh['x'=4,'z'=8,'y'=4,'core'=2] {'z'}, dimensions={0} | all-to-all | bytes 1179648 | tf_op jit(solution)/shard_map/all_to_all | solution.py:315
  163.9 11.5 %all_to_all.33.ga_ref = bf16[4,480,128]{2,1,0:T(8,128)(2,1)S(1)} all-to-all(bf16[4,480,128]{2,1,0:T(8,128)(2,1)} %bitcast.24), channel_id=1, replica_groups=mesh['x'=4,'z'=8,'y'=4,'core'=2] {'x'}, dimensions={0} | all-to-all | bytes 983040 | tf_op jit(solution)/shard_map/all_to_all | solution.py:316
  175.4 1.4 optimizer.1
  177.6 11.1 %all_to_all.34 = f32[8,8,128]{2,1,0:T(8,128)S(1)} all-to-all(f32[8,8,128]{2,1,0:T(8,128)S(1)} %broadcast_in_dim.4), channel_id=1, replica_groups=mesh['x'=4,'z'=8,'y'=4,'core'=2] {'y','core'}, dimensions={0} | all-to-all | bytes 65536 | tf_op jit(solution)/shard_map/all_to_all | solution.py:302
  189.3 5.0 %all-to-all-start.5 = ((f32[32,8,128]{2,1,0:T(8,128)}), f32[32,8,128]{2,1,0:T(8,128)S(1)}, u32[]{:S(2)}, u32[]{:S(2)}) async-start(f32[32,8,128]{2,1,0:T(8,128)} %broadcast_in_dim.5), calls=%async_computation.6 | async-start | bytes 262144 | tf_op jit(solution)/shard_map/all_to_all | solution.py:302
  194.4 2.8 %collective-permute-start.2 = (bf16[2,64,768]{2,1,0:T(8,128)(2,1)S(1)}, bf16[2,64,768]{2,1,0:T(8,128)(2,1)S(1)}, u32[]{:S(2)}, u32[]{:S(2)}) collective-permute-start(bf16[2,64,768]{2,1,0:T(8,128)(2,1)S(1)} %get-tuple-element.20.a0), channel_id=1, source_target_pairs={{0,128},{64,192},{128,0},{192,64},{1,129},{65,193},{129,1},{193,65... | collective-permute-start | bytes 589832 | tf_op jit(solution)/shard_map/ppermute | solution.py:297
  197.2 0.9 collective-permute-start.1
  198.7 3.2 %collective-permute-done.2.a3 = bf16[2,64,768]{2,1,0:T(8,128)(2,1)S(1)} collective-permute-done((bf16[2,64,768]{2,1,0:T(8,128)(2,1)S(1)}, bf16[2,64,768]{2,1,0:T(8,128)(2,1)S(1)}, u32[]{:S(2)}, u32[]{:S(2)}) %collective-permute-start.2) | collective-permute-done | bytes 196640 | tf_op jit(solution)/shard_map/ppermute | solution.py:297
  201.9 5.4 %collective-permute-done.1.a2 = bf16[2,64,768]{2,1,0:T(8,128)(2,1)S(1)} collective-permute-done((bf16[2,64,768]{2,1,0:T(8,128)(2,1)S(1)}, bf16[2,64,768]{2,1,0:T(8,128)(2,1)S(1)}, u32[]{:S(2)}, u32[]{:S(2)}) %collective-permute-start.1) | collective-permute-done | bytes 196640 | tf_op jit(solution)/shard_map/ppermute | solution.py:297
  207.6 6.6 %all-gather.9.cloned.1.call-done = bf16[16,64,768]{2,1,0:T(8,128)(2,1)} async-done(((bf16[2,64,768]{2,1,0:T(8,128)(2,1)}), bf16[16,64,768]{2,1,0:T(8,128)(2,1)}) %all-gather.9.cloned.1.call-update) | async-done | bytes 1572880 | tf_op jit(solution)/shard_map/all_gather | solution.py:327
  214.1 1.4 copy-done.1
  215.5 1.5 apply.1
  217.0 2.4 collective-permute-start.4
  219.5 13.1 %collective-permute-done.4.b2 = bf16[8,64,768]{2,1,0:T(8,128)(2,1)S(1)} collective-permute-done((bf16[8,64,768]{2,1,0:T(8,128)(2,1)S(1)}, bf16[8,64,768]{2,1,0:T(8,128)(2,1)S(1)}, u32[]{:S(2)}, u32[]{:S(2)}) %collective-permute-start.4) | collective-permute-done | bytes 786464 | tf_op jit(solution)/shard_map/ppermute | solution.py:297
  232.6 0.8 slice.17
  233.4 3.4 %collective-permute-start.6 = (bf16[4,64,768]{2,1,0:T(8,128)(2,1)}, bf16[4,64,768]{2,1,0:T(8,128)(2,1)S(1)}, u32[]{:S(2)}, u32[]{:S(2)}) collective-permute-start(bf16[4,64,768]{2,1,0:T(8,128)(2,1)} %slice.17), channel_id=1, source_target_pairs={{0,192},{64,0},{128,64},{192,128},{1,193},{65,1},{129,65},{193,129... | collective-permute-start | bytes 1179656 | tf_op jit(solution)/shard_map/ppermute | solution.py:297
  236.8 0.8 slice.16
  239.5 1.8 broadcast_multiply_fusion
  241.9 4.2 %collective-permute-done.5.b3 = bf16[4,64,768]{2,1,0:T(8,128)(2,1)S(1)} collective-permute-done((bf16[4,64,768]{2,1,0:T(8,128)(2,1)}, bf16[4,64,768]{2,1,0:T(8,128)(2,1)S(1)}, u32[]{:S(2)}, u32[]{:S(2)}) %collective-permute-start.5) | collective-permute-done | bytes 393248 | tf_op jit(solution)/shard_map/ppermute | solution.py:297
  246.0 3.9 %join_x.1.base_ref = bf16[4,8,128,768]{3,2,1,0:T(8,128)(2,1)} custom-call(s32[4]{0:T(128)S(1)} %pad_add_fusion.place_ref, bf16[8,64,768]{2,1,0:T(8,128)(2,1)S(1)} %get-tuple-element.22.b0, bf16[8,64,768]{2,1,0:T(8,128)(2,1)S(1)} %collective-permute-done.3.b1, bf16[8,64,768]{2,1,0:T(8,128)(2,1)S(1)} %collective-permute-done.4.b2, ...), custom_call_target="tpu_custom_call" | custom-call | bytes 7340032 | tf_op jit(solution)/shard_map/join_x/pallas_call | solution.py:257
  249.9 14.7 %all-gather.11.cloned.1.call-done = bf16[32,64,768]{2,1,0:T(8,128)(2,1)} async-done(((bf16[4,64,768]{2,1,0:T(8,128)(2,1)}), bf16[32,64,768]{2,1,0:T(8,128)(2,1)}) %all-gather.11.cloned.1.call-update) | async-done | bytes 3145744 | tf_op jit(solution)/shard_map/all_gather | solution.py:330
  264.6 1.9 copy-done
  266.5 2.3 join_sc.1
  (34 shorter events, 4.5 us)
Async XLA Ops:
  7.2 78.3 %all-gather.7.cloned.1.call-start = ((), (), s32[]{:S(2)}) async-start(), calls=%async_computation.8 | async-start | bytes 9437184 | tf_op jit(solution)/shard_map/all_gather | solution.py:308
  7.9 156.0 %reduce-scatter.2.cloned.1.call-start = ((), (), s32[]{:S(2)}) async-start(), calls=%async_computation.7 | async-start | bytes 4423680 | tf_op jit(solution)/shard_map/reduce_scatter | solution.py:312
  82.1 1.2 copy-start.6
  97.9 1.7 copy-start.7
  97.9 116.2 %all-gather.9.cloned.1.call-start = ((), (), s32[]{:S(2)}) async-start(), calls=%async_computation.9 | async-start | bytes 1769472 | tf_op jit(solution)/shard_map/all_gather | solution.py:327
  131.6 43.8 %copy-start.3 = (f32[128,768]{1,0:T(8,128)S(1)}, f32[128,768]{1,0:T(8,128)}, u32[]{:S(2)}) copy-start(f32[128,768]{1,0:T(8,128)} %w_ref.1) | copy-start | bytes 1179652
  131.6 43.8 %copy-start.4 = (f32[128,768]{1,0:T(8,128)S(1)}, f32[128,768]{1,0:T(8,128)}, u32[]{:S(2)}) copy-start(f32[128,768]{1,0:T(8,128)} %m_ref.1) | copy-start | bytes 1179652
  131.6 43.8 %copy-start.5 = (f32[128,768]{1,0:T(8,128)S(1)}, f32[128,768]{1,0:T(8,128)}, u32[]{:S(2)}) copy-start(f32[128,768]{1,0:T(8,128)} %v_ref.1) | copy-start | bytes 1179652
  176.8 0.7 copy-start.2
  189.3 18.2 %all-to-all-start.5 = ((f32[32,8,128]{2,1,0:T(8,128)}), f32[32,8,128]{2,1,0:T(8,128)S(1)}, u32[]{:S(2)}, u32[]{:S(2)}) async-start(f32[32,8,128]{2,1,0:T(8,128)} %broadcast_in_dim.5), calls=%async_computation.6 | async-start | bytes 262144 | tf_op jit(solution)/shard_map/all_to_all | solution.py:302
  194.3 70.3 %all-gather.11.cloned.1.call-start = ((), (), s32[]{:S(2)}) async-start(), calls=%async_computation.10 | async-start | bytes 3538944 | tf_op jit(solution)/shard_map/all_gather | solution.py:330
  194.4 7.5 %collective-permute-start.2 = (bf16[2,64,768]{2,1,0:T(8,128)(2,1)S(1)}, bf16[2,64,768]{2,1,0:T(8,128)(2,1)S(1)}, u32[]{:S(2)}, u32[]{:S(2)}) collective-permute-start(bf16[2,64,768]{2,1,0:T(8,128)(2,1)S(1)} %get-tuple-element.20.a0), channel_id=1, source_target_pairs={{0,128},{64,192},{128,0},{192,64},{1,129},{65,193},{129,1},{193,65... | collective-permute-start | bytes 589832 | tf_op jit(solution)/shard_map/ppermute | solution.py:297
  197.2 10.1 %collective-permute-start.1 = (bf16[2,64,768]{2,1,0:T(8,128)(2,1)S(1)}, bf16[2,64,768]{2,1,0:T(8,128)(2,1)S(1)}, u32[]{:S(2)}, u32[]{:S(2)}) collective-permute-start(bf16[2,64,768]{2,1,0:T(8,128)(2,1)S(1)} %get-tuple-element.20.a0), channel_id=1, source_target_pairs={{0,192},{64,0},{128,64},{192,128},{1,193},{65,1},{129,65},{193,129... | collective-permute-start | bytes 589832 | tf_op jit(solution)/shard_map/ppermute | solution.py:297
  198.1 9.5 %collective-permute-start = (bf16[2,64,768]{2,1,0:T(8,128)(2,1)S(1)}, bf16[2,64,768]{2,1,0:T(8,128)(2,1)S(1)}, u32[]{:S(2)}, u32[]{:S(2)}) collective-permute-start(bf16[2,64,768]{2,1,0:T(8,128)(2,1)S(1)} %get-tuple-element.20.a0), channel_id=1, source_target_pairs={{0,64},{64,128},{128,192},{192,0},{1,65},{65,129},{129,193},{193,1... | collective-permute-start | bytes 589832 | tf_op jit(solution)/shard_map/ppermute | solution.py:297
  214.1 1.4 copy-start.1
  217.0 15.6 %collective-permute-start.4 = (bf16[8,64,768]{2,1,0:T(8,128)(2,1)S(1)}, bf16[8,64,768]{2,1,0:T(8,128)(2,1)S(1)}, u32[]{:S(2)}, u32[]{:S(2)}) collective-permute-start(bf16[8,64,768]{2,1,0:T(8,128)(2,1)S(1)} %get-tuple-element.22.b0), channel_id=1, source_target_pairs={{0,192},{64,0},{128,64},{192,128},{1,193},{65,1},{129,65},{193,129... | collective-permute-start | bytes 2359304 | tf_op jit(solution)/shard_map/ppermute | solution.py:297
  219.5 17.3 %collective-permute-start.3 = (bf16[8,64,768]{2,1,0:T(8,128)(2,1)S(1)}, bf16[8,64,768]{2,1,0:T(8,128)(2,1)S(1)}, u32[]{:S(2)}, u32[]{:S(2)}) collective-permute-start(bf16[8,64,768]{2,1,0:T(8,128)(2,1)S(1)} %get-tuple-element.22.b0), channel_id=1, source_target_pairs={{0,64},{64,128},{128,192},{192,0},{1,65},{65,129},{129,193},{193,1... | collective-permute-start | bytes 2359304 | tf_op jit(solution)/shard_map/ppermute | solution.py:297
  233.4 8.4 %collective-permute-start.6 = (bf16[4,64,768]{2,1,0:T(8,128)(2,1)}, bf16[4,64,768]{2,1,0:T(8,128)(2,1)S(1)}, u32[]{:S(2)}, u32[]{:S(2)}) collective-permute-start(bf16[4,64,768]{2,1,0:T(8,128)(2,1)} %slice.17), channel_id=1, source_target_pairs={{0,192},{64,0},{128,64},{192,128},{1,193},{65,1},{129,65},{193,129... | collective-permute-start | bytes 1179656 | tf_op jit(solution)/shard_map/ppermute | solution.py:297
  237.6 8.4 %collective-permute-start.5 = (bf16[4,64,768]{2,1,0:T(8,128)(2,1)}, bf16[4,64,768]{2,1,0:T(8,128)(2,1)S(1)}, u32[]{:S(2)}, u32[]{:S(2)}) collective-permute-start(bf16[4,64,768]{2,1,0:T(8,128)(2,1)} %slice.16), channel_id=1, source_target_pairs={{0,64},{64,128},{128,192},{192,0},{1,65},{65,129},{129,193},{193,1... | collective-permute-start | bytes 1179656 | tf_op jit(solution)/shard_map/ppermute | solution.py:297
  264.6 1.9 copy-start
Sparse Core Ops, SparseCore 0:
  9.9 75.5 all-gather.6
  98.0 60.4 reduce-scatter.1
  177.7 36.3 all-gather.8
  217.2 47.3 all-gather.10

commit v4 on v3

--- a/solution.py
+++ b/solution.py
@@ -16,8 +16,9 @@
 ROWS = 128
 PACKED = 1280
 BLOCK = 256
-COLS_A = 480
-COLS_B = COLS - COLS_A
+PART_A = 80
+PART_B = ROWS - PART_A
+TILE = 4
 ROWS_A = 64
 ROWS_B = ROWS - ROWS_A
 
@@ -63,6 +64,33 @@
         cost_estimate=pl.CostEstimate(flops=0, bytes_accessed=5 << 20, transcendentals=0),
         name="pack",
     )(q, k, v, g)
+
+
+def turn_kernel(x_ref, a_ref, b_ref):
+    for i in range(x_ref.shape[1] // ROWS):
+        tile = x_ref[:, i * ROWS : (i + 1) * ROWS].T
+        a_ref[i] = tile[:PART_A]
+        b_ref[i] = tile[PART_A:]
+
+
+def turn(x):
+    tokens = x.shape[0]
+    each = 16
+    return pl.pallas_call(
+        turn_kernel,
+        grid=(NX * NZ // each,),
+        in_specs=[pl.BlockSpec((tokens, ROWS * each), lambda i: (0, i))],
+        out_specs=[
+            pl.BlockSpec((each, PART_A, tokens), lambda i: (i, 0, 0)),
+            pl.BlockSpec((each, PART_B, tokens), lambda i: (i, 0, 0)),
+        ],
+        out_shape=[
+            jax.ShapeDtypeStruct((NX * NZ, PART_A, tokens), bf16),
+            jax.ShapeDtypeStruct((NX * NZ, PART_B, tokens), bf16),
+        ],
+        cost_estimate=pl.CostEstimate(flops=0, bytes_accessed=2 << 20, transcendentals=0),
+        name="turn",
+    )(x)
 
 
 def attention_kernel(q_ref, k_ref, v_ref, g_ref, out_ref, kt_ref, dk_acc, dv_acc):
@@ -92,14 +120,14 @@
         row_delta = jnp.sum(probs_b.astype(f32) * prob_grad, axis=0, keepdims=True)
         dscore = (probs * (prob_grad - row_delta)).astype(bf16)
         dq_t = dot(kt_ref[:, :hi], dscore, 1, 0) * score_scale
-        out_ref[pl.ds(pl.multiple_of(head * 128, 128), 128), lo:hi] = dq_t.astype(bf16)
+        out_ref[lo:hi, pl.ds(pl.multiple_of(head * 128, 128), 128)] = dq_t.astype(bf16).T
         dk_acc[:hi, :] += dot(dscore, q, 1, 0)
         dv_acc[:hi, :] += dot(probs_b, g, 1, 0)
 
     @pl.when(head == GROUP - 1)
     def _():
-        out_ref[512:640, :] = (dk_acc[...] * score_scale).astype(bf16).T
-        out_ref[640:768, :] = dv_acc[...].astype(bf16).T
+        out_ref[:, 512:640] = (dk_acc[...] * score_scale).astype(bf16)
+        out_ref[:, 640:768] = dv_acc[...].astype(bf16)
 
 
 def attention(packed):
@@ -112,8 +140,8 @@
             pl.BlockSpec((LENGTH, 128), lambda h: (0, 5)),
             pl.BlockSpec((LENGTH, 128), lambda h: (0, 6 + h)),
         ],
-        out_specs=pl.BlockSpec((COLS, LENGTH), lambda h: (0, 0)),
-        out_shape=jax.ShapeDtypeStruct((COLS, LENGTH), bf16),
+        out_specs=pl.BlockSpec((LENGTH, COLS), lambda h: (0, 0)),
+        out_shape=jax.ShapeDtypeStruct((LENGTH, COLS), bf16),
         scratch_shapes=[
             pltpu.VMEM((128, LENGTH), bf16),
             pltpu.VMEM((LENGTH, 128), f32),
@@ -127,40 +155,103 @@
     )(packed, packed, packed, packed)
 
 
-def project_kernel(grouped_ref, x_ref, a_ref, b_ref):
-    res = dot(grouped_ref[...], x_ref[...], 1, 0).astype(bf16)
-    for i in range(a_ref.shape[0]):
-        a_ref[i, 0] = res[:COLS_A, i * ROWS : (i + 1) * ROWS]
-        b_ref[0, i] = res[COLS_A:, i * ROWS : (i + 1) * ROWS]
-
-
-def project(grouped, x):
-    tile = 4
-    return pl.pallas_call(
-        project_kernel,
-        grid=(NX, NZ // tile),
-        in_specs=[
-            pl.BlockSpec((COLS, LENGTH), lambda x, z: (0, 0)),
-            pl.BlockSpec((LENGTH, ROWS * tile), lambda x, z: (0, x * (NZ // tile) + z)),
-        ],
-        out_specs=[
-            pl.BlockSpec((tile, 1, COLS_A, ROWS), lambda x, z: (z, x, 0, 0)),
-            pl.BlockSpec((1, tile, COLS_B, ROWS), lambda x, z: (x, z, 0, 0)),
-        ],
-        out_shape=[
-            jax.ShapeDtypeStruct((NZ, NX, COLS_A, ROWS), bf16),
-            jax.ShapeDtypeStruct((NX, NZ, COLS_B, ROWS), bf16),
-        ],
+def project_a_kernel(at_x, grouped_ref, x_ref, out_ref):
+    rows = jnp.concatenate(
+        [x_ref[t].reshape(TILE * PART_A, ROWS) for t in range(x_ref.shape[0])], axis=1
+    )
+    res = dot(rows, grouped_ref[...], 1, 0).astype(bf16)
+    out_ref[...] = res.reshape(out_ref.shape)
+
+
+def project_a(at_x, grouped, x):
+    per = NZ // TILE
+    return pl.pallas_call(
+        project_a_kernel,
+        grid_spec=pltpu.PrefetchScalarGridSpec(
+            num_scalar_prefetch=1,
+            grid=(NX, per),
+            in_specs=[
+                pl.BlockSpec((LENGTH, COLS), lambda x, z, at_x: (0, 0)),
+                pl.BlockSpec((8, TILE, PART_A, ROWS), lambda x, z, at_x: (0, x * per + z, 0, 0)),
+            ],
+            out_specs=pl.BlockSpec(
+                (TILE, 1, PART_A, COLS),
+                lambda x, z, at_x: (z, lax.rem(x - at_x[0] + NX, NX), 0, 0),
+            ),
+        ),
+        out_shape=jax.ShapeDtypeStruct((NZ, NX, PART_A, COLS), bf16),
         compiler_params=pltpu.CompilerParams(vmem_limit_bytes=60 << 20),
-        cost_estimate=pl.CostEstimate(flops=6 << 30, bytes_accessed=16 << 20, transcendentals=0),
-        name="project",
-    )(grouped, x)
-
-
-def optimizer_kernel(ga_ref, gb_ref, w_ref, m_ref, v_ref, m_out, v_out, dir_out, a_out, b_out, sums_out):
-    grad_a = jnp.sum(ga_ref[...].astype(f32), axis=0)
+        cost_estimate=pl.CostEstimate(
+            flops=2 * LENGTH * COLS * WIDTH * PART_A // ROWS,
+            bytes_accessed=10 << 20,
+            transcendentals=0,
+        ),
+        name="project_a",
+    )(at_x, grouped, x)
+
+
+def project_b_kernel(offsets, grouped_ref, *refs):
+    *pieces, out_ref, ordered_ref = refs
+    step = pl.program_id(0) * (NZ // TILE) + pl.program_id(1)
+
+    @pl.when(step == 0)
+    def _():
+        for k in range(8):
+            start = pl.multiple_of(offsets[k], ROWS)
+            ordered_ref[k * ROWS : (k + 1) * ROWS, :] = grouped_ref[pl.ds(start, ROWS), :]
+
+    flat = [ref[...].reshape(TILE * PART_B, ROWS) for ref in pieces]
+    early = step < NX * NZ // TILE // 2
+    far = [jnp.where(early, flat[6], flat[8]), jnp.where(early, flat[7], flat[9])]
+    rows = jnp.concatenate(flat[:6] + far, axis=1)
+    res = dot(rows, ordered_ref[...], 1, 0).astype(bf16)
+    out_ref[...] = res.reshape(out_ref.shape)
+
+
+def project_b(offsets, grouped, pieces):
+    per = NZ // TILE
+    half = NX * NZ // TILE // 2
+    block = (TILE, PART_B, ROWS)
+    return pl.pallas_call(
+        project_b_kernel,
+        grid_spec=pltpu.PrefetchScalarGridSpec(
+            num_scalar_prefetch=1,
+            grid=(NX, per),
+            in_specs=[
+                pl.BlockSpec((LENGTH, COLS), lambda x, z, offsets: (0, 0)),
+                *[pl.BlockSpec(block, lambda x, z, offsets: (x * per + z, 0, 0))] * 6,
+                *[
+                    pl.BlockSpec(
+                        block, lambda x, z, offsets: (jnp.minimum(x * per + z, half - 1), 0, 0)
+                    )
+                ]
+                * 2,
+                *[
+                    pl.BlockSpec(
+                        block, lambda x, z, offsets: (jnp.maximum(x * per + z - half, 0), 0, 0)
+                    )
+                ]
+                * 2,
+            ],
+            out_specs=pl.BlockSpec((1, TILE, PART_B, COLS), lambda x, z, offsets: (x, z, 0, 0)),
+            scratch_shapes=[pltpu.VMEM((LENGTH, COLS), bf16)],
+        ),
+        out_shape=jax.ShapeDtypeStruct((NX, NZ, PART_B, COLS), bf16),
+        compiler_params=pltpu.CompilerParams(vmem_limit_bytes=60 << 20),
+        cost_estimate=pl.CostEstimate(
+            flops=2 * LENGTH * COLS * WIDTH * PART_B // ROWS,
+            bytes_accessed=8 << 20,
+            transcendentals=0,
+        ),
+        name="project_b",
+    )(offsets, grouped, *pieces)
+
+
+def optimizer_kernel(ga0, ga1, ga2, ga3, gb_ref, w_ref, m_ref, v_ref, m_out, v_out, dir_out, a_out, b_out, sums_out):
+    grad_a = ga0[...].astype(f32) + ga1[...].astype(f32)
+    grad_a = grad_a + ga2[...].astype(f32) + ga3[...].astype(f32)
     grad_b = jnp.sum(gb_ref[...].astype(f32), axis=0)
-    gradient = jnp.concatenate([grad_a, grad_b], axis=0).T
+    gradient = jnp.concatenate([grad_a, grad_b], axis=0)
     weight = w_ref[...]
     first_new = beta_first * m_ref[...] + (1.0 - beta_first) * gradient
     second_new = beta_second * v_ref[...] + (1.0 - beta_second) * gradient * gradient
@@ -197,7 +288,7 @@
         ],
         compiler_params=pltpu.CompilerParams(vmem_limit_bytes=32 << 20),
         name="optimizer",
-    )(ga, gb, w, m, v)
+    )(*ga, gb, w, m, v)
 
 
 def apply_kernel(place_ref, sums_ref, a0, a1, a2, a3, b_ref, a_out, b_out):
@@ -287,7 +378,7 @@
         out_specs=pl.BlockSpec((1, NZ, ROWS_A, COLS), lambda x: (x, 0, 0, 0)),
         out_shape=jax.ShapeDtypeStruct(FULL, bf16),
         input_output_aliases={0: 0},
-        compiler_params=pltpu.CompilerParams(vmem_limit_bytes=48 << 20),
+        compiler_params=pltpu.CompilerParams(vmem_limit_bytes=60 << 20),
         cost_estimate=pl.CostEstimate(flops=0, bytes_accessed=4 << 20, transcendentals=0),
         name="join_sc",
     )(base, full)
@@ -303,20 +394,36 @@
 
 
 def body(x, q, k, v, g, w, m, s):
+    x_a, x_b = turn(x[0])
     packed = pack(q[0], k[0], v[0], g[0])
     heads = lax.all_to_all(packed, ("y", "core"), 0, 0, tiled=True).reshape(LENGTH, PACKED)
-    x_full = lax.all_gather(x[0], ("y", "core"), axis=0, tiled=True)
+    x_a = lax.all_gather(x_a, ("y", "core"), axis=0, tiled=False)
+    half = NX * NZ // 2
+    x_before, x_after = shift(x_b, "y", NY, 1), shift(x_b, "y", NY, -1)
+    far_lo = shift(x_before[:half], "y", NY, 1)
+    far_hi = shift(x_after[half:], "y", NY, -1)
+    pieces = []
+    for piece in (x_b, x_before, x_after, far_lo, far_hi):
+        pieces += [piece, shift(piece, "core", NCORE, 1)]
+    heads, pieces = lax.optimization_barrier((heads, pieces))
     grouped = attention(heads)
 
-    part_a, part_b = project(grouped, x_full)
+    at_x = lax.axis_index("x")
+    at_y, at_core = lax.axis_index("y"), lax.axis_index("core")
+    blocks = []
+    for by in (0, NY - 1, 1, 2):
+        for other in (at_core, 1 - at_core):
+            blocks.append(((at_y + by) % NY) * NCORE + other)
+    offsets = (jnp.stack(blocks) * ROWS).astype(jnp.int32)
+    part_a = project_a(at_x.reshape(1).astype(jnp.int32), grouped, x_a)
+    part_b = project_b(offsets, grouped, pieces)
     part_a = lax.psum_scatter(part_a, "z", scatter_dimension=0, tiled=True)[0]
     part_b = lax.all_to_all(part_b, "x", 0, 0, tiled=True)
     part_b = jnp.sum(part_b.astype(f32), axis=0).astype(bf16)
     part_b = lax.all_to_all(part_b, "z", 0, 0, tiled=True)
-    part_a = lax.all_to_all(part_a, "x", 0, 0, tiled=True)
+    part_a = [part_a[0]] + [shift(part_a[by], "x", NX, by) for by in range(1, NX)]
 
     first_new, second_new, direction, mine_a, mine_b, sums = optimizer(part_a, part_b, w, m, s)
-    at_x = lax.axis_index("x")
     place = jnp.stack([at_x, (at_x + 3) % NX, (at_x + 1) % NX, (at_x + 2) % NX]).astype(jnp.int32)
     pieces = (
         mine_a,

time: 276 us -> 284 us (1.029)
  blocking collectives: 142 us -> 42.2 us
  waiting for transfers between devices: 50.9 us -> 124 us
  starting transfers between devices: 15.3 us -> 39.6 us
  Pallas kernels: 38 us -> 48.9 us
    all_to_all x3 -> x0, blocking collectives: 99.1 us -> none  [the longest x1 57.6 us: body(): lax.all_to_all(packed, ('y', 'core'), 0, 0, tiled=True)]
    ppermute x7 -> x19, waiting for transfers between devices: 26.7 us -> 89.4 us  [shift(): lax.ppermute(value, axis, [(i, (i + by) % size) for i in range(size)])]
    all_to_all x0 -> x2, starting transfers between devices: none -> 14.1 us  [the longest x1 7.37 us: body(): part_b = lax.all_to_all(part_b, 'z', 0, 0, tiled=True)]
    all_to_all x0 -> x2, waiting for transfers between devices: none -> 14.1 us  [the longest x1 14.1 us: body(): part_b = lax.all_to_all(part_b, 'z', 0, 0, tiled=True)]
    ppermute x7 -> x19, starting transfers between devices: 10.2 us -> 21.3 us  [shift(): lax.ppermute(value, axis, [(i, (i + by) % size) for i in range(size)])]
    pallas_call x1 -> x3, Pallas kernels: 12.4 us -> 21.2 us  [the longest x1 9.85 us: project_a(): pl.pallas_call(project_a_kernel, grid_spec=pltpu.PrefetchScalarGridSpec(n...]
    unnamed x16, local copies, waits for them, and re-layouts: 6.79 us -> 3.34 us
  transfers between devices with their start and end apart: 12 -> 26, of which waited for: 9 -> 13; matrix products, arithmetic and copies ran while one was open for 2% -> 3% of each run, Pallas kernels for 7% -> 10%
where the time goes in v4:
time: 284 us; the launch traced here: 283 us
  waiting for transfers between devices  124 us (44%)
  Pallas kernels  48.9 us (17%)
  blocking collectives  42.2 us (15%)
  starting transfers between devices  39.6 us (14%)
  between operations  15.3 us (5%)
  local copies, waits for them, and re-layouts  7.39 us (3%)
  other arithmetic  5.52 us (2%)
    ppermute x19, waiting for transfers between devices, shift(): lax.ppermute(value, axis, [(i, (i + by) % size) for i in range(size)])  89.4 us
    all_to_all x1, blocking collectives, body(): part_b = lax.all_to_all(part_b, 'x', 0, 0, tiled=True)  33.3 us
    ppermute x19, starting transfers between devices, shift(): lax.ppermute(value, axis, [(i, (i + by) % size) for i in range(size)])  21.3 us
    all_gather x1, waiting for transfers between devices, body(): full_a = lax.all_gather(new_a, 'z', axis=0, tiled=False)  15.1 us
    all_to_all x1, waiting for transfers between devices, body(): part_b = lax.all_to_all(part_b, 'z', 0, 0, tiled=True)  14.1 us
    pallas_call x1, Pallas kernels, attention(): pl.pallas_call(attention_kernel, grid=(GROUP,), in_specs=[pl.BlockSpec((L...  13.5 us
    pallas_call x1, Pallas kernels, project_a(): pl.pallas_call(project_a_kernel, grid_spec=pltpu.PrefetchScalarGridSpec(n...  9.85 us
    pallas_call x1, Pallas kernels, project_b(): pl.pallas_call(project_b_kernel, grid_spec=pltpu.PrefetchScalarGridSpec(n...  9.12 us
  transfers between devices with their start and end apart: 26, of which 13 were waited for; matrix products, arithmetic and copies ran while one was open for 3% of the time, Pallas kernels for 10%

profile of v4, /device:TPU:1, one launch (start us, length us, event | category | flops | bytes accessed | tf_op | source)
XLA Modules:
  0.0 282.6 jit_solution(15139162359625400002)
XLA Ops:
  7.2 2.2 turn.1
  9.5 2.9 %pack.1 = bf16[8,128,1280]{2,1,0:T(8,128)(2,1)} custom-call(bf16[128,4096]{1,0:T(8,128)(2,1)} %bitcast.38, bf16[128,1024]{1,0:T(8,128)(2,1)} %bitcast.41, bf16[128,1024]{1,0:T(8,128)(2,1)} %bitcast.42, bf16[128,4096]{1,0:T(8,128)(2,1)} %bitcast.39), custom_call_target="tpu_custom_call" | custom-call | bytes 5242880 | tf_op jit(solution)/shard_map/pack/pallas_call | solution.py:53
  12.4 6.8 %all-to-all-start = ((bf16[8,128,1280]{2,1,0:T(8,128)(2,1)}), bf16[8,128,1280]{2,1,0:T(8,128)(2,1)S(1)}, u32[]{:S(2)}, u32[]{:S(2)}) async-start(bf16[8,128,1280]{2,1,0:T(8,128)(2,1)} %pack.1), calls=%async_computation | async-start | bytes 5242880 | tf_op jit(solution)/shard_map/all_to_all | solution.py:399
  19.2 2.6 collective-permute-start.3
  22.4 56.8 %collective-permute-done.3.refs_4_ = bf16[32,48,128]{2,1,0:T(8,128)(2,1)S(1)} collective-permute-done((bf16[32,48,128]{2,1,0:T(8,128)(2,1)}, bf16[32,48,128]{2,1,0:T(8,128)(2,1)S(1)}, u32[]{:S(2)}, u32[]{:S(2)}) %collective-permute-start.3) | collective-permute-done | bytes 393248 | tf_op jit(solution)/shard_map/ppermute | solution.py:388
  82.2 2.9 %collective-permute-done.7.refs_8_ = bf16[16,48,128]{2,1,0:T(8,128)(2,1)} collective-permute-done((bf16[16,48,128]{2,1,0:T(8,128)(2,1)S(1)}, bf16[16,48,128]{2,1,0:T(8,128)(2,1)}, u32[]{:S(2)}, u32[]{:S(2)}) %collective-permute-start.7) | collective-permute-done | bytes 196640 | tf_op jit(solution)/shard_map/ppermute | solution.py:388
  85.1 1.7 collective-permute-start.8
  86.7 2.2 collective-permute-done.5.refs_6_
  91.1 13.5 %attention_backward.1.grouped_ref = bf16[1024,768]{1,0:T(8,128)(2,1)S(1)} custom-call(bf16[1024,1280]{1,0:T(8,128)(2,1)S(1)} %bitcast.31, bf16[1024,1280]{1,0:T(8,128)(2,1)S(1)} %bitcast.32, bf16[1024,1280]{1,0:T(8,128)(2,1)S(1)} %bitcast.33, bf16[1024,1280]{1,0:T(8,128)(2,1)S(1)} %bitcast.34), custom_call_target="tpu_custom_call" | custom-call | flops 4294967296 | bytes 5242880 | tf_op jit(solution)/shard_map/attention_backward/pallas_call | solution.py:134
  105.8 9.9 %project_a.1 = bf16[8,4,80,768]{3,2,1,0:T(8,128)(2,1)} custom-call(s32[1]{0:T(128)} %bitcast.at_x, bf16[1024,768]{1,0:T(8,128)(2,1)} %copy-done.5, bf16[8,32,80,128]{3,2,1,0:T(8,128)(2,1)} %bitcast.43), custom_call_target="tpu_custom_call" | custom-call | flops 4026531840 | bytes 10485760 | tf_op jit(solution)/shard_map/project_a/pallas_call | solution.py:168
  116.4 9.1 %project_b.1 = bf16[4,8,48,768]{3,2,1,0:T(8,128)(2,1)} custom-call(s32[8]{0:T(128)} %broadcast_multiply_fusion.1.offsets, bf16[1024,768]{1,0:T(8,128)(2,1)} %copy-done.5, bf16[32,48,128]{2,1,0:T(8,128)(2,1)} %get-tuple-element.28.refs_0_, bf16[32,48,128]{2,1,0:T(8,128)(2,1)} %collective-permute-done.refs_1_, bf16[32,48,128]{2,1,0:T(8,128)(2,1)} %copy-done.7, ...), custom_call_target="tpu_custom_call" | custom-call | flops 2415919104 | bytes 8388608 | tf_op jit(solution)/shard_map/project_b/pallas_call | solution.py:215
  125.5 33.3 %all_to_all.25 = bf16[4,8,48,768]{3,2,1,0:T(8,128)(2,1)} all-to-all(bf16[4,8,48,768]{3,2,1,0:T(8,128)(2,1)} %project_b.1), channel_id=1, replica_groups=mesh['x'=4,'z'=8,'y'=4,'core'=2] {'x'}, dimensions={0} | all-to-all | bytes 4718592 | tf_op jit(solution)/shard_map/all_to_all | solution.py:421
  158.8 3.1 %reduce_sum.30 = bf16[8,48,768]{2,1,0:T(8,128)(2,1)} reduce(bf16[4,8,48,768]{3,2,1,0:T(8,128)(2,1)} %all_to_all.25, bf16[]{:T(256)} %constant.66.clone.1), dimensions={0}, to_apply=%region_1.2 | reduce | flops 884736 | bytes 2949122 | tf_op jit(solution)/shard_map/reduce_sum | solution.py:422
  161.9 7.4 %all-to-all-start.2 = ((bf16[8,48,768]{2,1,0:T(8,128)(2,1)}), bf16[8,48,768]{2,1,0:T(8,128)(2,1)S(1)}, u32[]{:S(2)}, u32[]{:S(2)}) async-start(bf16[8,48,768]{2,1,0:T(8,128)(2,1)} %reduce_sum.30), calls=%async_computation.3 | async-start | bytes 1179648 | tf_op jit(solution)/shard_map/all_to_all | solution.py:423
  170.7 1.5 collective-permute-start.11
  173.3 14.1 %all-to-all-done.2.gb_ref = bf16[8,48,768]{2,1,0:T(8,128)(2,1)S(1)} async-done(((bf16[8,48,768]{2,1,0:T(8,128)(2,1)}), bf16[8,48,768]{2,1,0:T(8,128)(2,1)S(1)}, u32[]{:S(2)}, u32[]{:S(2)}) %all-to-all-start.2) | async-done | bytes 589856 | tf_op jit(solution)/shard_map/all_to_all | solution.py:423
  187.4 1.7 optimizer.1
  189.9 8.9 %all_to_all.26 = f32[8,8,128]{2,1,0:T(8,128)S(1)} all-to-all(f32[8,8,128]{2,1,0:T(8,128)S(1)} %broadcast_in_dim.4), channel_id=1, replica_groups=mesh['x'=4,'z'=8,'y'=4,'core'=2] {'y','core'}, dimensions={0} | all-to-all | bytes 65536 | tf_op jit(solution)/shard_map/all_to_all | solution.py:393
  199.4 3.8 %all-to-all-start.4 = ((f32[32,8,128]{2,1,0:T(8,128)}), f32[32,8,128]{2,1,0:T(8,128)S(1)}, u32[]{:S(2)}, u32[]{:S(2)}) async-start(f32[32,8,128]{2,1,0:T(8,128)} %broadcast_in_dim.5), calls=%async_computation.5 | async-start | bytes 262144 | tf_op jit(solution)/shard_map/all_to_all | solution.py:393
  203.3 2.8 collective-permute-start.14
  207.7 3.6 %collective-permute-done.14.a3 = bf16[2,64,768]{2,1,0:T(8,128)(2,1)S(1)} collective-permute-done((bf16[2,64,768]{2,1,0:T(8,128)(2,1)S(1)}, bf16[2,64,768]{2,1,0:T(8,128)(2,1)S(1)}, u32[]{:S(2)}, u32[]{:S(2)}) %collective-permute-start.14) | collective-permute-done | bytes 196640 | tf_op jit(solution)/shard_map/ppermute | solution.py:388
  211.3 5.0 %collective-permute-done.13.a2 = bf16[2,64,768]{2,1,0:T(8,128)(2,1)S(1)} collective-permute-done((bf16[2,64,768]{2,1,0:T(8,128)(2,1)S(1)}, bf16[2,64,768]{2,1,0:T(8,128)(2,1)S(1)}, u32[]{:S(2)}, u32[]{:S(2)}) %collective-permute-start.13) | collective-permute-done | bytes 196640 | tf_op jit(solution)/shard_map/ppermute | solution.py:388
  216.8 5.2 %all-gather.9.cloned.1.call-done = bf16[16,64,768]{2,1,0:T(8,128)(2,1)} async-done(((bf16[2,64,768]{2,1,0:T(8,128)(2,1)}), bf16[16,64,768]{2,1,0:T(8,128)(2,1)}) %all-gather.9.cloned.1.call-update) | async-done | bytes 1572880 | tf_op jit(solution)/shard_map/all_gather | solution.py:434
  223.4 1.5 apply.1
  224.9 2.3 collective-permute-start.16
  227.2 12.4 %collective-permute-done.16.b2 = bf16[8,64,768]{2,1,0:T(8,128)(2,1)S(1)} collective-permute-done((bf16[8,64,768]{2,1,0:T(8,128)(2,1)S(1)}, bf16[8,64,768]{2,1,0:T(8,128)(2,1)S(1)}, u32[]{:S(2)}, u32[]{:S(2)}) %collective-permute-start.16) | collective-permute-done | bytes 786464 | tf_op jit(solution)/shard_map/ppermute | solution.py:388
  240.4 3.4 %collective-permute-start.18 = (bf16[4,64,768]{2,1,0:T(8,128)(2,1)}, bf16[4,64,768]{2,1,0:T(8,128)(2,1)S(1)}, u32[]{:S(2)}, u32[]{:S(2)}) collective-permute-start(bf16[4,64,768]{2,1,0:T(8,128)(2,1)} %slice.51), channel_id=1, source_target_pairs={{0,192},{64,0},{128,64},{192,128},{1,193},{65,1},{129,65},{193,129... | collective-permute-start | bytes 1179656 | tf_op jit(solution)/shard_map/ppermute | solution.py:388
  246.5 1.8 broadcast_multiply_fusion
  248.9 4.1 %collective-permute-done.17.b3 = bf16[4,64,768]{2,1,0:T(8,128)(2,1)S(1)} collective-permute-done((bf16[4,64,768]{2,1,0:T(8,128)(2,1)}, bf16[4,64,768]{2,1,0:T(8,128)(2,1)S(1)}, u32[]{:S(2)}, u32[]{:S(2)}) %collective-permute-start.17) | collective-permute-done | bytes 393248 | tf_op jit(solution)/shard_map/ppermute | solution.py:388
  253.0 3.9 %join_x.1.base_ref = bf16[4,8,128,768]{3,2,1,0:T(8,128)(2,1)} custom-call(s32[4]{0:T(128)S(1)} %pad_add_fusion.place_ref, bf16[8,64,768]{2,1,0:T(8,128)(2,1)S(1)} %get-tuple-element.44.b0, bf16[8,64,768]{2,1,0:T(8,128)(2,1)S(1)} %collective-permute-done.15.b1, bf16[8,64,768]{2,1,0:T(8,128)(2,1)S(1)} %collective-permute-done.16.b2, ...), custom_call_target="tpu_custom_call" | custom-call | bytes 7340032 | tf_op jit(solution)/shard_map/join_x/pallas_call | solution.py:348
  256.8 15.1 %all-gather.11.cloned.1.call-done = bf16[32,64,768]{2,1,0:T(8,128)(2,1)} async-done(((bf16[4,64,768]{2,1,0:T(8,128)(2,1)}), bf16[32,64,768]{2,1,0:T(8,128)(2,1)}) %all-gather.11.cloned.1.call-update) | async-done | bytes 3145744 | tf_op jit(solution)/shard_map/all_gather | solution.py:437
  271.9 4.2 %join_sc.1 = bf16[4,8,128,768]{3,2,1,0:T(8,128)(2,1)} custom-call(bf16[4,8,128,768]{3,2,1,0:T(8,128)(2,1)} %join_x.1.base_ref, bf16[8,4,64,768]{3,2,1,0:T(8,128)(2,1)} %bitcast.37), custom_call_target="tpu_custom_call", output_to_operand_aliasing={{}: (0, {})} | custom-call | bytes 4194304 | tf_op jit(solution)/shard_map/join_sc/pallas_call | solution.py:371
  (66 shorter events, 18.0 us)
Async XLA Ops:
  7.2 98.7 %all-gather.7.cloned.1.call-start = ((), (), s32[]{:S(2)}) async-start(), calls=%async_computation.7 | async-start | bytes 5898240 | tf_op jit(solution)/shard_map/all_gather | solution.py:400
  12.4 78.7 %all-to-all-start = ((bf16[8,128,1280]{2,1,0:T(8,128)(2,1)}), bf16[8,128,1280]{2,1,0:T(8,128)(2,1)S(1)}, u32[]{:S(2)}, u32[]{:S(2)}) async-start(bf16[8,128,1280]{2,1,0:T(8,128)(2,1)} %pack.1), calls=%async_computation | async-start | bytes 5242880 | tf_op jit(solution)/shard_map/all_to_all | solution.py:399
  19.2 150.4 %reduce-scatter.2.cloned.1.call-start = ((), (), s32[]{:S(2)}) async-start(), calls=%async_computation.6 | async-start | bytes 4423680 | tf_op jit(solution)/shard_map/reduce_scatter | solution.py:420
  19.2 60.0 %collective-permute-start.3 = (bf16[32,48,128]{2,1,0:T(8,128)(2,1)}, bf16[32,48,128]{2,1,0:T(8,128)(2,1)S(1)}, u32[]{:S(2)}, u32[]{:S(2)}) collective-permute-start(bf16[32,48,128]{2,1,0:T(8,128)(2,1)} %get-tuple-element.28.refs_0_), channel_id=1, source_target_pairs={{0,6},{2,0},{4,2},{6,4},{1,7},{3,1},{5,3},{7,5},{8,14},{10,8},{12,... | collective-permute-start | bytes 1179656 | tf_op jit(solution)/shard_map/ppermute | solution.py:388
  21.8 59.2 %collective-permute-start.1 = (bf16[32,48,128]{2,1,0:T(8,128)(2,1)}, bf16[32,48,128]{2,1,0:T(8,128)(2,1)S(1)}, u32[]{:S(2)}, u32[]{:S(2)}) collective-permute-start(bf16[32,48,128]{2,1,0:T(8,128)(2,1)} %get-tuple-element.28.refs_0_), channel_id=1, source_target_pairs={{0,2},{2,4},{4,6},{6,0},{1,3},{3,5},{5,7},{7,1},{8,10},{10,12},{12... | collective-permute-start | bytes 1179656 | tf_op jit(solution)/shard_map/ppermute | solution.py:388
  21.8 67.9 %collective-permute-start = (bf16[32,48,128]{2,1,0:T(8,128)(2,1)}, bf16[32,48,128]{2,1,0:T(8,128)(2,1)}, u32[]{:S(2)}, u32[]{:S(2)}) collective-permute-start(bf16[32,48,128]{2,1,0:T(8,128)(2,1)} %get-tuple-element.28.refs_0_), channel_id=1, source_target_pairs={{0,1},{1,0},{2,3},{3,2},{4,5},{5,4},{6,7},{7,6},{8,9},{9,8},{10,11... | collective-permute-start | bytes 1179656 | tf_op jit(solution)/shard_map/ppermute | solution.py:388
  79.2 25.4 %copy-start.6 = (bf16[32,48,128]{2,1,0:T(8,128)(2,1)}, bf16[32,48,128]{2,1,0:T(8,128)(2,1)S(1)}, u32[]{:S(2)}) copy-start(bf16[32,48,128]{2,1,0:T(8,128)(2,1)S(1)} %collective-permute-done.3.refs_4_) | copy-start | bytes 1179652
  79.2 5.8 %collective-permute-start.7 = (bf16[16,48,128]{2,1,0:T(8,128)(2,1)S(1)}, bf16[16,48,128]{2,1,0:T(8,128)(2,1)}, u32[]{:S(2)}, u32[]{:S(2)}) collective-permute-start(bf16[16,48,128]{2,1,0:T(8,128)(2,1)S(1)} %slice.45), channel_id=1, source_target_pairs={{0,6},{2,0},{4,2},{6,4},{1,7},{3,1},{5,3},{7,5},{8,14},{10,8},{12,... | collective-permute-start | bytes 589832 | tf_op jit(solution)/shard_map/ppermute | solution.py:388
  79.8 9.9 %collective-permute-start.4 = (bf16[32,48,128]{2,1,0:T(8,128)(2,1)S(1)}, bf16[32,48,128]{2,1,0:T(8,128)(2,1)}, u32[]{:S(2)}, u32[]{:S(2)}) collective-permute-start(bf16[32,48,128]{2,1,0:T(8,128)(2,1)S(1)} %collective-permute-done.3.refs_4_), channel_id=1, source_target_pairs={{0,1},{1,0},{2,3},{3,2},{4,5},{5,4},{6,7},{7,6},{8,9},{9,8},{10,11... | collective-permute-start | bytes 1179656 | tf_op jit(solution)/shard_map/ppermute | solution.py:388
  81.0 23.7 %copy-start.7 = (bf16[32,48,128]{2,1,0:T(8,128)(2,1)}, bf16[32,48,128]{2,1,0:T(8,128)(2,1)S(1)}, u32[]{:S(2)}) copy-start(bf16[32,48,128]{2,1,0:T(8,128)(2,1)S(1)} %collective-permute-done.1.refs_2_) | copy-start | bytes 1179652
  81.0 7.9 %collective-permute-start.5 = (bf16[16,48,128]{2,1,0:T(8,128)(2,1)S(1)}, bf16[16,48,128]{2,1,0:T(8,128)(2,1)}, u32[]{:S(2)}, u32[]{:S(2)}) collective-permute-start(bf16[16,48,128]{2,1,0:T(8,128)(2,1)S(1)} %slice.44), channel_id=1, source_target_pairs={{0,2},{2,4},{4,6},{6,0},{1,3},{3,5},{5,7},{7,1},{8,10},{10,12},{12... | collective-permute-start | bytes 589832 | tf_op jit(solution)/shard_map/ppermute | solution.py:388
  81.9 9.2 %collective-permute-start.2 = (bf16[32,48,128]{2,1,0:T(8,128)(2,1)S(1)}, bf16[32,48,128]{2,1,0:T(8,128)(2,1)}, u32[]{:S(2)}, u32[]{:S(2)}) collective-permute-start(bf16[32,48,128]{2,1,0:T(8,128)(2,1)S(1)} %collective-permute-done.1.refs_2_), channel_id=1, source_target_pairs={{0,1},{1,0},{2,3},{3,2},{4,5},{5,4},{6,7},{7,6},{8,9},{9,8},{10,11... | collective-permute-start | bytes 1179656 | tf_op jit(solution)/shard_map/ppermute | solution.py:388
  85.1 4.6 %collective-permute-start.8 = (bf16[16,48,128]{2,1,0:T(8,128)(2,1)}, bf16[16,48,128]{2,1,0:T(8,128)(2,1)}, u32[]{:S(2)}, u32[]{:S(2)}) collective-permute-start(bf16[16,48,128]{2,1,0:T(8,128)(2,1)} %collective-permute-done.7.refs_8_), channel_id=1, source_target_pairs={{0,1},{1,0},{2,3},{3,2},{4,5},{5,4},{6,7},{7,6},{8,9},{9,8},{10,11... | collective-permute-start | bytes 589832 | tf_op jit(solution)/shard_map/ppermute | solution.py:388
  88.9 2.2 collective-permute-start.6
  158.8 28.6 %copy-start.2 = (f32[128,768]{1,0:T(8,128)S(1)}, f32[128,768]{1,0:T(8,128)}, u32[]{:S(2)}) copy-start(f32[128,768]{1,0:T(8,128)} %w_ref.1) | copy-start | bytes 1179652
  158.8 28.6 %copy-start.3 = (f32[128,768]{1,0:T(8,128)S(1)}, f32[128,768]{1,0:T(8,128)}, u32[]{:S(2)}) copy-start(f32[128,768]{1,0:T(8,128)} %m_ref.1) | copy-start | bytes 1179652
  158.8 28.6 %copy-start.4 = (f32[128,768]{1,0:T(8,128)S(1)}, f32[128,768]{1,0:T(8,128)}, u32[]{:S(2)}) copy-start(f32[128,768]{1,0:T(8,128)} %v_ref.1) | copy-start | bytes 1179652
  161.9 25.5 %all-to-all-start.2 = ((bf16[8,48,768]{2,1,0:T(8,128)(2,1)}), bf16[8,48,768]{2,1,0:T(8,128)(2,1)S(1)}, u32[]{:S(2)}, u32[]{:S(2)}) async-start(bf16[8,48,768]{2,1,0:T(8,128)(2,1)} %reduce_sum.30), calls=%async_computation.3 | async-start | bytes 1179648 | tf_op jit(solution)/shard_map/all_to_all | solution.py:423
  169.3 52.7 %all-gather.9.cloned.1.call-start = ((), (), s32[]{:S(2)}) async-start(), calls=%async_computation.8 | async-start | bytes 1769472 | tf_op jit(solution)/shard_map/all_gather | solution.py:434
  170.7 16.7 %collective-permute-start.11 = (bf16[80,768]{1,0:T(8,128)(2,1)S(1)}, bf16[80,768]{1,0:T(8,128)(2,1)S(1)}, u32[]{:S(2)}, u32[]{:S(2)}) collective-permute-start(bf16[80,768]{1,0:T(8,128)(2,1)S(1)} %get-tuple-element.46), channel_id=1, source_target_pairs={{0,192},{64,0},{128,64},{192,128},{1,193},{65,1},{129,65},{193,129... | collective-permute-start | bytes 368648 | tf_op jit(solution)/shard_map/ppermute | solution.py:388
  172.1 15.2 %collective-permute-start.10 = (bf16[80,768]{1,0:T(8,128)(2,1)S(1)}, bf16[80,768]{1,0:T(8,128)(2,1)S(1)}, u32[]{:S(2)}, u32[]{:S(2)}) collective-permute-start(bf16[80,768]{1,0:T(8,128)(2,1)S(1)} %get-tuple-element.47), channel_id=1, source_target_pairs={{0,128},{64,192},{128,0},{192,64},{1,129},{65,193},{129,1},{193,65... | collective-permute-start | bytes 368648 | tf_op jit(solution)/shard_map/ppermute | solution.py:388
  172.8 14.5 %collective-permute-start.9 = (bf16[80,768]{1,0:T(8,128)(2,1)S(1)}, bf16[80,768]{1,0:T(8,128)(2,1)S(1)}, u32[]{:S(2)}, u32[]{:S(2)}) collective-permute-start(bf16[80,768]{1,0:T(8,128)(2,1)S(1)} %get-tuple-element.48), channel_id=1, source_target_pairs={{0,64},{64,128},{128,192},{192,0},{1,65},{65,129},{129,193},{193,1... | collective-permute-start | bytes 368648 | tf_op jit(solution)/shard_map/ppermute | solution.py:388
  199.4 17.4 %all-to-all-start.4 = ((f32[32,8,128]{2,1,0:T(8,128)}), f32[32,8,128]{2,1,0:T(8,128)S(1)}, u32[]{:S(2)}, u32[]{:S(2)}) async-start(f32[32,8,128]{2,1,0:T(8,128)} %broadcast_in_dim.5), calls=%async_computation.5 | async-start | bytes 262144 | tf_op jit(solution)/shard_map/all_to_all | solution.py:393
  203.3 68.6 %all-gather.11.cloned.1.call-start = ((), (), s32[]{:S(2)}) async-start(), calls=%async_computation.9 | async-start | bytes 3538944 | tf_op jit(solution)/shard_map/all_gather | solution.py:437
  203.3 7.9 %collective-permute-start.14 = (bf16[2,64,768]{2,1,0:T(8,128)(2,1)S(1)}, bf16[2,64,768]{2,1,0:T(8,128)(2,1)S(1)}, u32[]{:S(2)}, u32[]{:S(2)}) collective-permute-start(bf16[2,64,768]{2,1,0:T(8,128)(2,1)S(1)} %get-tuple-element.42.a0), channel_id=1, source_target_pairs={{0,128},{64,192},{128,0},{192,64},{1,129},{65,193},{129,1},{193,65... | collective-permute-start | bytes 589832 | tf_op jit(solution)/shard_map/ppermute | solution.py:388
  206.1 10.2 %collective-permute-start.13 = (bf16[2,64,768]{2,1,0:T(8,128)(2,1)S(1)}, bf16[2,64,768]{2,1,0:T(8,128)(2,1)S(1)}, u32[]{:S(2)}, u32[]{:S(2)}) collective-permute-start(bf16[2,64,768]{2,1,0:T(8,128)(2,1)S(1)} %get-tuple-element.42.a0), channel_id=1, source_target_pairs={{0,192},{64,0},{128,64},{192,128},{1,193},{65,1},{129,65},{193,129... | collective-permute-start | bytes 589832 | tf_op jit(solution)/shard_map/ppermute | solution.py:388
  207.0 9.8 %collective-permute-start.12 = (bf16[2,64,768]{2,1,0:T(8,128)(2,1)S(1)}, bf16[2,64,768]{2,1,0:T(8,128)(2,1)S(1)}, u32[]{:S(2)}, u32[]{:S(2)}) collective-permute-start(bf16[2,64,768]{2,1,0:T(8,128)(2,1)S(1)} %get-tuple-element.42.a0), channel_id=1, source_target_pairs={{0,64},{64,128},{128,192},{192,0},{1,65},{65,129},{129,193},{193,1... | collective-permute-start | bytes 589832 | tf_op jit(solution)/shard_map/ppermute | solution.py:388
  221.9 1.4 copy-start
  224.9 14.7 %collective-permute-start.16 = (bf16[8,64,768]{2,1,0:T(8,128)(2,1)S(1)}, bf16[8,64,768]{2,1,0:T(8,128)(2,1)S(1)}, u32[]{:S(2)}, u32[]{:S(2)}) collective-permute-start(bf16[8,64,768]{2,1,0:T(8,128)(2,1)S(1)} %get-tuple-element.44.b0), channel_id=1, source_target_pairs={{0,192},{64,0},{128,64},{192,128},{1,193},{65,1},{129,65},{193,129... | collective-permute-start | bytes 2359304 | tf_op jit(solution)/shard_map/ppermute | solution.py:388
  227.2 16.5 %collective-permute-start.15 = (bf16[8,64,768]{2,1,0:T(8,128)(2,1)S(1)}, bf16[8,64,768]{2,1,0:T(8,128)(2,1)S(1)}, u32[]{:S(2)}, u32[]{:S(2)}) collective-permute-start(bf16[8,64,768]{2,1,0:T(8,128)(2,1)S(1)} %get-tuple-element.44.b0), channel_id=1, source_target_pairs={{0,64},{64,128},{128,192},{192,0},{1,65},{65,129},{129,193},{193,1... | collective-permute-start | bytes 2359304 | tf_op jit(solution)/shard_map/ppermute | solution.py:388
  240.4 8.5 %collective-permute-start.18 = (bf16[4,64,768]{2,1,0:T(8,128)(2,1)}, bf16[4,64,768]{2,1,0:T(8,128)(2,1)S(1)}, u32[]{:S(2)}, u32[]{:S(2)}) collective-permute-start(bf16[4,64,768]{2,1,0:T(8,128)(2,1)} %slice.51), channel_id=1, source_target_pairs={{0,192},{64,0},{128,64},{192,128},{1,193},{65,1},{129,65},{193,129... | collective-permute-start | bytes 1179656 | tf_op jit(solution)/shard_map/ppermute | solution.py:388
  244.5 8.4 %collective-permute-start.17 = (bf16[4,64,768]{2,1,0:T(8,128)(2,1)}, bf16[4,64,768]{2,1,0:T(8,128)(2,1)S(1)}, u32[]{:S(2)}, u32[]{:S(2)}) collective-permute-start(bf16[4,64,768]{2,1,0:T(8,128)(2,1)} %slice.50), channel_id=1, source_target_pairs={{0,64},{64,128},{128,192},{192,0},{1,65},{65,129},{129,193},{193,1... | collective-permute-start | bytes 1179656 | tf_op jit(solution)/shard_map/ppermute | solution.py:388
  (2 other events, 1.9 us)
Sparse Core Ops, SparseCore 0:
  9.8 72.9 all-gather.6
  115.8 52.6 reduce-scatter.1
  190.0 31.8 all-gather.8
  225.0 46.8 all-gather.10

commit v5 on v3

--- a/solution.py
+++ b/solution.py
@@ -16,8 +16,8 @@
 ROWS = 128
 PACKED = 1280
 BLOCK = 256
-COLS_A = 480
-COLS_B = COLS - COLS_A
+PART_A = 80
+PART_B = ROWS - PART_A
 ROWS_A = 64
 ROWS_B = ROWS - ROWS_A
 
@@ -63,6 +63,25 @@
         cost_estimate=pl.CostEstimate(flops=0, bytes_accessed=5 << 20, transcendentals=0),
         name="pack",
     )(q, k, v, g)
+
+
+def turn_kernel(x_ref, out_ref):
+    for i in range(out_ref.shape[0]):
+        out_ref[i] = x_ref[:, i * ROWS : (i + 1) * ROWS].T
+
+
+def turn(x):
+    tokens = x.shape[0]
+    each = 16
+    return pl.pallas_call(
+        turn_kernel,
+        grid=(NX * NZ // each,),
+        in_specs=[pl.BlockSpec((tokens, ROWS * each), lambda i: (0, i))],
+        out_specs=pl.BlockSpec((each, ROWS, tokens), lambda i: (i, 0, 0)),
+        out_shape=jax.ShapeDtypeStruct((NX * NZ, ROWS, tokens), bf16),
+        cost_estimate=pl.CostEstimate(flops=0, bytes_accessed=2 << 20, transcendentals=0),
+        name="turn",
+    )(x)
 
 
 def attention_kernel(q_ref, k_ref, v_ref, g_ref, out_ref, kt_ref, dk_acc, dv_acc):
@@ -92,14 +111,14 @@
         row_delta = jnp.sum(probs_b.astype(f32) * prob_grad, axis=0, keepdims=True)
         dscore = (probs * (prob_grad - row_delta)).astype(bf16)
         dq_t = dot(kt_ref[:, :hi], dscore, 1, 0) * score_scale
-        out_ref[pl.ds(pl.multiple_of(head * 128, 128), 128), lo:hi] = dq_t.astype(bf16)
+        out_ref[lo:hi, pl.ds(pl.multiple_of(head * 128, 128), 128)] = dq_t.astype(bf16).T
         dk_acc[:hi, :] += dot(dscore, q, 1, 0)
         dv_acc[:hi, :] += dot(probs_b, g, 1, 0)
 
     @pl.when(head == GROUP - 1)
     def _():
-        out_ref[512:640, :] = (dk_acc[...] * score_scale).astype(bf16).T
-        out_ref[640:768, :] = dv_acc[...].astype(bf16).T
+        out_ref[:, 512:640] = (dk_acc[...] * score_scale).astype(bf16)
+        out_ref[:, 640:768] = dv_acc[...].astype(bf16)
 
 
 def attention(packed):
@@ -112,8 +131,8 @@
             pl.BlockSpec((LENGTH, 128), lambda h: (0, 5)),
             pl.BlockSpec((LENGTH, 128), lambda h: (0, 6 + h)),
         ],
-        out_specs=pl.BlockSpec((COLS, LENGTH), lambda h: (0, 0)),
-        out_shape=jax.ShapeDtypeStruct((COLS, LENGTH), bf16),
+        out_specs=pl.BlockSpec((LENGTH, COLS), lambda h: (0, 0)),
+        out_shape=jax.ShapeDtypeStruct((LENGTH, COLS), bf16),
         scratch_shapes=[
             pltpu.VMEM((128, LENGTH), bf16),
             pltpu.VMEM((LENGTH, 128), f32),
@@ -127,40 +146,50 @@
     )(packed, packed, packed, packed)
 
 
-def project_kernel(grouped_ref, x_ref, a_ref, b_ref):
-    res = dot(grouped_ref[...], x_ref[...], 1, 0).astype(bf16)
-    for i in range(a_ref.shape[0]):
-        a_ref[i, 0] = res[:COLS_A, i * ROWS : (i + 1) * ROWS]
-        b_ref[0, i] = res[COLS_A:, i * ROWS : (i + 1) * ROWS]
-
-
-def project(grouped, x):
-    tile = 4
-    return pl.pallas_call(
-        project_kernel,
-        grid=(NX, NZ // tile),
-        in_specs=[
-            pl.BlockSpec((COLS, LENGTH), lambda x, z: (0, 0)),
-            pl.BlockSpec((LENGTH, ROWS * tile), lambda x, z: (0, x * (NZ // tile) + z)),
-        ],
-        out_specs=[
-            pl.BlockSpec((tile, 1, COLS_A, ROWS), lambda x, z: (z, x, 0, 0)),
-            pl.BlockSpec((1, tile, COLS_B, ROWS), lambda x, z: (x, z, 0, 0)),
-        ],
-        out_shape=[
-            jax.ShapeDtypeStruct((NZ, NX, COLS_A, ROWS), bf16),
-            jax.ShapeDtypeStruct((NX, NZ, COLS_B, ROWS), bf16),
-        ],
+def project(grouped, x, lo, hi, at_x, name):
+    part = hi - lo
+
+    def kernel(place, grouped_ref, x_ref, out_ref):
+        rows = jnp.concatenate(
+            [x_ref[t, :, lo:hi, :].reshape(NZ * part, ROWS) for t in range(8)], axis=1
+        )
+        res = dot(rows, grouped_ref[...], 1, 0).astype(bf16)
+        out_ref[...] = res.reshape(out_ref.shape)
+
+    if at_x is None:
+        shape, block = (NX, NZ, part, COLS), (1, NZ, part, COLS)
+        out_map = lambda x, place: (x, 0, 0, 0)
+        at_x = jnp.zeros((1,), jnp.int32)
+    else:
+        shape, block = (NZ, NX, part, COLS), (NZ, 1, part, COLS)
+        out_map = lambda x, place: (0, lax.rem(x - place[0] + NX, NX), 0, 0)
+    return pl.pallas_call(
+        kernel,
+        grid_spec=pltpu.PrefetchScalarGridSpec(
+            num_scalar_prefetch=1,
+            grid=(NX,),
+            in_specs=[
+                pl.BlockSpec((LENGTH, COLS), lambda x, place: (0, 0)),
+                pl.BlockSpec((8, NZ, ROWS, ROWS), lambda x, place: (0, x, 0, 0)),
+            ],
+            out_specs=pl.BlockSpec(block, out_map),
+        ),
+        out_shape=jax.ShapeDtypeStruct(shape, bf16),
         compiler_params=pltpu.CompilerParams(vmem_limit_bytes=60 << 20),
-        cost_estimate=pl.CostEstimate(flops=6 << 30, bytes_accessed=16 << 20, transcendentals=0),
-        name="project",
-    )(grouped, x)
-
-
-def optimizer_kernel(ga_ref, gb_ref, w_ref, m_ref, v_ref, m_out, v_out, dir_out, a_out, b_out, sums_out):
-    grad_a = jnp.sum(ga_ref[...].astype(f32), axis=0)
+        cost_estimate=pl.CostEstimate(
+            flops=2 * LENGTH * COLS * WIDTH * part // ROWS,
+            bytes_accessed=12 << 20,
+            transcendentals=0,
+        ),
+        name=name,
+    )(at_x, grouped, x)
+
+
+def optimizer_kernel(ga0, ga1, ga2, ga3, gb_ref, w_ref, m_ref, v_ref, m_out, v_out, dir_out, a_out, b_out, sums_out):
+    grad_a = ga0[...].astype(f32) + ga1[...].astype(f32)
+    grad_a = grad_a + ga2[...].astype(f32) + ga3[...].astype(f32)
     grad_b = jnp.sum(gb_ref[...].astype(f32), axis=0)
-    gradient = jnp.concatenate([grad_a, grad_b], axis=0).T
+    gradient = jnp.concatenate([grad_a, grad_b], axis=0)
     weight = w_ref[...]
     first_new = beta_first * m_ref[...] + (1.0 - beta_first) * gradient
     second_new = beta_second * v_ref[...] + (1.0 - beta_second) * gradient * gradient
@@ -197,7 +226,7 @@
         ],
         compiler_params=pltpu.CompilerParams(vmem_limit_bytes=32 << 20),
         name="optimizer",
-    )(ga, gb, w, m, v)
+    )(*ga, gb, w, m, v)
 
 
 def apply_kernel(place_ref, sums_ref, a0, a1, a2, a3, b_ref, a_out, b_out):
@@ -287,7 +316,7 @@
         out_specs=pl.BlockSpec((1, NZ, ROWS_A, COLS), lambda x: (x, 0, 0, 0)),
         out_shape=jax.ShapeDtypeStruct(FULL, bf16),
         input_output_aliases={0: 0},
-        compiler_params=pltpu.CompilerParams(vmem_limit_bytes=48 << 20),
+        compiler_params=pltpu.CompilerParams(vmem_limit_bytes=60 << 20),
         cost_estimate=pl.CostEstimate(flops=0, bytes_accessed=4 << 20, transcendentals=0),
         name="join_sc",
     )(base, full)
@@ -303,20 +332,23 @@
 
 
 def body(x, q, k, v, g, w, m, s):
+    x_turned = turn(x[0])
     packed = pack(q[0], k[0], v[0], g[0])
     heads = lax.all_to_all(packed, ("y", "core"), 0, 0, tiled=True).reshape(LENGTH, PACKED)
-    x_full = lax.all_gather(x[0], ("y", "core"), axis=0, tiled=True)
+    x_full = lax.all_gather(x_turned, ("y", "core"), axis=0, tiled=False)
     grouped = attention(heads)
 
-    part_a, part_b = project(grouped, x_full)
+    at_x = lax.axis_index("x")
+    place_x = at_x.reshape(1).astype(jnp.int32)
+    part_a = project(grouped, x_full, 0, PART_A, place_x, "project_a")
+    part_b = project(grouped, x_full, PART_A, ROWS, None, "project_b")
     part_a = lax.psum_scatter(part_a, "z", scatter_dimension=0, tiled=True)[0]
     part_b = lax.all_to_all(part_b, "x", 0, 0, tiled=True)
     part_b = jnp.sum(part_b.astype(f32), axis=0).astype(bf16)
     part_b = lax.all_to_all(part_b, "z", 0, 0, tiled=True)
-    part_a = lax.all_to_all(part_a, "x", 0, 0, tiled=True)
+    part_a = [part_a[0]] + [shift(part_a[by], "x", NX, by) for by in range(1, NX)]
 
     first_new, second_new, direction, mine_a, mine_b, sums = optimizer(part_a, part_b, w, m, s)
-    at_x = lax.axis_index("x")
     place = jnp.stack([at_x, (at_x + 3) % NX, (at_x + 1) % NX, (at_x + 2) % NX]).astype(jnp.int32)
     pieces = (
         mine_a,

time: 276 us -> 265 us (0.960)
  blocking collectives: 142 us -> 44.9 us
  waiting for transfers between devices: 50.9 us -> 112 us
  starting transfers between devices: 15.3 us -> 33.1 us
  Pallas kernels: 38 us -> 45.9 us
    all_to_all x3 -> x0, blocking collectives: 99.1 us -> none  [the longest x1 57.6 us: body(): lax.all_to_all(packed, ('y', 'core'), 0, 0, tiled=True)]
    all_to_all x0 -> x2, waiting for transfers between devices: none -> 59.8 us  [the longest x1 52.1 us: body(): lax.all_to_all(packed, ('y', 'core'), 0, 0, tiled=True)]
    all_to_all x0 -> x2, starting transfers between devices: none -> 13.4 us  [the longest x1 6.77 us: body(): lax.all_to_all(packed, ('y', 'core'), 0, 0, tiled=True)]
    pallas_call x1 -> x3, Pallas kernels: 12.4 us -> 18.3 us  [the longest x2 16 us: project(): pl.pallas_call(kernel, grid_spec=pltpu.PrefetchScalarGridSpec(num_scalar_...]
    ppermute x7 -> x10, starting transfers between devices: 10.2 us -> 14 us  [shift(): lax.ppermute(value, axis, [(i, (i + by) % size) for i in range(size)])]
    reduce_scatter x1, waiting for transfers between devices: 0.01 us -> 3.62 us  [body(): part_a = lax.psum_scatter(part_a, 'z', scatter_dimension=0, tiled=True)[0]]
    unnamed x16 -> x12, local copies, waits for them, and re-layouts: 6.79 us -> 3.33 us
    ppermute x7 -> x10, waiting for transfers between devices: 26.7 us -> 26.7 us  [shift(): lax.ppermute(value, axis, [(i, (i + by) % size) for i in range(size)])]
  transfers between devices with their start and end apart: 12 -> 17, of which waited for: 9 -> 12; matrix products, arithmetic and copies ran while one was open for 2% -> 3% of each run, Pallas kernels for 7% -> 10%
where the time goes in v5:
time: 265 us; the launch traced here: 264 us
  waiting for transfers between devices  112 us (42%)
  Pallas kernels  45.9 us (17%)
  blocking collectives  44.9 us (17%)
  starting transfers between devices  33.1 us (12%)
  between operations  15.2 us (6%)
  local copies, waits for them, and re-layouts  7.22 us (3%)
  other arithmetic  4.99 us (2%)
    all_to_all x1, waiting for transfers between devices, body(): lax.all_to_all(packed, ('y', 'core'), 0, 0, tiled=True)  52.1 us
    all_to_all x1, blocking collectives, body(): part_b = lax.all_to_all(part_b, 'x', 0, 0, tiled=True)  32.7 us
    ppermute x10, waiting for transfers between devices, shift(): lax.ppermute(value, axis, [(i, (i + by) % size) for i in range(size)])  26.7 us
    pallas_call x2, Pallas kernels, project(): pl.pallas_call(kernel, grid_spec=pltpu.PrefetchScalarGridSpec(num_scalar_...  16 us
    all_gather x1, waiting for transfers between devices, body(): full_a = lax.all_gather(new_a, 'z', axis=0, tiled=False)  14.6 us
    ppermute x10, starting transfers between devices, shift(): lax.ppermute(value, axis, [(i, (i + by) % size) for i in range(size)])  14 us
    pallas_call x1, Pallas kernels, attention(): pl.pallas_call(attention_kernel, grid=(GROUP,), in_specs=[pl.BlockSpec((L...  13.5 us
    all_to_all x1, blocking collectives, spread(): return lax.all_to_all(wide, axes, 0, 0, tiled=True)  12.2 us
  transfers between devices with their start and end apart: 17, of which 12 were waited for; matrix products, arithmetic and copies ran while one was open for 3% of the time, Pallas kernels for 10%

profile of v5, /device:TPU:1, one launch (start us, length us, event | category | flops | bytes accessed | tf_op | source)
XLA Modules:
  0.0 263.8 jit_solution(9591570608213472925)
XLA Ops:
  7.2 2.3 turn.1
  9.6 2.9 %pack.1 = bf16[8,128,1280]{2,1,0:T(8,128)(2,1)} custom-call(bf16[128,4096]{1,0:T(8,128)(2,1)} %bitcast.32, bf16[128,1024]{1,0:T(8,128)(2,1)} %bitcast.35, bf16[128,1024]{1,0:T(8,128)(2,1)} %bitcast.36, bf16[128,4096]{1,0:T(8,128)(2,1)} %bitcast.33), custom_call_target="tpu_custom_call" | custom-call | bytes 5242880 | tf_op jit(solution)/shard_map/pack/pallas_call | solution.py:52
  12.5 6.8 %all-to-all-start = ((bf16[8,128,1280]{2,1,0:T(8,128)(2,1)}), bf16[8,128,1280]{2,1,0:T(8,128)(2,1)S(1)}, u32[]{:S(2)}, u32[]{:S(2)}) async-start(bf16[8,128,1280]{2,1,0:T(8,128)(2,1)} %pack.1), calls=%async_computation | async-start | bytes 5242880 | tf_op jit(solution)/shard_map/all_to_all | solution.py:337
  19.3 52.1 %all-to-all-done = bf16[8,128,1280]{2,1,0:T(8,128)(2,1)S(1)} async-done(((bf16[8,128,1280]{2,1,0:T(8,128)(2,1)}), bf16[8,128,1280]{2,1,0:T(8,128)(2,1)S(1)}, u32[]{:S(2)}, u32[]{:S(2)}) %all-to-all-start) | async-done | bytes 2621472 | tf_op jit(solution)/shard_map/all_to_all | solution.py:337
  71.3 13.5 %attention_backward.1.grouped_ref = bf16[1024,768]{1,0:T(8,128)(2,1)S(1)} custom-call(bf16[1024,1280]{1,0:T(8,128)(2,1)S(1)} %bitcast.23, bf16[1024,1280]{1,0:T(8,128)(2,1)S(1)} %bitcast.24, bf16[1024,1280]{1,0:T(8,128)(2,1)S(1)} %bitcast.25, bf16[1024,1280]{1,0:T(8,128)(2,1)S(1)} %bitcast.26), custom_call_target="tpu_custom_call" | custom-call | flops 4294967296 | bytes 5242880 | tf_op jit(solution)/shard_map/attention_backward/pallas_call | solution.py:125
  84.9 1.2 copy-done
  87.1 8.7 %project_a.1 = bf16[8,4,80,768]{3,2,1,0:T(8,128)(2,1)} custom-call(s32[1]{0:T(128)} %bitcast.place, bf16[1024,768]{1,0:T(8,128)(2,1)} %copy-done, bf16[8,32,128,128]{3,2,1,0:T(8,128)(2,1)} %bitcast.29), custom_call_target="tpu_custom_call" | custom-call | flops 4026531840 | bytes 12582912 | tf_op jit(solution)/shard_map/project_a/pallas_call | solution.py:166
  95.9 7.3 %project_b.1 = bf16[4,8,48,768]{3,2,1,0:T(8,128)(2,1)} custom-call(s32[1]{0:T(128)} %constant.30.clone.1.place, bf16[1024,768]{1,0:T(8,128)(2,1)} %copy-done, bf16[8,32,128,128]{3,2,1,0:T(8,128)(2,1)} %bitcast.30), custom_call_target="tpu_custom_call" | custom-call | flops 2415919104 | bytes 12582912 | tf_op jit(solution)/shard_map/project_b/pallas_call | solution.py:166
  103.1 32.7 %all_to_all.25 = bf16[4,8,48,768]{3,2,1,0:T(8,128)(2,1)} all-to-all(bf16[4,8,48,768]{3,2,1,0:T(8,128)(2,1)} %project_b.1), channel_id=1, replica_groups=mesh['x'=4,'z'=8,'y'=4,'core'=2] {'x'}, dimensions={0} | all-to-all | bytes 4718592 | tf_op jit(solution)/shard_map/all_to_all | solution.py:346
  135.8 3.1 %reduce_sum.30 = bf16[8,48,768]{2,1,0:T(8,128)(2,1)} reduce(bf16[4,8,48,768]{3,2,1,0:T(8,128)(2,1)} %all_to_all.25, bf16[]{:T(256)} %constant.31.clone.1), dimensions={0}, to_apply=%region_1.0 | reduce | flops 884736 | bytes 2949122 | tf_op jit(solution)/shard_map/reduce_sum | solution.py:347
  138.9 6.6 %all-to-all-start.2 = ((bf16[8,48,768]{2,1,0:T(8,128)(2,1)}), bf16[8,48,768]{2,1,0:T(8,128)(2,1)S(1)}, u32[]{:S(2)}, u32[]{:S(2)}) async-start(bf16[8,48,768]{2,1,0:T(8,128)(2,1)} %reduce_sum.30), calls=%async_computation.3 | async-start | bytes 1179648 | tf_op jit(solution)/shard_map/all_to_all | solution.py:348
  145.5 3.6 %reduce-scatter.2.cloned.1.call-done = bf16[1,4,80,768]{3,2,1,0:T(8,128)(2,1)} async-done(((bf16[8,4,80,768]{3,2,1,0:T(8,128)(2,1)}), bf16[1,4,80,768]{3,2,1,0:T(8,128)(2,1)}) %reduce-scatter.2.cloned.1.call-update) | async-done | bytes 491536 | tf_op jit(solution)/shard_map/reduce_scatter | solution.py:345
  149.2 1.1 slice_bitcast_fusion
  150.3 2.5 collective-permute-start.2
  154.1 7.7 %all-to-all-done.2.gb_ref = bf16[8,48,768]{2,1,0:T(8,128)(2,1)S(1)} async-done(((bf16[8,48,768]{2,1,0:T(8,128)(2,1)}), bf16[8,48,768]{2,1,0:T(8,128)(2,1)S(1)}, u32[]{:S(2)}, u32[]{:S(2)}) %all-to-all-start.2) | async-done | bytes 589856 | tf_op jit(solution)/shard_map/all_to_all | solution.py:348
  161.8 1.7 optimizer.1
  164.3 12.2 %all_to_all.26 = f32[8,8,128]{2,1,0:T(8,128)S(1)} all-to-all(f32[8,8,128]{2,1,0:T(8,128)S(1)} %broadcast_in_dim.4), channel_id=1, replica_groups=mesh['x'=4,'z'=8,'y'=4,'core'=2] {'y','core'}, dimensions={0} | all-to-all | bytes 65536 | tf_op jit(solution)/shard_map/all_to_all | solution.py:331
  177.1 5.7 %all-to-all-start.4 = ((f32[32,8,128]{2,1,0:T(8,128)}), f32[32,8,128]{2,1,0:T(8,128)S(1)}, u32[]{:S(2)}, u32[]{:S(2)}) async-start(f32[32,8,128]{2,1,0:T(8,128)} %broadcast_in_dim.5), calls=%async_computation.5 | async-start | bytes 262144 | tf_op jit(solution)/shard_map/all_to_all | solution.py:331
  182.9 2.8 %collective-permute-start.5 = (bf16[2,64,768]{2,1,0:T(8,128)(2,1)S(1)}, bf16[2,64,768]{2,1,0:T(8,128)(2,1)S(1)}, u32[]{:S(2)}, u32[]{:S(2)}) collective-permute-start(bf16[2,64,768]{2,1,0:T(8,128)(2,1)S(1)} %get-tuple-element.16.a0), channel_id=1, source_target_pairs={{0,128},{64,192},{128,0},{192,64},{1,129},{65,193},{129,1},{193,65... | collective-permute-start | bytes 589832 | tf_op jit(solution)/shard_map/ppermute | solution.py:326
  187.3 3.2 %collective-permute-done.5.a3 = bf16[2,64,768]{2,1,0:T(8,128)(2,1)S(1)} collective-permute-done((bf16[2,64,768]{2,1,0:T(8,128)(2,1)S(1)}, bf16[2,64,768]{2,1,0:T(8,128)(2,1)S(1)}, u32[]{:S(2)}, u32[]{:S(2)}) %collective-permute-start.5) | collective-permute-done | bytes 196640 | tf_op jit(solution)/shard_map/ppermute | solution.py:326
  190.4 5.3 %collective-permute-done.4.a2 = bf16[2,64,768]{2,1,0:T(8,128)(2,1)S(1)} collective-permute-done((bf16[2,64,768]{2,1,0:T(8,128)(2,1)S(1)}, bf16[2,64,768]{2,1,0:T(8,128)(2,1)S(1)}, u32[]{:S(2)}, u32[]{:S(2)}) %collective-permute-start.4) | collective-permute-done | bytes 196640 | tf_op jit(solution)/shard_map/ppermute | solution.py:326
  196.1 6.6 %all-gather.9.cloned.1.call-done = bf16[16,64,768]{2,1,0:T(8,128)(2,1)} async-done(((bf16[2,64,768]{2,1,0:T(8,128)(2,1)}), bf16[16,64,768]{2,1,0:T(8,128)(2,1)}) %all-gather.9.cloned.1.call-update) | async-done | bytes 1572880 | tf_op jit(solution)/shard_map/all_gather | solution.py:359
  202.7 1.4 copy-done.1
  204.1 1.5 apply.1
  205.6 2.5 collective-permute-start.7
  208.0 13.1 %collective-permute-done.7.b2 = bf16[8,64,768]{2,1,0:T(8,128)(2,1)S(1)} collective-permute-done((bf16[8,64,768]{2,1,0:T(8,128)(2,1)S(1)}, bf16[8,64,768]{2,1,0:T(8,128)(2,1)S(1)}, u32[]{:S(2)}, u32[]{:S(2)}) %collective-permute-start.7) | collective-permute-done | bytes 786464 | tf_op jit(solution)/shard_map/ppermute | solution.py:326
  221.9 3.4 %collective-permute-start.9 = (bf16[4,64,768]{2,1,0:T(8,128)(2,1)}, bf16[4,64,768]{2,1,0:T(8,128)(2,1)S(1)}, u32[]{:S(2)}, u32[]{:S(2)}) collective-permute-start(bf16[4,64,768]{2,1,0:T(8,128)(2,1)} %slice.41), channel_id=1, source_target_pairs={{0,192},{64,0},{128,64},{192,128},{1,193},{65,1},{129,65},{193,129... | collective-permute-start | bytes 1179656 | tf_op jit(solution)/shard_map/ppermute | solution.py:326
  228.1 1.8 broadcast_multiply_fusion
  230.4 4.2 %collective-permute-done.8.b3 = bf16[4,64,768]{2,1,0:T(8,128)(2,1)S(1)} collective-permute-done((bf16[4,64,768]{2,1,0:T(8,128)(2,1)}, bf16[4,64,768]{2,1,0:T(8,128)(2,1)S(1)}, u32[]{:S(2)}, u32[]{:S(2)}) %collective-permute-start.8) | collective-permute-done | bytes 393248 | tf_op jit(solution)/shard_map/ppermute | solution.py:326
  234.6 3.9 %join_x.1.base_ref = bf16[4,8,128,768]{3,2,1,0:T(8,128)(2,1)} custom-call(s32[4]{0:T(128)S(1)} %pad_add_fusion.place_ref, bf16[8,64,768]{2,1,0:T(8,128)(2,1)S(1)} %get-tuple-element.18.b0, bf16[8,64,768]{2,1,0:T(8,128)(2,1)S(1)} %collective-permute-done.6.b1, bf16[8,64,768]{2,1,0:T(8,128)(2,1)S(1)} %collective-permute-done.7.b2, ...), custom_call_target="tpu_custom_call" | custom-call | bytes 7340032 | tf_op jit(solution)/shard_map/join_x/pallas_call | solution.py:286
  238.4 14.6 %all-gather.11.cloned.1.call-done = bf16[32,64,768]{2,1,0:T(8,128)(2,1)} async-done(((bf16[4,64,768]{2,1,0:T(8,128)(2,1)}), bf16[32,64,768]{2,1,0:T(8,128)(2,1)}) %all-gather.11.cloned.1.call-update) | async-done | bytes 3145744 | tf_op jit(solution)/shard_map/all_gather | solution.py:362
  253.1 4.2 %join_sc.1 = bf16[4,8,128,768]{3,2,1,0:T(8,128)(2,1)} custom-call(bf16[4,8,128,768]{3,2,1,0:T(8,128)(2,1)} %join_x.1.base_ref, bf16[8,4,64,768]{3,2,1,0:T(8,128)(2,1)} %bitcast.31), custom_call_target="tpu_custom_call", output_to_operand_aliasing={{}: (0, {})} | custom-call | bytes 4194304 | tf_op jit(solution)/shard_map/join_sc/pallas_call | solution.py:309
  (40 shorter events, 8.6 us)
Async XLA Ops:
  7.2 80.0 %all-gather.7.cloned.1.call-start = ((), (), s32[]{:S(2)}) async-start(), calls=%async_computation.7 | async-start | bytes 9437184 | tf_op jit(solution)/shard_map/all_gather | solution.py:338
  12.5 58.9 %all-to-all-start = ((bf16[8,128,1280]{2,1,0:T(8,128)(2,1)}), bf16[8,128,1280]{2,1,0:T(8,128)(2,1)S(1)}, u32[]{:S(2)}, u32[]{:S(2)}) async-start(bf16[8,128,1280]{2,1,0:T(8,128)(2,1)} %pack.1), calls=%async_computation | async-start | bytes 5242880 | tf_op jit(solution)/shard_map/all_to_all | solution.py:337
  19.3 129.9 %reduce-scatter.2.cloned.1.call-start = ((), (), s32[]{:S(2)}) async-start(), calls=%async_computation.6 | async-start | bytes 4423680 | tf_op jit(solution)/shard_map/reduce_scatter | solution.py:345
  84.9 1.2 copy-start
  135.8 26.0 %copy-start.3 = (f32[128,768]{1,0:T(8,128)S(1)}, f32[128,768]{1,0:T(8,128)}, u32[]{:S(2)}) copy-start(f32[128,768]{1,0:T(8,128)} %w_ref.1) | copy-start | bytes 1179652
  135.8 26.0 %copy-start.4 = (f32[128,768]{1,0:T(8,128)S(1)}, f32[128,768]{1,0:T(8,128)}, u32[]{:S(2)}) copy-start(f32[128,768]{1,0:T(8,128)} %m_ref.1) | copy-start | bytes 1179652
  135.8 26.0 %copy-start.5 = (f32[128,768]{1,0:T(8,128)S(1)}, f32[128,768]{1,0:T(8,128)}, u32[]{:S(2)}) copy-start(f32[128,768]{1,0:T(8,128)} %v_ref.1) | copy-start | bytes 1179652
  138.9 22.9 %all-to-all-start.2 = ((bf16[8,48,768]{2,1,0:T(8,128)(2,1)}), bf16[8,48,768]{2,1,0:T(8,128)(2,1)S(1)}, u32[]{:S(2)}, u32[]{:S(2)}) async-start(bf16[8,48,768]{2,1,0:T(8,128)(2,1)} %reduce_sum.30), calls=%async_computation.3 | async-start | bytes 1179648 | tf_op jit(solution)/shard_map/all_to_all | solution.py:348
  145.5 57.2 %all-gather.9.cloned.1.call-start = ((), (), s32[]{:S(2)}) async-start(), calls=%async_computation.8 | async-start | bytes 1769472 | tf_op jit(solution)/shard_map/all_gather | solution.py:359
  150.3 11.5 %collective-permute-start.2 = (bf16[80,768]{1,0:T(8,128)(2,1)S(1)}, bf16[80,768]{1,0:T(8,128)(2,1)S(1)}, u32[]{:S(2)}, u32[]{:S(2)}) collective-permute-start(bf16[80,768]{1,0:T(8,128)(2,1)S(1)} %get-tuple-element.20), channel_id=1, source_target_pairs={{0,192},{64,0},{128,64},{192,128},{1,193},{65,1},{129,65},{193,129... | collective-permute-start | bytes 368648 | tf_op jit(solution)/shard_map/ppermute | solution.py:326
  152.8 9.0 %collective-permute-start.1 = (bf16[80,768]{1,0:T(8,128)(2,1)S(1)}, bf16[80,768]{1,0:T(8,128)(2,1)S(1)}, u32[]{:S(2)}, u32[]{:S(2)}) collective-permute-start(bf16[80,768]{1,0:T(8,128)(2,1)S(1)} %get-tuple-element.21), channel_id=1, source_target_pairs={{0,128},{64,192},{128,0},{192,64},{1,129},{65,193},{129,1},{193,65... | collective-permute-start | bytes 368648 | tf_op jit(solution)/shard_map/ppermute | solution.py:326
  153.3 8.5 %collective-permute-start = (bf16[80,768]{1,0:T(8,128)(2,1)S(1)}, bf16[80,768]{1,0:T(8,128)(2,1)S(1)}, u32[]{:S(2)}, u32[]{:S(2)}) collective-permute-start(bf16[80,768]{1,0:T(8,128)(2,1)S(1)} %get-tuple-element.22), channel_id=1, source_target_pairs={{0,64},{64,128},{128,192},{192,0},{1,65},{65,129},{129,193},{193,1... | collective-permute-start | bytes 368648 | tf_op jit(solution)/shard_map/ppermute | solution.py:326
  163.5 0.7 copy-start.2
  177.1 18.9 %all-to-all-start.4 = ((f32[32,8,128]{2,1,0:T(8,128)}), f32[32,8,128]{2,1,0:T(8,128)S(1)}, u32[]{:S(2)}, u32[]{:S(2)}) async-start(f32[32,8,128]{2,1,0:T(8,128)} %broadcast_in_dim.5), calls=%async_computation.5 | async-start | bytes 262144 | tf_op jit(solution)/shard_map/all_to_all | solution.py:331
  182.8 70.2 %all-gather.11.cloned.1.call-start = ((), (), s32[]{:S(2)}) async-start(), calls=%async_computation.9 | async-start | bytes 3538944 | tf_op jit(solution)/shard_map/all_gather | solution.py:362
  182.9 7.5 %collective-permute-start.5 = (bf16[2,64,768]{2,1,0:T(8,128)(2,1)S(1)}, bf16[2,64,768]{2,1,0:T(8,128)(2,1)S(1)}, u32[]{:S(2)}, u32[]{:S(2)}) collective-permute-start(bf16[2,64,768]{2,1,0:T(8,128)(2,1)S(1)} %get-tuple-element.16.a0), channel_id=1, source_target_pairs={{0,128},{64,192},{128,0},{192,64},{1,129},{65,193},{129,1},{193,65... | collective-permute-start | bytes 589832 | tf_op jit(solution)/shard_map/ppermute | solution.py:326
  185.7 10.1 %collective-permute-start.4 = (bf16[2,64,768]{2,1,0:T(8,128)(2,1)S(1)}, bf16[2,64,768]{2,1,0:T(8,128)(2,1)S(1)}, u32[]{:S(2)}, u32[]{:S(2)}) collective-permute-start(bf16[2,64,768]{2,1,0:T(8,128)(2,1)S(1)} %get-tuple-element.16.a0), channel_id=1, source_target_pairs={{0,192},{64,0},{128,64},{192,128},{1,193},{65,1},{129,65},{193,129... | collective-permute-start | bytes 589832 | tf_op jit(solution)/shard_map/ppermute | solution.py:326
  186.6 9.5 %collective-permute-start.3 = (bf16[2,64,768]{2,1,0:T(8,128)(2,1)S(1)}, bf16[2,64,768]{2,1,0:T(8,128)(2,1)S(1)}, u32[]{:S(2)}, u32[]{:S(2)}) collective-permute-start(bf16[2,64,768]{2,1,0:T(8,128)(2,1)S(1)} %get-tuple-element.16.a0), channel_id=1, source_target_pairs={{0,64},{64,128},{128,192},{192,0},{1,65},{65,129},{129,193},{193,1... | collective-permute-start | bytes 589832 | tf_op jit(solution)/shard_map/ppermute | solution.py:326
  202.6 1.4 copy-start.1
  205.6 15.6 %collective-permute-start.7 = (bf16[8,64,768]{2,1,0:T(8,128)(2,1)S(1)}, bf16[8,64,768]{2,1,0:T(8,128)(2,1)S(1)}, u32[]{:S(2)}, u32[]{:S(2)}) collective-permute-start(bf16[8,64,768]{2,1,0:T(8,128)(2,1)S(1)} %get-tuple-element.18.b0), channel_id=1, source_target_pairs={{0,192},{64,0},{128,64},{192,128},{1,193},{65,1},{129,65},{193,129... | collective-permute-start | bytes 2359304 | tf_op jit(solution)/shard_map/ppermute | solution.py:326
  208.0 17.3 %collective-permute-start.6 = (bf16[8,64,768]{2,1,0:T(8,128)(2,1)S(1)}, bf16[8,64,768]{2,1,0:T(8,128)(2,1)S(1)}, u32[]{:S(2)}, u32[]{:S(2)}) collective-permute-start(bf16[8,64,768]{2,1,0:T(8,128)(2,1)S(1)} %get-tuple-element.18.b0), channel_id=1, source_target_pairs={{0,64},{64,128},{128,192},{192,0},{1,65},{65,129},{129,193},{193,1... | collective-permute-start | bytes 2359304 | tf_op jit(solution)/shard_map/ppermute | solution.py:326
  221.9 8.4 %collective-permute-start.9 = (bf16[4,64,768]{2,1,0:T(8,128)(2,1)}, bf16[4,64,768]{2,1,0:T(8,128)(2,1)S(1)}, u32[]{:S(2)}, u32[]{:S(2)}) collective-permute-start(bf16[4,64,768]{2,1,0:T(8,128)(2,1)} %slice.41), channel_id=1, source_target_pairs={{0,192},{64,0},{128,64},{192,128},{1,193},{65,1},{129,65},{193,129... | collective-permute-start | bytes 1179656 | tf_op jit(solution)/shard_map/ppermute | solution.py:326
  226.1 8.4 %collective-permute-start.8 = (bf16[4,64,768]{2,1,0:T(8,128)(2,1)}, bf16[4,64,768]{2,1,0:T(8,128)(2,1)S(1)}, u32[]{:S(2)}, u32[]{:S(2)}) collective-permute-start(bf16[4,64,768]{2,1,0:T(8,128)(2,1)} %slice.40), channel_id=1, source_target_pairs={{0,64},{64,128},{128,192},{192,0},{1,65},{65,129},{129,193},{193,1... | collective-permute-start | bytes 1179656 | tf_op jit(solution)/shard_map/ppermute | solution.py:326
Sparse Core Ops, SparseCore 0:
  9.9 77.2 all-gather.6
  96.0 53.1 reduce-scatter.1
  164.4 38.1 all-gather.8
  205.7 47.3 all-gather.10

commit v6 on v5

--- a/solution.py
+++ b/solution.py
@@ -138,7 +138,7 @@
             pltpu.VMEM((LENGTH, 128), f32),
             pltpu.VMEM((LENGTH, 128), f32),
         ],
-        compiler_params=pltpu.CompilerParams(vmem_limit_bytes=48 << 20),
+        compiler_params=pltpu.CompilerParams(vmem_limit_bytes=62 << 20),
         cost_estimate=pl.CostEstimate(
             flops=4 << 30, bytes_accessed=5 << 20, transcendentals=4 << 20
         ),
@@ -146,25 +146,16 @@
     )(packed, packed, packed, packed)
 
 
-def project(grouped, x, lo, hi, at_x, name):
-    part = hi - lo
-
-    def kernel(place, grouped_ref, x_ref, out_ref):
-        rows = jnp.concatenate(
-            [x_ref[t, :, lo:hi, :].reshape(NZ * part, ROWS) for t in range(8)], axis=1
-        )
-        res = dot(rows, grouped_ref[...], 1, 0).astype(bf16)
-        out_ref[...] = res.reshape(out_ref.shape)
-
-    if at_x is None:
-        shape, block = (NX, NZ, part, COLS), (1, NZ, part, COLS)
-        out_map = lambda x, place: (x, 0, 0, 0)
-        at_x = jnp.zeros((1,), jnp.int32)
-    else:
-        shape, block = (NZ, NX, part, COLS), (NZ, 1, part, COLS)
-        out_map = lambda x, place: (0, lax.rem(x - place[0] + NX, NX), 0, 0)
-    return pl.pallas_call(
-        kernel,
+def project_kernel(place, grouped_ref, x_ref, a_ref, b_ref):
+    rows = jnp.concatenate([x_ref[t].reshape(NZ * ROWS, ROWS) for t in range(8)], axis=1)
+    res = dot(rows, grouped_ref[...], 1, 0).astype(bf16).reshape(NZ, ROWS, COLS)
+    a_ref[:, 0] = res[:, :PART_A]
+    b_ref[0] = res[:, PART_A:]
+
+
+def project(at_x, grouped, x):
+    return pl.pallas_call(
+        project_kernel,
         grid_spec=pltpu.PrefetchScalarGridSpec(
             num_scalar_prefetch=1,
             grid=(NX,),
@@ -172,17 +163,39 @@
                 pl.BlockSpec((LENGTH, COLS), lambda x, place: (0, 0)),
                 pl.BlockSpec((8, NZ, ROWS, ROWS), lambda x, place: (0, x, 0, 0)),
             ],
-            out_specs=pl.BlockSpec(block, out_map),
+            out_specs=[
+                pl.BlockSpec(
+                    (NZ, 1, PART_A, COLS),
+                    lambda x, place: (0, lax.rem(x - place[0] + NX, NX), 0, 0),
+                ),
+                pl.BlockSpec((1, NZ, PART_B, COLS), lambda x, place: (x, 0, 0, 0)),
+            ],
         ),
-        out_shape=jax.ShapeDtypeStruct(shape, bf16),
+        out_shape=[
+            jax.ShapeDtypeStruct((NZ, NX, PART_A, COLS), bf16),
+            jax.ShapeDtypeStruct((NX, NZ, PART_B, COLS), bf16),
+        ],
+        compiler_params=pltpu.CompilerParams(vmem_limit_bytes=62 << 20),
+        cost_estimate=pl.CostEstimate(flops=6 << 30, bytes_accessed=16 << 20, transcendentals=0),
+        name="project",
+    )(at_x, grouped, x)
+
+
+def fold_kernel(part_ref, out_ref):
+    out_ref[...] = jnp.sum(part_ref[...].astype(f32), axis=0).astype(bf16)
+
+
+def fold(part):
+    return pl.pallas_call(
+        fold_kernel,
+        grid=(4,),
+        in_specs=[pl.BlockSpec((NX, NZ // 4, PART_B, COLS), lambda z: (0, z, 0, 0))],
+        out_specs=pl.BlockSpec((NZ // 4, PART_B, COLS), lambda z: (z, 0, 0)),
+        out_shape=jax.ShapeDtypeStruct((NZ, PART_B, COLS), bf16),
         compiler_params=pltpu.CompilerParams(vmem_limit_bytes=60 << 20),
-        cost_estimate=pl.CostEstimate(
-            flops=2 * LENGTH * COLS * WIDTH * part // ROWS,
-            bytes_accessed=12 << 20,
-            transcendentals=0,
-        ),
-        name=name,
-    )(at_x, grouped, x)
+        cost_estimate=pl.CostEstimate(flops=0, bytes_accessed=3 << 20, transcendentals=0),
+        name="fold",
+    )(part)
 
 
 def optimizer_kernel(ga0, ga1, ga2, ga3, gb_ref, w_ref, m_ref, v_ref, m_out, v_out, dir_out, a_out, b_out, sums_out):
@@ -340,11 +353,10 @@
 
     at_x = lax.axis_index("x")
     place_x = at_x.reshape(1).astype(jnp.int32)
-    part_a = project(grouped, x_full, 0, PART_A, place_x, "project_a")
-    part_b = project(grouped, x_full, PART_A, ROWS, None, "project_b")
+    part_a, part_b = project(place_x, grouped, x_full)
     part_a = lax.psum_scatter(part_a, "z", scatter_dimension=0, tiled=True)[0]
     part_b = lax.all_to_all(part_b, "x", 0, 0, tiled=True)
-    part_b = jnp.sum(part_b.astype(f32), axis=0).astype(bf16)
+    part_b = fold(part_b)
     part_b = lax.all_to_all(part_b, "z", 0, 0, tiled=True)
     part_a = [part_a[0]] + [shift(part_a[by], "x", NX, by) for by in range(1, NX)]
 

time: 265 us -> 276 us (1.042)
  waiting for transfers between devices: 112 us -> 127 us
  blocking collectives: 44.9 us -> 41.7 us
  starting transfers between devices: 33.1 us -> 36.2 us
  other arithmetic: 4.99 us -> 1.9 us
    reduce_scatter x1, waiting for transfers between devices: 3.62 us -> 18.5 us  [body(): part_a = lax.psum_scatter(part_a, 'z', scatter_dimension=0, tiled=True)[0]]
    all_to_all x1, waiting for transfers between devices: 7.69 us -> 0.01 us  [body(): part_b = lax.all_to_all(part_b, 'z', 0, 0, tiled=True)]
    ppermute x10, waiting for transfers between devices: 26.7 us -> 34 us  [shift(): lax.ppermute(value, axis, [(i, (i + by) % size) for i in range(size)])]
    reduce_sum x1 -> x0, other arithmetic: 3.09 us -> none  [body(): part_b = jnp.sum(part_b.astype(f32), axis=0).astype(bf16)]
  transfers between devices with their start and end apart: 17 -> 17, of which waited for: 12 -> 13; matrix products, arithmetic and copies ran while one was open for 3% -> 2% of each run, Pallas kernels for 10% -> 9%
where the time goes in v6:
time: 276 us
  waiting for transfers between devices  127 us (46%)
  Pallas kernels  46.5 us (17%)
  blocking collectives  41.7 us (15%)
  starting transfers between devices  36.2 us (13%)
  between operations  15 us (5%)
  local copies, waits for them, and re-layouts  7.66 us (3%)
    all_to_all x1, waiting for transfers between devices, body(): lax.all_to_all(packed, ('y', 'core'), 0, 0, tiled=True)  52.9 us
    ppermute x10, waiting for transfers between devices, shift(): lax.ppermute(value, axis, [(i, (i + by) % size) for i in range(size)])  34 us
    all_to_all x1, blocking collectives, body(): part_b = lax.all_to_all(part_b, 'x', 0, 0, tiled=True)  30.6 us
    reduce_scatter x1, waiting for transfers between devices, body(): part_a = lax.psum_scatter(part_a, 'z', scatter_dimension=0, tiled=True)[0]  18.5 us
    ppermute x10, starting transfers between devices, shift(): lax.ppermute(value, axis, [(i, (i + by) % size) for i in range(size)])  16.1 us
    pallas_call x1, Pallas kernels, attention(): pl.pallas_call(attention_kernel, grid=(GROUP,), in_specs=[pl.BlockSpec((L...  15.4 us
    all_gather x1, waiting for transfers between devices, body(): full_a = lax.all_gather(new_a, 'z', axis=0, tiled=False)  14.7 us
    all_to_all x1, blocking collectives, spread(): return lax.all_to_all(wide, axes, 0, 0, tiled=True)  11.1 us
  transfers between devices with their start and end apart: 17, of which 13 were waited for; matrix products, arithmetic and copies ran while one was open for 2% of the time, Pallas kernels for 9%

profile of v6, /device:TPU:1, one launch (start us, length us, event | category | flops | bytes accessed | tf_op | source)
XLA Modules:
  0.0 275.6 jit_solution(500799434780488160)
XLA Ops:
  7.2 2.3 turn.1
  9.5 2.9 %pack.1 = bf16[8,128,1280]{2,1,0:T(8,128)(2,1)} custom-call(bf16[128,4096]{1,0:T(8,128)(2,1)} %bitcast.26, bf16[128,1024]{1,0:T(8,128)(2,1)} %bitcast.29, bf16[128,1024]{1,0:T(8,128)(2,1)} %bitcast.30, bf16[128,4096]{1,0:T(8,128)(2,1)} %bitcast.27), custom_call_target="tpu_custom_call" | custom-call | bytes 5242880 | tf_op jit(solution)/shard_map/pack/pallas_call | solution.py:52
  12.4 7.5 %all-to-all-start = ((bf16[8,128,1280]{2,1,0:T(8,128)(2,1)}), bf16[8,128,1280]{2,1,0:T(8,128)(2,1)}, u32[]{:S(2)}, u32[]{:S(2)}) async-start(bf16[8,128,1280]{2,1,0:T(8,128)(2,1)} %pack.1), calls=%async_computation | async-start | bytes 5242880 | tf_op jit(solution)/shard_map/all_to_all | solution.py:350
  20.0 52.9 %all-to-all-done = bf16[8,128,1280]{2,1,0:T(8,128)(2,1)} async-done(((bf16[8,128,1280]{2,1,0:T(8,128)(2,1)}), bf16[8,128,1280]{2,1,0:T(8,128)(2,1)}, u32[]{:S(2)}, u32[]{:S(2)}) %all-to-all-start) | async-done | bytes 2621472 | tf_op jit(solution)/shard_map/all_to_all | solution.py:350
  72.9 15.4 %attention_backward.1.grouped_ref = bf16[1024,768]{1,0:T(8,128)(2,1)} custom-call(bf16[1024,1280]{1,0:T(8,128)(2,1)} %bitcast.5.q_ref.k_ref.v_ref.g_ref, bf16[1024,1280]{1,0:T(8,128)(2,1)} %bitcast.5.q_ref.k_ref.v_ref.g_ref, bf16[1024,1280]{1,0:T(8,128)(2,1)} %bitcast.5.q_ref.k_ref.v_ref.g_ref, bf16[1024,1280]{1,0:T(8,128)(2,1)} %bitcast.5.q_ref.k_ref.v_ref.g_ref), custom_call_target="tpu_custom_call" | custom-call | flops 4294967296 | bytes 5242880 | tf_op jit(solution)/shard_map/attention_backward/pallas_call | solution.py:125
  88.3 10.9 %project.1 = (bf16[8,4,80,768]{3,2,1,0:T(8,128)(2,1)}, bf16[4,8,48,768]{3,2,1,0:T(8,128)(2,1)}) custom-call(s32[1]{0:T(128)} %bitcast.place, bf16[1024,768]{1,0:T(8,128)(2,1)} %attention_backward.1.grouped_ref, bf16[8,32,128,128]{3,2,1,0:T(8,128)(2,1)} %bitcast.31), custom_call_target="tpu_custom_call" | custom-call | flops 6442450944 | bytes 16777216 | tf_op jit(solution)/shard_map/project/pallas_call | solution.py:157
  99.2 1.6 copy-done.5
  100.9 30.6 %all_to_all.25.part_ref = bf16[4,8,48,768]{3,2,1,0:T(8,128)(2,1)} all-to-all(bf16[4,8,48,768]{3,2,1,0:T(8,128)(2,1)S(1)} %copy-done.5), channel_id=1, replica_groups=mesh['x'=4,'z'=8,'y'=4,'core'=2] {'x'}, dimensions={0} | all-to-all | bytes 4718592 | tf_op jit(solution)/shard_map/all_to_all | solution.py:358
  131.5 3.7 %fold.1 = bf16[8,48,768]{2,1,0:T(8,128)(2,1)} custom-call(bf16[4,8,48,768]{3,2,1,0:T(8,128)(2,1)} %all_to_all.25.part_ref), custom_call_target="tpu_custom_call" | custom-call | bytes 3145728 | tf_op jit(solution)/shard_map/fold/pallas_call | solution.py:189
  135.2 6.6 %all-to-all-start.2 = ((bf16[8,48,768]{2,1,0:T(8,128)(2,1)}), bf16[8,48,768]{2,1,0:T(8,128)(2,1)S(1)}, u32[]{:S(2)}, u32[]{:S(2)}) async-start(bf16[8,48,768]{2,1,0:T(8,128)(2,1)} %fold.1), calls=%async_computation.3 | async-start | bytes 1179648 | tf_op jit(solution)/shard_map/all_to_all | solution.py:360
  141.8 18.5 %reduce-scatter.2.cloned.1.call-done = bf16[1,4,80,768]{3,2,1,0:T(8,128)(2,1)} async-done(((bf16[8,4,80,768]{3,2,1,0:T(8,128)(2,1)}), bf16[1,4,80,768]{3,2,1,0:T(8,128)(2,1)}) %reduce-scatter.2.cloned.1.call-update) | async-done | bytes 491536 | tf_op jit(solution)/shard_map/reduce_scatter | solution.py:357
  160.4 1.1 slice_bitcast_fusion
  161.5 4.2 %collective-permute-start.2 = (bf16[80,768]{1,0:T(8,128)(2,1)S(1)}, bf16[80,768]{1,0:T(8,128)(2,1)S(1)}, u32[]{:S(2)}, u32[]{:S(2)}) collective-permute-start(bf16[80,768]{1,0:T(8,128)(2,1)S(1)} %get-tuple-element.24), channel_id=1, source_target_pairs={{0,192},{64,0},{128,64},{192,128},{1,193},{65,1},{129,65},{193,129... | collective-permute-start | bytes 368648 | tf_op jit(solution)/shard_map/ppermute | solution.py:339
  167.6 3.4 %collective-permute-done.1.ga2 = bf16[80,768]{1,0:T(8,128)(2,1)S(1)} collective-permute-done((bf16[80,768]{1,0:T(8,128)(2,1)S(1)}, bf16[80,768]{1,0:T(8,128)(2,1)S(1)}, u32[]{:S(2)}, u32[]{:S(2)}) %collective-permute-start.1) | collective-permute-done | bytes 122912 | tf_op jit(solution)/shard_map/ppermute | solution.py:339
  171.0 3.5 %collective-permute-done.ga1 = bf16[80,768]{1,0:T(8,128)(2,1)S(1)} collective-permute-done((bf16[80,768]{1,0:T(8,128)(2,1)S(1)}, bf16[80,768]{1,0:T(8,128)(2,1)S(1)}, u32[]{:S(2)}, u32[]{:S(2)}) %collective-permute-start) | collective-permute-done | bytes 122912 | tf_op jit(solution)/shard_map/ppermute | solution.py:339
  174.5 1.7 optimizer.1
  177.0 11.1 %all_to_all.26 = f32[8,8,128]{2,1,0:T(8,128)S(1)} all-to-all(f32[8,8,128]{2,1,0:T(8,128)S(1)} %broadcast_in_dim.4), channel_id=1, replica_groups=mesh['x'=4,'z'=8,'y'=4,'core'=2] {'y','core'}, dimensions={0} | all-to-all | bytes 65536 | tf_op jit(solution)/shard_map/all_to_all | solution.py:344
  188.8 5.9 %all-to-all-start.4 = ((f32[32,8,128]{2,1,0:T(8,128)}), f32[32,8,128]{2,1,0:T(8,128)S(1)}, u32[]{:S(2)}, u32[]{:S(2)}) async-start(f32[32,8,128]{2,1,0:T(8,128)} %broadcast_in_dim.5), calls=%async_computation.5 | async-start | bytes 262144 | tf_op jit(solution)/shard_map/all_to_all | solution.py:344
  194.7 2.8 %collective-permute-start.5 = (bf16[2,64,768]{2,1,0:T(8,128)(2,1)S(1)}, bf16[2,64,768]{2,1,0:T(8,128)(2,1)S(1)}, u32[]{:S(2)}, u32[]{:S(2)}) collective-permute-start(bf16[2,64,768]{2,1,0:T(8,128)(2,1)S(1)} %get-tuple-element.20.a0), channel_id=1, source_target_pairs={{0,128},{64,192},{128,0},{192,64},{1,129},{65,193},{129,1},{193,65... | collective-permute-start | bytes 589832 | tf_op jit(solution)/shard_map/ppermute | solution.py:339
  199.1 3.2 %collective-permute-done.5.a3 = bf16[2,64,768]{2,1,0:T(8,128)(2,1)S(1)} collective-permute-done((bf16[2,64,768]{2,1,0:T(8,128)(2,1)S(1)}, bf16[2,64,768]{2,1,0:T(8,128)(2,1)S(1)}, u32[]{:S(2)}, u32[]{:S(2)}) %collective-permute-start.5) | collective-permute-done | bytes 196640 | tf_op jit(solution)/shard_map/ppermute | solution.py:339
  202.2 5.4 %collective-permute-done.4.a2 = bf16[2,64,768]{2,1,0:T(8,128)(2,1)S(1)} collective-permute-done((bf16[2,64,768]{2,1,0:T(8,128)(2,1)S(1)}, bf16[2,64,768]{2,1,0:T(8,128)(2,1)S(1)}, u32[]{:S(2)}, u32[]{:S(2)}) %collective-permute-start.4) | collective-permute-done | bytes 196640 | tf_op jit(solution)/shard_map/ppermute | solution.py:339
  207.9 6.5 %all-gather.9.cloned.1.call-done = bf16[16,64,768]{2,1,0:T(8,128)(2,1)} async-done(((bf16[2,64,768]{2,1,0:T(8,128)(2,1)}), bf16[16,64,768]{2,1,0:T(8,128)(2,1)}) %all-gather.9.cloned.1.call-update) | async-done | bytes 1572880 | tf_op jit(solution)/shard_map/all_gather | solution.py:371
  214.5 1.4 copy-done
  215.9 1.5 apply.1
  217.4 2.5 collective-permute-start.7
  219.8 13.1 %collective-permute-done.7.b2 = bf16[8,64,768]{2,1,0:T(8,128)(2,1)S(1)} collective-permute-done((bf16[8,64,768]{2,1,0:T(8,128)(2,1)S(1)}, bf16[8,64,768]{2,1,0:T(8,128)(2,1)S(1)}, u32[]{:S(2)}, u32[]{:S(2)}) %collective-permute-start.7) | collective-permute-done | bytes 786464 | tf_op jit(solution)/shard_map/ppermute | solution.py:339
  233.7 3.4 %collective-permute-start.9 = (bf16[4,64,768]{2,1,0:T(8,128)(2,1)}, bf16[4,64,768]{2,1,0:T(8,128)(2,1)S(1)}, u32[]{:S(2)}, u32[]{:S(2)}) collective-permute-start(bf16[4,64,768]{2,1,0:T(8,128)(2,1)} %slice.41), channel_id=1, source_target_pairs={{0,192},{64,0},{128,64},{192,128},{1,193},{65,1},{129,65},{193,129... | collective-permute-start | bytes 1179656 | tf_op jit(solution)/shard_map/ppermute | solution.py:339
  239.7 1.8 broadcast_multiply_fusion
  242.2 4.2 %collective-permute-done.8.b3 = bf16[4,64,768]{2,1,0:T(8,128)(2,1)S(1)} collective-permute-done((bf16[4,64,768]{2,1,0:T(8,128)(2,1)}, bf16[4,64,768]{2,1,0:T(8,128)(2,1)S(1)}, u32[]{:S(2)}, u32[]{:S(2)}) %collective-permute-start.8) | collective-permute-done | bytes 393248 | tf_op jit(solution)/shard_map/ppermute | solution.py:339
  246.4 3.9 %join_x.1.base_ref = bf16[4,8,128,768]{3,2,1,0:T(8,128)(2,1)} custom-call(s32[4]{0:T(128)S(1)} %pad_add_fusion.place_ref, bf16[8,64,768]{2,1,0:T(8,128)(2,1)S(1)} %get-tuple-element.22.b0, bf16[8,64,768]{2,1,0:T(8,128)(2,1)S(1)} %collective-permute-done.6.b1, bf16[8,64,768]{2,1,0:T(8,128)(2,1)S(1)} %collective-permute-done.7.b2, ...), custom_call_target="tpu_custom_call" | custom-call | bytes 7340032 | tf_op jit(solution)/shard_map/join_x/pallas_call | solution.py:299
  250.2 14.7 %all-gather.11.cloned.1.call-done = bf16[32,64,768]{2,1,0:T(8,128)(2,1)} async-done(((bf16[4,64,768]{2,1,0:T(8,128)(2,1)}), bf16[32,64,768]{2,1,0:T(8,128)(2,1)}) %all-gather.11.cloned.1.call-update) | async-done | bytes 3145744 | tf_op jit(solution)/shard_map/all_gather | solution.py:374
  264.9 4.2 %join_sc.1 = bf16[4,8,128,768]{3,2,1,0:T(8,128)(2,1)} custom-call(bf16[4,8,128,768]{3,2,1,0:T(8,128)(2,1)} %join_x.1.base_ref, bf16[8,4,64,768]{3,2,1,0:T(8,128)(2,1)} %bitcast.25), custom_call_target="tpu_custom_call", output_to_operand_aliasing={{}: (0, {})} | custom-call | bytes 4194304 | tf_op jit(solution)/shard_map/join_sc/pallas_call | solution.py:322
  (39 shorter events, 8.2 us)
Async XLA Ops:
  7.2 81.1 %all-gather.7.cloned.1.call-start = ((), (), s32[]{:S(2)}) async-start(), calls=%async_computation.7 | async-start | bytes 9437184 | tf_op jit(solution)/shard_map/all_gather | solution.py:351
  12.4 60.4 %all-to-all-start = ((bf16[8,128,1280]{2,1,0:T(8,128)(2,1)}), bf16[8,128,1280]{2,1,0:T(8,128)(2,1)}, u32[]{:S(2)}, u32[]{:S(2)}) async-start(bf16[8,128,1280]{2,1,0:T(8,128)(2,1)} %pack.1), calls=%async_computation | async-start | bytes 5242880 | tf_op jit(solution)/shard_map/all_to_all | solution.py:350
  20.0 140.4 %reduce-scatter.2.cloned.1.call-start = ((), (), s32[]{:S(2)}) async-start(), calls=%async_computation.6 | async-start | bytes 4423680 | tf_op jit(solution)/shard_map/reduce_scatter | solution.py:357
  99.2 1.7 copy-start.5
  131.5 43.0 %copy-start.2 = (f32[128,768]{1,0:T(8,128)S(1)}, f32[128,768]{1,0:T(8,128)}, u32[]{:S(2)}) copy-start(f32[128,768]{1,0:T(8,128)} %w_ref.1) | copy-start | bytes 1179652
  131.5 43.0 %copy-start.3 = (f32[128,768]{1,0:T(8,128)S(1)}, f32[128,768]{1,0:T(8,128)}, u32[]{:S(2)}) copy-start(f32[128,768]{1,0:T(8,128)} %m_ref.1) | copy-start | bytes 1179652
  131.5 43.0 %copy-start.4 = (f32[128,768]{1,0:T(8,128)S(1)}, f32[128,768]{1,0:T(8,128)}, u32[]{:S(2)}) copy-start(f32[128,768]{1,0:T(8,128)} %v_ref.1) | copy-start | bytes 1179652
  135.2 32.2 %all-to-all-start.2 = ((bf16[8,48,768]{2,1,0:T(8,128)(2,1)}), bf16[8,48,768]{2,1,0:T(8,128)(2,1)S(1)}, u32[]{:S(2)}, u32[]{:S(2)}) async-start(bf16[8,48,768]{2,1,0:T(8,128)(2,1)} %fold.1), calls=%async_computation.3 | async-start | bytes 1179648 | tf_op jit(solution)/shard_map/all_to_all | solution.py:360
  141.8 72.7 %all-gather.9.cloned.1.call-start = ((), (), s32[]{:S(2)}) async-start(), calls=%async_computation.8 | async-start | bytes 1769472 | tf_op jit(solution)/shard_map/all_gather | solution.py:371
  161.5 6.1 %collective-permute-start.2 = (bf16[80,768]{1,0:T(8,128)(2,1)S(1)}, bf16[80,768]{1,0:T(8,128)(2,1)S(1)}, u32[]{:S(2)}, u32[]{:S(2)}) collective-permute-start(bf16[80,768]{1,0:T(8,128)(2,1)S(1)} %get-tuple-element.24), channel_id=1, source_target_pairs={{0,192},{64,0},{128,64},{192,128},{1,193},{65,1},{129,65},{193,129... | collective-permute-start | bytes 368648 | tf_op jit(solution)/shard_map/ppermute | solution.py:339
  165.7 5.3 %collective-permute-start.1 = (bf16[80,768]{1,0:T(8,128)(2,1)S(1)}, bf16[80,768]{1,0:T(8,128)(2,1)S(1)}, u32[]{:S(2)}, u32[]{:S(2)}) collective-permute-start(bf16[80,768]{1,0:T(8,128)(2,1)S(1)} %get-tuple-element.25), channel_id=1, source_target_pairs={{0,128},{64,192},{128,0},{192,64},{1,129},{65,193},{129,1},{193,65... | collective-permute-start | bytes 368648 | tf_op jit(solution)/shard_map/ppermute | solution.py:339
  166.6 7.9 %collective-permute-start = (bf16[80,768]{1,0:T(8,128)(2,1)S(1)}, bf16[80,768]{1,0:T(8,128)(2,1)S(1)}, u32[]{:S(2)}, u32[]{:S(2)}) collective-permute-start(bf16[80,768]{1,0:T(8,128)(2,1)S(1)} %get-tuple-element.26), channel_id=1, source_target_pairs={{0,64},{64,128},{128,192},{192,0},{1,65},{65,129},{129,193},{193,1... | collective-permute-start | bytes 368648 | tf_op jit(solution)/shard_map/ppermute | solution.py:339
  176.2 0.7 copy-start.1
  188.8 19.1 %all-to-all-start.4 = ((f32[32,8,128]{2,1,0:T(8,128)}), f32[32,8,128]{2,1,0:T(8,128)S(1)}, u32[]{:S(2)}, u32[]{:S(2)}) async-start(f32[32,8,128]{2,1,0:T(8,128)} %broadcast_in_dim.5), calls=%async_computation.5 | async-start | bytes 262144 | tf_op jit(solution)/shard_map/all_to_all | solution.py:344
  194.7 70.3 %all-gather.11.cloned.1.call-start = ((), (), s32[]{:S(2)}) async-start(), calls=%async_computation.9 | async-start | bytes 3538944 | tf_op jit(solution)/shard_map/all_gather | solution.py:374
  194.7 7.5 %collective-permute-start.5 = (bf16[2,64,768]{2,1,0:T(8,128)(2,1)S(1)}, bf16[2,64,768]{2,1,0:T(8,128)(2,1)S(1)}, u32[]{:S(2)}, u32[]{:S(2)}) collective-permute-start(bf16[2,64,768]{2,1,0:T(8,128)(2,1)S(1)} %get-tuple-element.20.a0), channel_id=1, source_target_pairs={{0,128},{64,192},{128,0},{192,64},{1,129},{65,193},{129,1},{193,65... | collective-permute-start | bytes 589832 | tf_op jit(solution)/shard_map/ppermute | solution.py:339
  197.5 10.1 %collective-permute-start.4 = (bf16[2,64,768]{2,1,0:T(8,128)(2,1)S(1)}, bf16[2,64,768]{2,1,0:T(8,128)(2,1)S(1)}, u32[]{:S(2)}, u32[]{:S(2)}) collective-permute-start(bf16[2,64,768]{2,1,0:T(8,128)(2,1)S(1)} %get-tuple-element.20.a0), channel_id=1, source_target_pairs={{0,192},{64,0},{128,64},{192,128},{1,193},{65,1},{129,65},{193,129... | collective-permute-start | bytes 589832 | tf_op jit(solution)/shard_map/ppermute | solution.py:339
  198.4 9.5 %collective-permute-start.3 = (bf16[2,64,768]{2,1,0:T(8,128)(2,1)S(1)}, bf16[2,64,768]{2,1,0:T(8,128)(2,1)S(1)}, u32[]{:S(2)}, u32[]{:S(2)}) collective-permute-start(bf16[2,64,768]{2,1,0:T(8,128)(2,1)S(1)} %get-tuple-element.20.a0), channel_id=1, source_target_pairs={{0,64},{64,128},{128,192},{192,0},{1,65},{65,129},{129,193},{193,1... | collective-permute-start | bytes 589832 | tf_op jit(solution)/shard_map/ppermute | solution.py:339
  214.5 1.4 copy-start
  217.4 15.6 %collective-permute-start.7 = (bf16[8,64,768]{2,1,0:T(8,128)(2,1)S(1)}, bf16[8,64,768]{2,1,0:T(8,128)(2,1)S(1)}, u32[]{:S(2)}, u32[]{:S(2)}) collective-permute-start(bf16[8,64,768]{2,1,0:T(8,128)(2,1)S(1)} %get-tuple-element.22.b0), channel_id=1, source_target_pairs={{0,192},{64,0},{128,64},{192,128},{1,193},{65,1},{129,65},{193,129... | collective-permute-start | bytes 2359304 | tf_op jit(solution)/shard_map/ppermute | solution.py:339
  219.8 17.3 %collective-permute-start.6 = (bf16[8,64,768]{2,1,0:T(8,128)(2,1)S(1)}, bf16[8,64,768]{2,1,0:T(8,128)(2,1)S(1)}, u32[]{:S(2)}, u32[]{:S(2)}) collective-permute-start(bf16[8,64,768]{2,1,0:T(8,128)(2,1)S(1)} %get-tuple-element.22.b0), channel_id=1, source_target_pairs={{0,64},{64,128},{128,192},{192,0},{1,65},{65,129},{129,193},{193,1... | collective-permute-start | bytes 2359304 | tf_op jit(solution)/shard_map/ppermute | solution.py:339
  233.7 8.4 %collective-permute-start.9 = (bf16[4,64,768]{2,1,0:T(8,128)(2,1)}, bf16[4,64,768]{2,1,0:T(8,128)(2,1)S(1)}, u32[]{:S(2)}, u32[]{:S(2)}) collective-permute-start(bf16[4,64,768]{2,1,0:T(8,128)(2,1)} %slice.41), channel_id=1, source_target_pairs={{0,192},{64,0},{128,64},{192,128},{1,193},{65,1},{129,65},{193,129... | collective-permute-start | bytes 1179656 | tf_op jit(solution)/shard_map/ppermute | solution.py:339
  237.9 8.4 %collective-permute-start.8 = (bf16[4,64,768]{2,1,0:T(8,128)(2,1)}, bf16[4,64,768]{2,1,0:T(8,128)(2,1)S(1)}, u32[]{:S(2)}, u32[]{:S(2)}) collective-permute-start(bf16[4,64,768]{2,1,0:T(8,128)(2,1)} %slice.40), channel_id=1, source_target_pairs={{0,64},{64,128},{128,192},{192,0},{1,65},{65,129},{129,193},{193,1... | collective-permute-start | bytes 1179656 | tf_op jit(solution)/shard_map/ppermute | solution.py:339
Sparse Core Ops, SparseCore 0:
  9.9 77.8 all-gather.6
  99.4 60.9 reduce-scatter.1
  177.1 37.2 all-gather.8
  217.5 47.3 all-gather.10

commit v7 on v5

--- a/solution.py
+++ b/solution.py
@@ -183,6 +183,62 @@
         ),
         name=name,
     )(at_x, grouped, x)
+
+
+def project_b_kernel(place, grouped_ref, x_ref, *outs):
+    rows = jnp.concatenate(
+        [x_ref[t, :, PART_A:, :].reshape(NZ * PART_B, ROWS) for t in range(8)], axis=1
+    )
+    res = dot(rows, grouped_ref[...], 1, 0).astype(bf16).reshape(NZ, PART_B, COLS)
+    for k, out_ref in enumerate(outs):
+
+        @pl.when(pl.program_id(0) == k)
+        def _(out_ref=out_ref):
+            out_ref[...] = res
+
+
+def project_b(at_x, grouped, x):
+    shape = (NZ, PART_B, COLS)
+    return pl.pallas_call(
+        project_b_kernel,
+        grid_spec=pltpu.PrefetchScalarGridSpec(
+            num_scalar_prefetch=1,
+            grid=(NX,),
+            in_specs=[
+                pl.BlockSpec((LENGTH, COLS), lambda r, place: (0, 0)),
+                pl.BlockSpec(
+                    (8, NZ, ROWS, ROWS), lambda r, place: (0, lax.rem(place[0] + r, NX), 0, 0)
+                ),
+            ],
+            out_specs=[pl.BlockSpec(shape, lambda r, place: (0, 0, 0))] * NX,
+        ),
+        out_shape=[jax.ShapeDtypeStruct(shape, bf16)] * NX,
+        compiler_params=pltpu.CompilerParams(vmem_limit_bytes=60 << 20),
+        cost_estimate=pl.CostEstimate(
+            flops=2 * LENGTH * COLS * WIDTH * PART_B // ROWS,
+            bytes_accessed=12 << 20,
+            transcendentals=0,
+        ),
+        name="project_b",
+    )(at_x, grouped, x)
+
+
+def fold_kernel(p0, p1, p2, p3, out_ref):
+    total = p0[...].astype(f32) + p1[...].astype(f32)
+    out_ref[...] = (total + p2[...].astype(f32) + p3[...].astype(f32)).astype(bf16)
+
+
+def fold(parts):
+    spec = pl.BlockSpec((NZ // 4, PART_B, COLS), lambda z: (z, 0, 0))
+    return pl.pallas_call(
+        fold_kernel,
+        grid=(4,),
+        in_specs=[spec] * NX,
+        out_specs=spec,
+        out_shape=jax.ShapeDtypeStruct((NZ, PART_B, COLS), bf16),
+        cost_estimate=pl.CostEstimate(flops=0, bytes_accessed=3 << 20, transcendentals=0),
+        name="fold",
+    )(*parts)
 
 
 def optimizer_kernel(ga0, ga1, ga2, ga3, gb_ref, w_ref, m_ref, v_ref, m_out, v_out, dir_out, a_out, b_out, sums_out):
@@ -229,30 +285,38 @@
     )(*ga, gb, w, m, v)
 
 
-def apply_kernel(place_ref, sums_ref, a0, a1, a2, a3, b_ref, a_out, b_out):
+def rate_of(sums_ref):
     sums = jnp.sum(sums_ref[...], axis=0)
-    rate = learn_rate * (jnp.sqrt(sums[0:1, 0:1]) / jnp.sqrt(sums[1:2, 0:1]))
+    return learn_rate * (jnp.sqrt(sums[0:1, 0:1]) / jnp.sqrt(sums[1:2, 0:1]))
+
+
+def updated(pair, rate):
+    return (pair[1].astype(f32) - rate * pair[0].astype(f32)).astype(bf16)
+
+
+def apply_a_kernel(place_ref, sums_ref, a0, a1, a2, a3, out_ref):
+    rate = rate_of(sums_ref)
     for k, ref in enumerate((a0, a1, a2, a3)):
-        new = ref[1].astype(f32) - rate * ref[0].astype(f32)
-        a_out[place_ref[k]] = new.astype(bf16)
+        out_ref[place_ref[k]] = updated(ref, rate)
+
+
+def apply_b_kernel(sums_ref, b_ref, out_ref):
+    rate = rate_of(sums_ref)
     for z in range(NZ):
-        new = b_ref[z, 1].astype(f32) - rate * b_ref[z, 0].astype(f32)
-        b_out[z] = new.astype(bf16)
-
-
-def apply_step(place, sums, pieces, gathered):
+        out_ref[z] = updated(b_ref[z], rate)
+
+
+def apply_step(kernel, operands, count, rows, name):
     vmem = pl.BlockSpec(memory_space=pltpu.VMEM)
-    return pl.pallas_call(
-        apply_kernel,
-        in_specs=[pl.BlockSpec(memory_space=pltpu.SMEM)] + [vmem] * 6,
-        out_specs=[vmem, vmem],
-        out_shape=[
-            jax.ShapeDtypeStruct((NX, ROWS_A, COLS), bf16),
-            jax.ShapeDtypeStruct((NZ, ROWS_B, COLS), bf16),
-        ],
+    smem = pl.BlockSpec(memory_space=pltpu.SMEM)
+    return pl.pallas_call(
+        kernel,
+        in_specs=[smem if a.ndim == 1 else vmem for a in operands],
+        out_specs=vmem,
+        out_shape=jax.ShapeDtypeStruct((count, rows, COLS), bf16),
         compiler_params=pltpu.CompilerParams(vmem_limit_bytes=32 << 20),
-        name="apply",
-    )(place, sums, *pieces, gathered)
+        name=name,
+    )(*operands)
 
 
 FULL = (NX, NZ, ROWS, COLS)
@@ -301,23 +365,37 @@
     )(place, own, before, after, far_lo, far_hi)
 
 
-def join_sc_kernel(base_ref, a_ref, out_ref):
-    out_ref[0] = a_ref[:, 0]
+def join_sc_kernel(base_ref, full_ref, out_ref, held, in_sems, out_sems):
+    loads, stores = [], []
+    for x in range(NX):
+        loads.append(pltpu.make_async_copy(full_ref.at[:, x], held.at[x], in_sems.at[x]))
+        stores.append(
+            pltpu.make_async_copy(
+                held.at[x], out_ref.at[x, :, pl.ds(0, ROWS_A), :], out_sems.at[x]
+            )
+        )
+    for load in loads:
+        load.start()
+    for load, store in zip(loads, stores):
+        load.wait()
+        store.start()
+    for store in stores:
+        store.wait()
 
 
 def join_sc(base, full):
     return pl.pallas_call(
         join_sc_kernel,
-        grid=(NX,),
-        in_specs=[
-            pl.BlockSpec(memory_space=pl.ANY),
-            pl.BlockSpec((NZ, 1, ROWS_A, COLS), lambda x: (0, x, 0, 0)),
+        in_specs=[pl.BlockSpec(memory_space=pl.ANY)] * 2,
+        out_specs=pl.BlockSpec(memory_space=pl.ANY),
+        out_shape=jax.ShapeDtypeStruct(FULL, bf16),
+        scratch_shapes=[
+            pltpu.VMEM((NX, NZ, ROWS_A, COLS), bf16),
+            pltpu.SemaphoreType.DMA((NX,)),
+            pltpu.SemaphoreType.DMA((NX,)),
         ],
-        out_specs=pl.BlockSpec((1, NZ, ROWS_A, COLS), lambda x: (x, 0, 0, 0)),
-        out_shape=jax.ShapeDtypeStruct(FULL, bf16),
         input_output_aliases={0: 0},
-        compiler_params=pltpu.CompilerParams(vmem_limit_bytes=60 << 20),
-        cost_estimate=pl.CostEstimate(flops=0, bytes_accessed=4 << 20, transcendentals=0),
+        compiler_params=pltpu.CompilerParams(vmem_limit_bytes=62 << 20),
         name="join_sc",
     )(base, full)
 
@@ -341,10 +419,9 @@
     at_x = lax.axis_index("x")
     place_x = at_x.reshape(1).astype(jnp.int32)
     part_a = project(grouped, x_full, 0, PART_A, place_x, "project_a")
-    part_b = project(grouped, x_full, PART_A, ROWS, None, "project_b")
+    part_b = project_b(place_x, grouped, x_full)
     part_a = lax.psum_scatter(part_a, "z", scatter_dimension=0, tiled=True)[0]
-    part_b = lax.all_to_all(part_b, "x", 0, 0, tiled=True)
-    part_b = jnp.sum(part_b.astype(f32), axis=0).astype(bf16)
+    part_b = fold([part_b[0]] + [shift(part_b[by], "x", NX, by) for by in range(1, NX)])
     part_b = lax.all_to_all(part_b, "z", 0, 0, tiled=True)
     part_a = [part_a[0]] + [shift(part_a[by], "x", NX, by) for by in range(1, NX)]
 
@@ -358,7 +435,8 @@
     )
     gathered_b = lax.all_gather(mine_b, "z", axis=0, tiled=False)
     sums = spread(jnp.sum(spread(sums, ("y", "core"), 8), axis=0), ("x", "z"), 32)
-    new_a, new_b = apply_step(place, sums, pieces, gathered_b)
+    new_a = apply_step(apply_a_kernel, (place, sums, *pieces), NX, ROWS_A, "apply_a")
+    new_b = apply_step(apply_b_kernel, (sums, gathered_b), NZ, ROWS_B, "apply_b")
     full_a = lax.all_gather(new_a, "z", axis=0, tiled=False)
     before, after = shift(new_b, "x", NX, 1), shift(new_b, "x", NX, -1)
     far_lo = shift(before[: NZ // 2], "x", NX, 1)

time: 265 us -> 261 us (0.985)
  blocking collectives: 44.9 us -> 10.5 us
  waiting for transfers between devices: 112 us -> 137 us
  starting transfers between devices: 33.1 us -> 39.3 us
  Pallas kernels: 45.9 us -> 49.1 us
  other arithmetic: 4.99 us -> 1.89 us
    all_to_all x1 -> x0, blocking collectives: 32.7 us -> none  [body(): part_b = lax.all_to_all(part_b, 'x', 0, 0, tiled=True)]
    ppermute x10 -> x13, waiting for transfers between devices: 26.7 us -> 51.9 us  [shift(): lax.ppermute(value, axis, [(i, (i + by) % size) for i in range(size)])]
    pallas_call x2 -> x5, Pallas kernels: 5.67 us -> 16.1 us  [the longest x1 7.79 us: project_b(): pl.pallas_call(project_b_kernel, grid_spec=pltpu.PrefetchScalarGridSpec(n...]
    pallas_call x2 -> x1, Pallas kernels: 16 us -> 8.7 us  [project(): pl.pallas_call(kernel, grid_spec=pltpu.PrefetchScalarGridSpec(num_scalar_...]
    ppermute x10 -> x13, starting transfers between devices: 14 us -> 18.1 us  [shift(): lax.ppermute(value, axis, [(i, (i + by) % size) for i in range(size)])]
    reduce_sum x1 -> x0, other arithmetic: 3.09 us -> none  [body(): part_b = jnp.sum(part_b.astype(f32), axis=0).astype(bf16)]
  transfers between devices with their start and end apart: 17 -> 20, of which waited for: 12 -> 16; matrix products, arithmetic and copies ran while one was open for 3% -> 2% of each run, Pallas kernels for 10% -> 13%
where the time goes in v7:
time: 261 us
  waiting for transfers between devices  137 us (52%)
  Pallas kernels  49.1 us (19%)
  starting transfers between devices  39.3 us (15%)
  between operations  15.3 us (6%)
  blocking collectives  10.5 us (4%)
  local copies, waits for them, and re-layouts  8.17 us (3%)
    all_to_all x1, waiting for transfers between devices, body(): lax.all_to_all(packed, ('y', 'core'), 0, 0, tiled=True)  52 us
    ppermute x13, waiting for transfers between devices, shift(): lax.ppermute(value, axis, [(i, (i + by) % size) for i in range(size)])  51.9 us
    ppermute x13, starting transfers between devices, shift(): lax.ppermute(value, axis, [(i, (i + by) % size) for i in range(size)])  18.1 us
    all_gather x1, waiting for transfers between devices, body(): full_a = lax.all_gather(new_a, 'z', axis=0, tiled=False)  14.4 us
    pallas_call x1, Pallas kernels, attention(): pl.pallas_call(attention_kernel, grid=(GROUP,), in_specs=[pl.BlockSpec((L...  13.5 us
    all_to_all x1, blocking collectives, spread(): return lax.all_to_all(wide, axes, 0, 0, tiled=True)  10.5 us
    pallas_call x1, Pallas kernels, project(): pl.pallas_call(kernel, grid_spec=pltpu.PrefetchScalarGridSpec(num_scalar_...  8.7 us
    pallas_call x1, Pallas kernels, project_b(): pl.pallas_call(project_b_kernel, grid_spec=pltpu.PrefetchScalarGridSpec(n...  7.79 us
  transfers between devices with their start and end apart: 20, of which 16 were waited for; matrix products, arithmetic and copies ran while one was open for 2% of the time, Pallas kernels for 13%

profile of v7, /device:TPU:1, one launch (start us, length us, event | category | flops | bytes accessed | tf_op | source)
XLA Modules:
  0.0 260.8 jit_solution(507129507449331238)
XLA Ops:
  7.2 2.2 turn.1
  9.5 2.9 %pack.1 = bf16[8,128,1280]{2,1,0:T(8,128)(2,1)} custom-call(bf16[128,4096]{1,0:T(8,128)(2,1)} %bitcast.32, bf16[128,1024]{1,0:T(8,128)(2,1)} %bitcast.35, bf16[128,1024]{1,0:T(8,128)(2,1)} %bitcast.36, bf16[128,4096]{1,0:T(8,128)(2,1)} %bitcast.33), custom_call_target="tpu_custom_call" | custom-call | bytes 5242880 | tf_op jit(solution)/shard_map/pack/pallas_call | solution.py:52
  12.4 6.8 %all-to-all-start = ((bf16[8,128,1280]{2,1,0:T(8,128)(2,1)}), bf16[8,128,1280]{2,1,0:T(8,128)(2,1)S(1)}, u32[]{:S(2)}, u32[]{:S(2)}) async-start(bf16[8,128,1280]{2,1,0:T(8,128)(2,1)} %pack.1), calls=%async_computation | async-start | bytes 5242880 | tf_op jit(solution)/shard_map/all_to_all | solution.py:415
  19.2 52.0 %all-to-all-done = bf16[8,128,1280]{2,1,0:T(8,128)(2,1)S(1)} async-done(((bf16[8,128,1280]{2,1,0:T(8,128)(2,1)}), bf16[8,128,1280]{2,1,0:T(8,128)(2,1)S(1)}, u32[]{:S(2)}, u32[]{:S(2)}) %all-to-all-start) | async-done | bytes 2621472 | tf_op jit(solution)/shard_map/all_to_all | solution.py:415
  71.2 13.5 %attention_backward.1.grouped_ref = bf16[1024,768]{1,0:T(8,128)(2,1)S(1)} custom-call(bf16[1024,1280]{1,0:T(8,128)(2,1)S(1)} %bitcast.23, bf16[1024,1280]{1,0:T(8,128)(2,1)S(1)} %bitcast.24, bf16[1024,1280]{1,0:T(8,128)(2,1)S(1)} %bitcast.25, bf16[1024,1280]{1,0:T(8,128)(2,1)S(1)} %bitcast.26), custom_call_target="tpu_custom_call" | custom-call | flops 4294967296 | bytes 5242880 | tf_op jit(solution)/shard_map/attention_backward/pallas_call | solution.py:125
  87.1 8.7 %project_a.1 = bf16[8,4,80,768]{3,2,1,0:T(8,128)(2,1)} custom-call(s32[1]{0:T(128)} %bitcast.place, bf16[1024,768]{1,0:T(8,128)(2,1)} %copy-done, bf16[8,32,128,128]{3,2,1,0:T(8,128)(2,1)} %bitcast.29), custom_call_target="tpu_custom_call" | custom-call | flops 4026531840 | bytes 12582912 | tf_op jit(solution)/shard_map/project_a/pallas_call | solution.py:166
  95.8 7.8 %project_b.1 = (bf16[8,48,768]{2,1,0:T(8,128)(2,1)}, bf16[8,48,768]{2,1,0:T(8,128)(2,1)}, bf16[8,48,768]{2,1,0:T(8,128)(2,1)}, bf16[8,48,768]{2,1,0:T(8,128)(2,1)}) custom-call(s32[1]{0:T(128)} %bitcast.place, bf16[1024,768]{1,0:T(8,128)(2,1)} %copy-done, bf16[8,32,128,128]{3,2,1,0:T(8,128)(2,1)} %bitcast.30), custom_call_target="tpu_custom_call" | custom-call | flops 2415919104 | bytes 12582912 | tf_op jit(solution)/shard_map/project_b/pallas_call | solution.py:202
  104.0 2.4 collective-permute-start.4
  107.6 11.8 %collective-permute-done.3.p1 = bf16[8,48,768]{2,1,0:T(8,128)(2,1)S(1)} collective-permute-done((bf16[8,48,768]{2,1,0:T(8,128)(2,1)}, bf16[8,48,768]{2,1,0:T(8,128)(2,1)S(1)}, u32[]{:S(2)}, u32[]{:S(2)}) %collective-permute-start.3) | collective-permute-done | bytes 589856 | tf_op jit(solution)/shard_map/ppermute | solution.py:404
  119.4 13.1 %collective-permute-done.4.p2 = bf16[8,48,768]{2,1,0:T(8,128)(2,1)S(1)} collective-permute-done((bf16[8,48,768]{2,1,0:T(8,128)(2,1)}, bf16[8,48,768]{2,1,0:T(8,128)(2,1)S(1)}, u32[]{:S(2)}, u32[]{:S(2)}) %collective-permute-start.4) | collective-permute-done | bytes 589856 | tf_op jit(solution)/shard_map/ppermute | solution.py:404
  133.6 3.7 %fold.1 = bf16[8,48,768]{2,1,0:T(8,128)(2,1)} custom-call(bf16[8,48,768]{2,1,0:T(8,128)(2,1)} %get-tuple-element.14.p0, bf16[8,48,768]{2,1,0:T(8,128)(2,1)} %copy-done.6, bf16[8,48,768]{2,1,0:T(8,128)(2,1)} %copy-done.7, bf16[8,48,768]{2,1,0:T(8,128)(2,1)} %copy-done.8), custom_call_target="tpu_custom_call" | custom-call | bytes 3145728 | tf_op jit(solution)/shard_map/fold/pallas_call | solution.py:233
  137.3 7.2 %all-to-all-start.1 = ((bf16[8,48,768]{2,1,0:T(8,128)(2,1)}), bf16[8,48,768]{2,1,0:T(8,128)(2,1)S(1)}, u32[]{:S(2)}, u32[]{:S(2)}) async-start(bf16[8,48,768]{2,1,0:T(8,128)(2,1)} %fold.1), calls=%async_computation.2 | async-start | bytes 1179648 | tf_op jit(solution)/shard_map/all_to_all | solution.py:425
  144.5 4.5 %reduce-scatter.2.cloned.1.call-done = bf16[1,4,80,768]{3,2,1,0:T(8,128)(2,1)} async-done(((bf16[8,4,80,768]{3,2,1,0:T(8,128)(2,1)}), bf16[1,4,80,768]{3,2,1,0:T(8,128)(2,1)}) %reduce-scatter.2.cloned.1.call-update) | async-done | bytes 491536 | tf_op jit(solution)/shard_map/reduce_scatter | solution.py:423
  150.1 2.5 collective-permute-start.2
  153.8 7.6 %all-to-all-done.1.gb_ref = bf16[8,48,768]{2,1,0:T(8,128)(2,1)S(1)} async-done(((bf16[8,48,768]{2,1,0:T(8,128)(2,1)}), bf16[8,48,768]{2,1,0:T(8,128)(2,1)S(1)}, u32[]{:S(2)}, u32[]{:S(2)}) %all-to-all-start.1) | async-done | bytes 589856 | tf_op jit(solution)/shard_map/all_to_all | solution.py:425
  161.7 1.7 optimizer.1
  164.2 10.5 %all_to_all.20 = f32[8,8,128]{2,1,0:T(8,128)S(1)} all-to-all(f32[8,8,128]{2,1,0:T(8,128)S(1)} %broadcast_in_dim.4), channel_id=1, replica_groups=mesh['x'=4,'z'=8,'y'=4,'core'=2] {'y','core'}, dimensions={0} | all-to-all | bytes 65536 | tf_op jit(solution)/shard_map/all_to_all | solution.py:409
  175.4 7.2 %all-to-all-start.3 = ((f32[32,8,128]{2,1,0:T(8,128)}), f32[32,8,128]{2,1,0:T(8,128)S(1)}, u32[]{:S(2)}, u32[]{:S(2)}) async-start(f32[32,8,128]{2,1,0:T(8,128)} %broadcast_in_dim.5), calls=%async_computation.4 | async-start | bytes 262144 | tf_op jit(solution)/shard_map/all_to_all | solution.py:409
  182.6 3.0 %collective-permute-start.12 = (bf16[2,64,768]{2,1,0:T(8,128)(2,1)S(1)}, bf16[2,64,768]{2,1,0:T(8,128)(2,1)S(1)}, u32[]{:S(2)}, u32[]{:S(2)}) collective-permute-start(bf16[2,64,768]{2,1,0:T(8,128)(2,1)S(1)} %get-tuple-element.23.a0), channel_id=1, source_target_pairs={{0,128},{64,192},{128,0},{192,64},{1,129},{65,193},{129,1},{193,65... | collective-permute-start | bytes 589832 | tf_op jit(solution)/shard_map/ppermute | solution.py:404
  187.1 3.4 %collective-permute-done.12.a3 = bf16[2,64,768]{2,1,0:T(8,128)(2,1)S(1)} collective-permute-done((bf16[2,64,768]{2,1,0:T(8,128)(2,1)S(1)}, bf16[2,64,768]{2,1,0:T(8,128)(2,1)S(1)}, u32[]{:S(2)}, u32[]{:S(2)}) %collective-permute-start.12) | collective-permute-done | bytes 196640 | tf_op jit(solution)/shard_map/ppermute | solution.py:404
  190.5 5.1 %collective-permute-done.11.a2 = bf16[2,64,768]{2,1,0:T(8,128)(2,1)S(1)} collective-permute-done((bf16[2,64,768]{2,1,0:T(8,128)(2,1)S(1)}, bf16[2,64,768]{2,1,0:T(8,128)(2,1)S(1)}, u32[]{:S(2)}, u32[]{:S(2)}) %collective-permute-start.11) | collective-permute-done | bytes 196640 | tf_op jit(solution)/shard_map/ppermute | solution.py:404
  196.0 1.5 apply_a.1
  197.5 4.9 %all-gather.9.cloned.1.call-done = bf16[16,64,768]{2,1,0:T(8,128)(2,1)} async-done(((bf16[2,64,768]{2,1,0:T(8,128)(2,1)}), bf16[16,64,768]{2,1,0:T(8,128)(2,1)}) %all-gather.9.cloned.1.call-update) | async-done | bytes 1572880 | tf_op jit(solution)/shard_map/all_gather | solution.py:436
  202.3 1.4 copy-done.1
  204.1 2.5 collective-permute-start.7
  206.5 13.2 %collective-permute-done.7.b2 = bf16[8,64,768]{2,1,0:T(8,128)(2,1)S(1)} collective-permute-done((bf16[8,64,768]{2,1,0:T(8,128)(2,1)S(1)}, bf16[8,64,768]{2,1,0:T(8,128)(2,1)S(1)}, u32[]{:S(2)}, u32[]{:S(2)}) %collective-permute-start.7) | collective-permute-done | bytes 786464 | tf_op jit(solution)/shard_map/ppermute | solution.py:404
  220.5 3.4 %collective-permute-start.9 = (bf16[4,64,768]{2,1,0:T(8,128)(2,1)}, bf16[4,64,768]{2,1,0:T(8,128)(2,1)S(1)}, u32[]{:S(2)}, u32[]{:S(2)}) collective-permute-start(bf16[4,64,768]{2,1,0:T(8,128)(2,1)} %slice.41), channel_id=1, source_target_pairs={{0,192},{64,0},{128,64},{192,128},{1,193},{65,1},{129,65},{193,129... | collective-permute-start | bytes 1179656 | tf_op jit(solution)/shard_map/ppermute | solution.py:404
  226.7 1.8 broadcast_multiply_fusion
  228.9 4.2 %collective-permute-done.8.b3 = bf16[4,64,768]{2,1,0:T(8,128)(2,1)S(1)} collective-permute-done((bf16[4,64,768]{2,1,0:T(8,128)(2,1)}, bf16[4,64,768]{2,1,0:T(8,128)(2,1)S(1)}, u32[]{:S(2)}, u32[]{:S(2)}) %collective-permute-start.8) | collective-permute-done | bytes 393248 | tf_op jit(solution)/shard_map/ppermute | solution.py:404
  233.1 3.9 %join_x.1.base_ref = bf16[4,8,128,768]{3,2,1,0:T(8,128)(2,1)} custom-call(s32[4]{0:T(128)S(1)} %pad_add_fusion.place_ref, bf16[8,64,768]{2,1,0:T(8,128)(2,1)S(1)} %apply_b.1.b0, bf16[8,64,768]{2,1,0:T(8,128)(2,1)S(1)} %collective-permute-done.6.b1, bf16[8,64,768]{2,1,0:T(8,128)(2,1)S(1)} %collective-permute-done.7.b2, ...), custom_call_target="tpu_custom_call" | custom-call | bytes 7340032 | tf_op jit(solution)/shard_map/join_x/pallas_call | solution.py:350
  237.0 14.4 %all-gather.11.cloned.1.call-done = bf16[32,64,768]{2,1,0:T(8,128)(2,1)} async-done(((bf16[4,64,768]{2,1,0:T(8,128)(2,1)}), bf16[32,64,768]{2,1,0:T(8,128)(2,1)}) %all-gather.11.cloned.1.call-update) | async-done | bytes 3145744 | tf_op jit(solution)/shard_map/all_gather | solution.py:440
  251.4 2.9 %join_sc.1 = bf16[4,8,128,768]{3,2,1,0:T(8,128)(2,1)} custom-call(bf16[4,8,128,768]{3,2,1,0:T(8,128)(2,1)} %join_x.1.base_ref, bf16[8,4,64,768]{3,2,1,0:T(8,128)(2,1)} %bitcast.31), custom_call_target="tpu_custom_call", output_to_operand_aliasing={{}: (0, {})} | custom-call | tf_op jit(solution)/shard_map/join_sc/pallas_call | solution.py:387
  (52 shorter events, 14.1 us)
Async XLA Ops:
  7.2 79.9 %all-gather.7.cloned.1.call-start = ((), (), s32[]{:S(2)}) async-start(), calls=%async_computation.6 | async-start | bytes 9437184 | tf_op jit(solution)/shard_map/all_gather | solution.py:416
  12.4 58.8 %all-to-all-start = ((bf16[8,128,1280]{2,1,0:T(8,128)(2,1)}), bf16[8,128,1280]{2,1,0:T(8,128)(2,1)S(1)}, u32[]{:S(2)}, u32[]{:S(2)}) async-start(bf16[8,128,1280]{2,1,0:T(8,128)(2,1)} %pack.1), calls=%async_computation | async-start | bytes 5242880 | tf_op jit(solution)/shard_map/all_to_all | solution.py:415
  19.2 129.8 %reduce-scatter.2.cloned.1.call-start = ((), (), s32[]{:S(2)}) async-start(), calls=%async_computation.5 | async-start | bytes 4423680 | tf_op jit(solution)/shard_map/reduce_scatter | solution.py:423
  84.7 1.2 copy-start
  103.6 58.2 %copy-start.3 = (f32[128,768]{1,0:T(8,128)S(1)}, f32[128,768]{1,0:T(8,128)}, u32[]{:S(2)}) copy-start(f32[128,768]{1,0:T(8,128)} %w_ref.1) | copy-start | bytes 1179652
  103.6 58.2 %copy-start.4 = (f32[128,768]{1,0:T(8,128)S(1)}, f32[128,768]{1,0:T(8,128)}, u32[]{:S(2)}) copy-start(f32[128,768]{1,0:T(8,128)} %m_ref.1) | copy-start | bytes 1179652
  103.6 58.2 %copy-start.5 = (f32[128,768]{1,0:T(8,128)S(1)}, f32[128,768]{1,0:T(8,128)}, u32[]{:S(2)}) copy-start(f32[128,768]{1,0:T(8,128)} %v_ref.1) | copy-start | bytes 1179652
  103.6 15.8 %collective-permute-start.3 = (bf16[8,48,768]{2,1,0:T(8,128)(2,1)}, bf16[8,48,768]{2,1,0:T(8,128)(2,1)S(1)}, u32[]{:S(2)}, u32[]{:S(2)}) collective-permute-start(bf16[8,48,768]{2,1,0:T(8,128)(2,1)} %get-tuple-element.15), channel_id=1, source_target_pairs={{0,64},{64,128},{128,192},{192,0},{1,65},{65,129},{129,193},{193,1... | collective-permute-start | bytes 1769480 | tf_op jit(solution)/shard_map/ppermute | solution.py:404
  104.0 28.5 %collective-permute-start.4 = (bf16[8,48,768]{2,1,0:T(8,128)(2,1)}, bf16[8,48,768]{2,1,0:T(8,128)(2,1)S(1)}, u32[]{:S(2)}, u32[]{:S(2)}) collective-permute-start(bf16[8,48,768]{2,1,0:T(8,128)(2,1)} %get-tuple-element.16), channel_id=1, source_target_pairs={{0,128},{64,192},{128,0},{192,64},{1,129},{65,193},{129,1},{193,65... | collective-permute-start | bytes 1769480 | tf_op jit(solution)/shard_map/ppermute | solution.py:404
  106.5 26.1 %collective-permute-start.5 = (bf16[8,48,768]{2,1,0:T(8,128)(2,1)}, bf16[8,48,768]{2,1,0:T(8,128)(2,1)S(1)}, u32[]{:S(2)}, u32[]{:S(2)}) collective-permute-start(bf16[8,48,768]{2,1,0:T(8,128)(2,1)} %get-tuple-element.17), channel_id=1, source_target_pairs={{0,192},{64,0},{128,64},{192,128},{1,193},{65,1},{129,65},{193,129... | collective-permute-start | bytes 1769480 | tf_op jit(solution)/shard_map/ppermute | solution.py:404
  119.4 13.2 %copy-start.6 = (bf16[8,48,768]{2,1,0:T(8,128)(2,1)}, bf16[8,48,768]{2,1,0:T(8,128)(2,1)S(1)}, u32[]{:S(2)}) copy-start(bf16[8,48,768]{2,1,0:T(8,128)(2,1)S(1)} %collective-permute-done.3.p1) | copy-start | bytes 1769476
  132.5 0.8 copy-start.7
  132.6 0.9 copy-start.8
  137.3 24.2 %all-to-all-start.1 = ((bf16[8,48,768]{2,1,0:T(8,128)(2,1)}), bf16[8,48,768]{2,1,0:T(8,128)(2,1)S(1)}, u32[]{:S(2)}, u32[]{:S(2)}) async-start(bf16[8,48,768]{2,1,0:T(8,128)(2,1)} %fold.1), calls=%async_computation.2 | async-start | bytes 1179648 | tf_op jit(solution)/shard_map/all_to_all | solution.py:425
  144.5 57.9 %all-gather.9.cloned.1.call-start = ((), (), s32[]{:S(2)}) async-start(), calls=%async_computation.7 | async-start | bytes 1769472 | tf_op jit(solution)/shard_map/all_gather | solution.py:436
  150.1 11.3 %collective-permute-start.2 = (bf16[80,768]{1,0:T(8,128)(2,1)S(1)}, bf16[80,768]{1,0:T(8,128)(2,1)S(1)}, u32[]{:S(2)}, u32[]{:S(2)}) collective-permute-start(bf16[80,768]{1,0:T(8,128)(2,1)S(1)} %get-tuple-element.24), channel_id=1, source_target_pairs={{0,192},{64,0},{128,64},{192,128},{1,193},{65,1},{129,65},{193,129... | collective-permute-start | bytes 368648 | tf_op jit(solution)/shard_map/ppermute | solution.py:404
  152.6 8.8 %collective-permute-start.1 = (bf16[80,768]{1,0:T(8,128)(2,1)S(1)}, bf16[80,768]{1,0:T(8,128)(2,1)S(1)}, u32[]{:S(2)}, u32[]{:S(2)}) collective-permute-start(bf16[80,768]{1,0:T(8,128)(2,1)S(1)} %get-tuple-element.25), channel_id=1, source_target_pairs={{0,128},{64,192},{128,0},{192,64},{1,129},{65,193},{129,1},{193,65... | collective-permute-start | bytes 368648 | tf_op jit(solution)/shard_map/ppermute | solution.py:404
  153.2 8.6 %collective-permute-start = (bf16[80,768]{1,0:T(8,128)(2,1)S(1)}, bf16[80,768]{1,0:T(8,128)(2,1)S(1)}, u32[]{:S(2)}, u32[]{:S(2)}) collective-permute-start(bf16[80,768]{1,0:T(8,128)(2,1)S(1)} %get-tuple-element.26), channel_id=1, source_target_pairs={{0,64},{64,128},{128,192},{192,0},{1,65},{65,129},{129,193},{193,1... | collective-permute-start | bytes 368648 | tf_op jit(solution)/shard_map/ppermute | solution.py:404
  163.4 0.7 copy-start.2
  175.4 20.6 %all-to-all-start.3 = ((f32[32,8,128]{2,1,0:T(8,128)}), f32[32,8,128]{2,1,0:T(8,128)S(1)}, u32[]{:S(2)}, u32[]{:S(2)}) async-start(f32[32,8,128]{2,1,0:T(8,128)} %broadcast_in_dim.5), calls=%async_computation.4 | async-start | bytes 262144 | tf_op jit(solution)/shard_map/all_to_all | solution.py:409
  182.5 68.8 %all-gather.11.cloned.1.call-start = ((), (), s32[]{:S(2)}) async-start(), calls=%async_computation.8 | async-start | bytes 3538944 | tf_op jit(solution)/shard_map/all_gather | solution.py:440
  182.6 8.0 %collective-permute-start.12 = (bf16[2,64,768]{2,1,0:T(8,128)(2,1)S(1)}, bf16[2,64,768]{2,1,0:T(8,128)(2,1)S(1)}, u32[]{:S(2)}, u32[]{:S(2)}) collective-permute-start(bf16[2,64,768]{2,1,0:T(8,128)(2,1)S(1)} %get-tuple-element.23.a0), channel_id=1, source_target_pairs={{0,128},{64,192},{128,0},{192,64},{1,129},{65,193},{129,1},{193,65... | collective-permute-start | bytes 589832 | tf_op jit(solution)/shard_map/ppermute | solution.py:404
  185.6 10.0 %collective-permute-start.11 = (bf16[2,64,768]{2,1,0:T(8,128)(2,1)S(1)}, bf16[2,64,768]{2,1,0:T(8,128)(2,1)S(1)}, u32[]{:S(2)}, u32[]{:S(2)}) collective-permute-start(bf16[2,64,768]{2,1,0:T(8,128)(2,1)S(1)} %get-tuple-element.23.a0), channel_id=1, source_target_pairs={{0,192},{64,0},{128,64},{192,128},{1,193},{65,1},{129,65},{193,129... | collective-permute-start | bytes 589832 | tf_op jit(solution)/shard_map/ppermute | solution.py:404
  186.5 9.5 %collective-permute-start.10 = (bf16[2,64,768]{2,1,0:T(8,128)(2,1)S(1)}, bf16[2,64,768]{2,1,0:T(8,128)(2,1)S(1)}, u32[]{:S(2)}, u32[]{:S(2)}) collective-permute-start(bf16[2,64,768]{2,1,0:T(8,128)(2,1)S(1)} %get-tuple-element.23.a0), channel_id=1, source_target_pairs={{0,64},{64,128},{128,192},{192,0},{1,65},{65,129},{129,193},{193,1... | collective-permute-start | bytes 589832 | tf_op jit(solution)/shard_map/ppermute | solution.py:404
  202.3 1.4 copy-start.1
  204.1 15.6 %collective-permute-start.7 = (bf16[8,64,768]{2,1,0:T(8,128)(2,1)S(1)}, bf16[8,64,768]{2,1,0:T(8,128)(2,1)S(1)}, u32[]{:S(2)}, u32[]{:S(2)}) collective-permute-start(bf16[8,64,768]{2,1,0:T(8,128)(2,1)S(1)} %apply_b.1.b0), channel_id=1, source_target_pairs={{0,192},{64,0},{128,64},{192,128},{1,193},{65,1},{129,65},{193,129... | collective-permute-start | bytes 2359304 | tf_op jit(solution)/shard_map/ppermute | solution.py:404
  206.5 17.4 %collective-permute-start.6 = (bf16[8,64,768]{2,1,0:T(8,128)(2,1)S(1)}, bf16[8,64,768]{2,1,0:T(8,128)(2,1)S(1)}, u32[]{:S(2)}, u32[]{:S(2)}) collective-permute-start(bf16[8,64,768]{2,1,0:T(8,128)(2,1)S(1)} %apply_b.1.b0), channel_id=1, source_target_pairs={{0,64},{64,128},{128,192},{192,0},{1,65},{65,129},{129,193},{193,1... | collective-permute-start | bytes 2359304 | tf_op jit(solution)/shard_map/ppermute | solution.py:404
  220.5 8.4 %collective-permute-start.9 = (bf16[4,64,768]{2,1,0:T(8,128)(2,1)}, bf16[4,64,768]{2,1,0:T(8,128)(2,1)S(1)}, u32[]{:S(2)}, u32[]{:S(2)}) collective-permute-start(bf16[4,64,768]{2,1,0:T(8,128)(2,1)} %slice.41), channel_id=1, source_target_pairs={{0,192},{64,0},{128,64},{192,128},{1,193},{65,1},{129,65},{193,129... | collective-permute-start | bytes 1179656 | tf_op jit(solution)/shard_map/ppermute | solution.py:404
  224.7 8.4 %collective-permute-start.8 = (bf16[4,64,768]{2,1,0:T(8,128)(2,1)}, bf16[4,64,768]{2,1,0:T(8,128)(2,1)S(1)}, u32[]{:S(2)}, u32[]{:S(2)}) collective-permute-start(bf16[4,64,768]{2,1,0:T(8,128)(2,1)} %slice.40), channel_id=1, source_target_pairs={{0,64},{64,128},{128,192},{192,0},{1,65},{65,129},{129,193},{193,1... | collective-permute-start | bytes 1179656 | tf_op jit(solution)/shard_map/ppermute | solution.py:404
Sparse Core Ops, SparseCore 0:
  9.9 77.1 all-gather.6
  95.9 53.0 reduce-scatter.1
  164.3 37.9 all-gather.8
  204.0 47.3 all-gather.10

commit v8 on v7

--- a/solution.py
+++ b/solution.py
@@ -18,7 +18,7 @@
 BLOCK = 256
 PART_A = 80
 PART_B = ROWS - PART_A
-ROWS_A = 64
+ROWS_A = 48
 ROWS_B = ROWS - ROWS_A
 
 beta_first = 0.9
@@ -258,10 +258,10 @@
     m_out[...] = first_new
     v_out[...] = second_new
     dir_out[...] = direction
-    a_out[0] = direction[:ROWS_A].astype(bf16)
-    a_out[1] = weight[:ROWS_A].astype(bf16)
-    b_out[0] = direction[ROWS_A:].astype(bf16)
-    b_out[1] = weight[ROWS_A:].astype(bf16)
+    a_out[0] = direction[ROWS_B:].astype(bf16)
+    a_out[1] = weight[ROWS_B:].astype(bf16)
+    b_out[0] = direction[:ROWS_B].astype(bf16)
+    b_out[1] = weight[:ROWS_B].astype(bf16)
     weight_sq = jnp.sum(weight * weight)
     update_sq = jnp.sum(direction * direction)
     row = lax.broadcasted_iota(jnp.int32, (8, 128), 0)
@@ -355,7 +355,7 @@
             in_specs=[b_spec(0), b_spec(1), b_spec(2), whole, whole],
             out_specs=pl.BlockSpec(
                 (1, half, ROWS_B, COLS),
-                lambda o, h, place: (place[o], h, ROWS_A // ROWS_B, 0),
+                lambda o, h, place: (place[o], h, 0, 0),
             ),
         ),
         out_shape=jax.ShapeDtypeStruct(FULL, bf16),
@@ -371,7 +371,7 @@
         loads.append(pltpu.make_async_copy(full_ref.at[:, x], held.at[x], in_sems.at[x]))
         stores.append(
             pltpu.make_async_copy(
-                held.at[x], out_ref.at[x, :, pl.ds(0, ROWS_A), :], out_sems.at[x]
+                held.at[x], out_ref.at[x, :, pl.ds(ROWS_B, ROWS_A), :], out_sems.at[x]
             )
         )
     for load in loads:

time: 261 us -> 258 us (0.989); the launches traced: 261 us -> 255 us
  waiting for transfers between devices: 137 us -> 130 us
    all_gather x1, waiting for transfers between devices: 14.4 us -> 3.52 us  [body(): full_a = lax.all_gather(new_a, 'z', axis=0, tiled=False)]
    all_gather x1, waiting for transfers between devices: 4.86 us -> 8.67 us  [body(): gathered_b = lax.all_gather(mine_b, 'z', axis=0, tiled=False)]
  transfers between devices with their start and end apart: 20 -> 20, of which waited for: 16 -> 13; matrix products, arithmetic and copies ran while one was open for 2% -> 2% of each run, Pallas kernels for 13% -> 14%
where the time goes in v8:
time: 258 us; the launch traced here: 255 us
  waiting for transfers between devices  130 us (50%)
  Pallas kernels  50.3 us (19%)
  starting transfers between devices  40.5 us (16%)
  between operations  15.3 us (6%)
  blocking collectives  10.7 us (4%)
  local copies, waits for them, and re-layouts  7.67 us (3%)
    ppermute x13, waiting for transfers between devices, shift(): lax.ppermute(value, axis, [(i, (i + by) % size) for i in range(size)])  53.4 us
    all_to_all x1, waiting for transfers between devices, body(): lax.all_to_all(packed, ('y', 'core'), 0, 0, tiled=True)  52 us
    ppermute x13, starting transfers between devices, shift(): lax.ppermute(value, axis, [(i, (i + by) % size) for i in range(size)])  18.9 us
    pallas_call x1, Pallas kernels, attention(): pl.pallas_call(attention_kernel, grid=(GROUP,), in_specs=[pl.BlockSpec((L...  13.5 us
    all_to_all x1, blocking collectives, spread(): return lax.all_to_all(wide, axes, 0, 0, tiled=True)  10.7 us
    pallas_call x1, Pallas kernels, project(): pl.pallas_call(kernel, grid_spec=pltpu.PrefetchScalarGridSpec(num_scalar_...  8.7 us
    all_gather x1, waiting for transfers between devices, body(): gathered_b = lax.all_gather(mine_b, 'z', axis=0, tiled=False)  8.67 us
    pallas_call x1, Pallas kernels, project_b(): pl.pallas_call(project_b_kernel, grid_spec=pltpu.PrefetchScalarGridSpec(n...  7.81 us
  transfers between devices with their start and end apart: 20, of which 13 were waited for; matrix products, arithmetic and copies ran while one was open for 2% of the time, Pallas kernels for 14%

profile of v8, /device:TPU:1, one launch (start us, length us, event | category | flops | bytes accessed | tf_op | source)
XLA Modules:
  0.0 255.1 jit_solution(16451812217540212279)
XLA Ops:
  7.2 2.3 turn.1
  9.5 2.9 %pack.1 = bf16[8,128,1280]{2,1,0:T(8,128)(2,1)} custom-call(bf16[128,4096]{1,0:T(8,128)(2,1)} %bitcast.32, bf16[128,1024]{1,0:T(8,128)(2,1)} %bitcast.35, bf16[128,1024]{1,0:T(8,128)(2,1)} %bitcast.36, bf16[128,4096]{1,0:T(8,128)(2,1)} %bitcast.33), custom_call_target="tpu_custom_call" | custom-call | bytes 5242880 | tf_op jit(solution)/shard_map/pack/pallas_call | solution.py:52
  12.4 6.8 %all-to-all-start = ((bf16[8,128,1280]{2,1,0:T(8,128)(2,1)}), bf16[8,128,1280]{2,1,0:T(8,128)(2,1)S(1)}, u32[]{:S(2)}, u32[]{:S(2)}) async-start(bf16[8,128,1280]{2,1,0:T(8,128)(2,1)} %pack.1), calls=%async_computation | async-start | bytes 5242880 | tf_op jit(solution)/shard_map/all_to_all | solution.py:415
  19.2 52.0 %all-to-all-done = bf16[8,128,1280]{2,1,0:T(8,128)(2,1)S(1)} async-done(((bf16[8,128,1280]{2,1,0:T(8,128)(2,1)}), bf16[8,128,1280]{2,1,0:T(8,128)(2,1)S(1)}, u32[]{:S(2)}, u32[]{:S(2)}) %all-to-all-start) | async-done | bytes 2621472 | tf_op jit(solution)/shard_map/all_to_all | solution.py:415
  71.2 13.5 %attention_backward.1.grouped_ref = bf16[1024,768]{1,0:T(8,128)(2,1)S(1)} custom-call(bf16[1024,1280]{1,0:T(8,128)(2,1)S(1)} %bitcast.23, bf16[1024,1280]{1,0:T(8,128)(2,1)S(1)} %bitcast.24, bf16[1024,1280]{1,0:T(8,128)(2,1)S(1)} %bitcast.25, bf16[1024,1280]{1,0:T(8,128)(2,1)S(1)} %bitcast.26), custom_call_target="tpu_custom_call" | custom-call | flops 4294967296 | bytes 5242880 | tf_op jit(solution)/shard_map/attention_backward/pallas_call | solution.py:125
  87.1 8.7 %project_a.1 = bf16[8,4,80,768]{3,2,1,0:T(8,128)(2,1)} custom-call(s32[1]{0:T(128)} %bitcast.place, bf16[1024,768]{1,0:T(8,128)(2,1)} %copy-done.1, bf16[8,32,128,128]{3,2,1,0:T(8,128)(2,1)} %bitcast.29), custom_call_target="tpu_custom_call" | custom-call | flops 4026531840 | bytes 12582912 | tf_op jit(solution)/shard_map/project_a/pallas_call | solution.py:166
  95.8 7.8 %project_b.1 = (bf16[8,48,768]{2,1,0:T(8,128)(2,1)}, bf16[8,48,768]{2,1,0:T(8,128)(2,1)}, bf16[8,48,768]{2,1,0:T(8,128)(2,1)}, bf16[8,48,768]{2,1,0:T(8,128)(2,1)}) custom-call(s32[1]{0:T(128)} %bitcast.place, bf16[1024,768]{1,0:T(8,128)(2,1)} %copy-done.1, bf16[8,32,128,128]{3,2,1,0:T(8,128)(2,1)} %bitcast.30), custom_call_target="tpu_custom_call" | custom-call | flops 2415919104 | bytes 12582912 | tf_op jit(solution)/shard_map/project_b/pallas_call | solution.py:202
  104.1 2.5 collective-permute-start.4
  107.7 11.7 %collective-permute-done.3.p1 = bf16[8,48,768]{2,1,0:T(8,128)(2,1)S(1)} collective-permute-done((bf16[8,48,768]{2,1,0:T(8,128)(2,1)}, bf16[8,48,768]{2,1,0:T(8,128)(2,1)S(1)}, u32[]{:S(2)}, u32[]{:S(2)}) %collective-permute-start.3) | collective-permute-done | bytes 589856 | tf_op jit(solution)/shard_map/ppermute | solution.py:404
  119.4 13.2 %collective-permute-done.4.p2 = bf16[8,48,768]{2,1,0:T(8,128)(2,1)S(1)} collective-permute-done((bf16[8,48,768]{2,1,0:T(8,128)(2,1)}, bf16[8,48,768]{2,1,0:T(8,128)(2,1)S(1)}, u32[]{:S(2)}, u32[]{:S(2)}) %collective-permute-start.4) | collective-permute-done | bytes 589856 | tf_op jit(solution)/shard_map/ppermute | solution.py:404
  133.6 3.7 %fold.1 = bf16[8,48,768]{2,1,0:T(8,128)(2,1)} custom-call(bf16[8,48,768]{2,1,0:T(8,128)(2,1)} %get-tuple-element.14.p0, bf16[8,48,768]{2,1,0:T(8,128)(2,1)} %copy-done.5, bf16[8,48,768]{2,1,0:T(8,128)(2,1)} %copy-done.6, bf16[8,48,768]{2,1,0:T(8,128)(2,1)} %copy-done.7), custom_call_target="tpu_custom_call" | custom-call | bytes 3145728 | tf_op jit(solution)/shard_map/fold/pallas_call | solution.py:233
  137.3 7.2 %all-to-all-start.1 = ((bf16[8,48,768]{2,1,0:T(8,128)(2,1)}), bf16[8,48,768]{2,1,0:T(8,128)(2,1)S(1)}, u32[]{:S(2)}, u32[]{:S(2)}) async-start(bf16[8,48,768]{2,1,0:T(8,128)(2,1)} %fold.1), calls=%async_computation.2 | async-start | bytes 1179648 | tf_op jit(solution)/shard_map/all_to_all | solution.py:425
  144.6 4.5 %reduce-scatter.2.cloned.1.call-done = bf16[1,4,80,768]{3,2,1,0:T(8,128)(2,1)} async-done(((bf16[8,4,80,768]{3,2,1,0:T(8,128)(2,1)}), bf16[1,4,80,768]{3,2,1,0:T(8,128)(2,1)}) %reduce-scatter.2.cloned.1.call-update) | async-done | bytes 491536 | tf_op jit(solution)/shard_map/reduce_scatter | solution.py:423
  151.4 2.4 collective-permute-start.1
  155.0 6.5 %all-to-all-done.1.gb_ref = bf16[8,48,768]{2,1,0:T(8,128)(2,1)S(1)} async-done(((bf16[8,48,768]{2,1,0:T(8,128)(2,1)}), bf16[8,48,768]{2,1,0:T(8,128)(2,1)S(1)}, u32[]{:S(2)}, u32[]{:S(2)}) %all-to-all-start.1) | async-done | bytes 589856 | tf_op jit(solution)/shard_map/all_to_all | solution.py:425
  161.5 1.7 optimizer.1
  163.3 10.7 %all_to_all.20 = f32[8,8,128]{2,1,0:T(8,128)S(1)} all-to-all(f32[8,8,128]{2,1,0:T(8,128)S(1)} %broadcast_in_dim.4), channel_id=1, replica_groups=mesh['x'=4,'z'=8,'y'=4,'core'=2] {'y','core'}, dimensions={0} | all-to-all | bytes 65536 | tf_op jit(solution)/shard_map/all_to_all | solution.py:409
  174.6 7.6 %all-to-all-start.3 = ((f32[32,8,128]{2,1,0:T(8,128)}), f32[32,8,128]{2,1,0:T(8,128)S(1)}, u32[]{:S(2)}, u32[]{:S(2)}) async-start(f32[32,8,128]{2,1,0:T(8,128)} %broadcast_in_dim.5), calls=%async_computation.4 | async-start | bytes 262144 | tf_op jit(solution)/shard_map/all_to_all | solution.py:409
  182.3 1.5 collective-permute-start.10
  185.2 1.5 collective-permute-start.12
  186.8 1.8 collective-permute-done.10.a1
  188.7 4.9 %collective-permute-done.12.a3 = bf16[2,48,768]{2,1,0:T(8,128)(2,1)S(1)} collective-permute-done((bf16[2,48,768]{2,1,0:T(8,128)(2,1)S(1)}, bf16[2,48,768]{2,1,0:T(8,128)(2,1)S(1)}, u32[]{:S(2)}, u32[]{:S(2)}) %collective-permute-start.12) | collective-permute-done | bytes 147488 | tf_op jit(solution)/shard_map/ppermute | solution.py:404
  193.5 1.4 apply_a.1
  195.0 8.7 %all-gather.9.cloned.1.call-done = bf16[16,80,768]{2,1,0:T(8,128)(2,1)} async-done(((bf16[2,80,768]{2,1,0:T(8,128)(2,1)}), bf16[16,80,768]{2,1,0:T(8,128)(2,1)}) %all-gather.9.cloned.1.call-update) | async-done | bytes 1966096 | tf_op jit(solution)/shard_map/all_gather | solution.py:436
  203.7 1.5 copy-done
  206.9 1.5 collective-permute-start.7
  208.4 18.2 %collective-permute-done.6.b1 = bf16[8,80,768]{2,1,0:T(8,128)(2,1)S(1)} collective-permute-done((bf16[8,80,768]{2,1,0:T(8,128)(2,1)S(1)}, bf16[8,80,768]{2,1,0:T(8,128)(2,1)S(1)}, u32[]{:S(2)}, u32[]{:S(2)}) %collective-permute-start.6) | collective-permute-done | bytes 983072 | tf_op jit(solution)/shard_map/ppermute | solution.py:404
  228.3 2.6 %collective-permute-start.9 = (bf16[4,80,768]{2,1,0:T(8,128)(2,1)}, bf16[4,80,768]{2,1,0:T(8,128)(2,1)}, u32[]{:S(2)}, u32[]{:S(2)}) collective-permute-start(bf16[4,80,768]{2,1,0:T(8,128)(2,1)} %slice.41), channel_id=1, source_target_pairs={{0,192},{64,0},{128,64},{192,128},{1,193},{65,1},{129,65},{193,129... | collective-permute-start | bytes 1474568 | tf_op jit(solution)/shard_map/ppermute | solution.py:404
  233.8 3.4 %collective-permute-done.8.b3 = bf16[4,80,768]{2,1,0:T(8,128)(2,1)} collective-permute-done((bf16[4,80,768]{2,1,0:T(8,128)(2,1)}, bf16[4,80,768]{2,1,0:T(8,128)(2,1)}, u32[]{:S(2)}, u32[]{:S(2)}) %collective-permute-start.8) | collective-permute-done | bytes 491552 | tf_op jit(solution)/shard_map/ppermute | solution.py:404
  237.3 5.2 %join_x.1.base_ref = bf16[4,8,128,768]{3,2,1,0:T(8,128)(2,1)} custom-call(s32[4]{0:T(128)S(1)} %pad_add_fusion.place_ref, bf16[8,80,768]{2,1,0:T(8,128)(2,1)S(1)} %apply_b.1.b0, bf16[8,80,768]{2,1,0:T(8,128)(2,1)S(1)} %collective-permute-done.6.b1, bf16[8,80,768]{2,1,0:T(8,128)(2,1)S(1)} %collective-permute-done.7.b2, ...), custom_call_target="tpu_custom_call" | custom-call | bytes 7340032 | tf_op jit(solution)/shard_map/join_x/pallas_call | solution.py:350
  242.5 3.5 %all-gather.11.cloned.1.call-done = bf16[32,48,768]{2,1,0:T(8,128)(2,1)} async-done(((bf16[4,48,768]{2,1,0:T(8,128)(2,1)}), bf16[32,48,768]{2,1,0:T(8,128)(2,1)}) %all-gather.11.cloned.1.call-update) | async-done | bytes 2359312 | tf_op jit(solution)/shard_map/all_gather | solution.py:440
  246.0 2.5 join_sc.1
  (50 shorter events, 15.7 us)
Async XLA Ops:
  7.2 79.9 %all-gather.7.cloned.1.call-start = ((), (), s32[]{:S(2)}) async-start(), calls=%async_computation.6 | async-start | bytes 9437184 | tf_op jit(solution)/shard_map/all_gather | solution.py:416
  12.4 58.8 %all-to-all-start = ((bf16[8,128,1280]{2,1,0:T(8,128)(2,1)}), bf16[8,128,1280]{2,1,0:T(8,128)(2,1)S(1)}, u32[]{:S(2)}, u32[]{:S(2)}) async-start(bf16[8,128,1280]{2,1,0:T(8,128)(2,1)} %pack.1), calls=%async_computation | async-start | bytes 5242880 | tf_op jit(solution)/shard_map/all_to_all | solution.py:415
  19.2 129.8 %reduce-scatter.2.cloned.1.call-start = ((), (), s32[]{:S(2)}) async-start(), calls=%async_computation.5 | async-start | bytes 4423680 | tf_op jit(solution)/shard_map/reduce_scatter | solution.py:423
  84.7 1.2 copy-start.1
  103.6 57.9 %copy-start.2 = (f32[128,768]{1,0:T(8,128)S(1)}, f32[128,768]{1,0:T(8,128)}, u32[]{:S(2)}) copy-start(f32[128,768]{1,0:T(8,128)} %w_ref.1) | copy-start | bytes 1179652
  103.6 57.9 %copy-start.3 = (f32[128,768]{1,0:T(8,128)S(1)}, f32[128,768]{1,0:T(8,128)}, u32[]{:S(2)}) copy-start(f32[128,768]{1,0:T(8,128)} %m_ref.1) | copy-start | bytes 1179652
  103.6 57.9 %copy-start.4 = (f32[128,768]{1,0:T(8,128)S(1)}, f32[128,768]{1,0:T(8,128)}, u32[]{:S(2)}) copy-start(f32[128,768]{1,0:T(8,128)} %v_ref.1) | copy-start | bytes 1179652
  103.6 15.8 %collective-permute-start.3 = (bf16[8,48,768]{2,1,0:T(8,128)(2,1)}, bf16[8,48,768]{2,1,0:T(8,128)(2,1)S(1)}, u32[]{:S(2)}, u32[]{:S(2)}) collective-permute-start(bf16[8,48,768]{2,1,0:T(8,128)(2,1)} %get-tuple-element.15), channel_id=1, source_target_pairs={{0,64},{64,128},{128,192},{192,0},{1,65},{65,129},{129,193},{193,1... | collective-permute-start | bytes 1769480 | tf_op jit(solution)/shard_map/ppermute | solution.py:404
  104.1 28.5 %collective-permute-start.4 = (bf16[8,48,768]{2,1,0:T(8,128)(2,1)}, bf16[8,48,768]{2,1,0:T(8,128)(2,1)S(1)}, u32[]{:S(2)}, u32[]{:S(2)}) collective-permute-start(bf16[8,48,768]{2,1,0:T(8,128)(2,1)} %get-tuple-element.16), channel_id=1, source_target_pairs={{0,128},{64,192},{128,0},{192,64},{1,129},{65,193},{129,1},{193,65... | collective-permute-start | bytes 1769480 | tf_op jit(solution)/shard_map/ppermute | solution.py:404
  106.5 26.1 %collective-permute-start.5 = (bf16[8,48,768]{2,1,0:T(8,128)(2,1)}, bf16[8,48,768]{2,1,0:T(8,128)(2,1)S(1)}, u32[]{:S(2)}, u32[]{:S(2)}) collective-permute-start(bf16[8,48,768]{2,1,0:T(8,128)(2,1)} %get-tuple-element.17), channel_id=1, source_target_pairs={{0,192},{64,0},{128,64},{192,128},{1,193},{65,1},{129,65},{193,129... | collective-permute-start | bytes 1769480 | tf_op jit(solution)/shard_map/ppermute | solution.py:404
  119.4 13.3 %copy-start.5 = (bf16[8,48,768]{2,1,0:T(8,128)(2,1)}, bf16[8,48,768]{2,1,0:T(8,128)(2,1)S(1)}, u32[]{:S(2)}) copy-start(bf16[8,48,768]{2,1,0:T(8,128)(2,1)S(1)} %collective-permute-done.3.p1) | copy-start | bytes 1769476
  132.6 0.9 copy-start.6
  132.7 0.9 copy-start.7
  137.3 24.2 %all-to-all-start.1 = ((bf16[8,48,768]{2,1,0:T(8,128)(2,1)}), bf16[8,48,768]{2,1,0:T(8,128)(2,1)S(1)}, u32[]{:S(2)}, u32[]{:S(2)}) async-start(bf16[8,48,768]{2,1,0:T(8,128)(2,1)} %fold.1), calls=%async_computation.2 | async-start | bytes 1179648 | tf_op jit(solution)/shard_map/all_to_all | solution.py:425
  144.5 59.2 %all-gather.9.cloned.1.call-start = ((), (), s32[]{:S(2)}) async-start(), calls=%async_computation.7 | async-start | bytes 2211840 | tf_op jit(solution)/shard_map/all_gather | solution.py:436
  150.1 11.4 %collective-permute-start = (bf16[80,768]{1,0:T(8,128)(2,1)S(1)}, bf16[80,768]{1,0:T(8,128)(2,1)S(1)}, u32[]{:S(2)}, u32[]{:S(2)}) collective-permute-start(bf16[80,768]{1,0:T(8,128)(2,1)S(1)} %get-tuple-element.26), channel_id=1, source_target_pairs={{0,64},{64,128},{128,192},{192,0},{1,65},{65,129},{129,193},{193,1... | collective-permute-start | bytes 368648 | tf_op jit(solution)/shard_map/ppermute | solution.py:404
  151.4 10.1 %collective-permute-start.1 = (bf16[80,768]{1,0:T(8,128)(2,1)S(1)}, bf16[80,768]{1,0:T(8,128)(2,1)S(1)}, u32[]{:S(2)}, u32[]{:S(2)}) collective-permute-start(bf16[80,768]{1,0:T(8,128)(2,1)S(1)} %get-tuple-element.25), channel_id=1, source_target_pairs={{0,128},{64,192},{128,0},{192,64},{1,129},{65,193},{129,1},{193,65... | collective-permute-start | bytes 368648 | tf_op jit(solution)/shard_map/ppermute | solution.py:404
  153.8 7.7 %collective-permute-start.2 = (bf16[80,768]{1,0:T(8,128)(2,1)S(1)}, bf16[80,768]{1,0:T(8,128)(2,1)S(1)}, u32[]{:S(2)}, u32[]{:S(2)}) collective-permute-start(bf16[80,768]{1,0:T(8,128)(2,1)S(1)} %get-tuple-element.24), channel_id=1, source_target_pairs={{0,192},{64,0},{128,64},{192,128},{1,193},{65,1},{129,65},{193,129... | collective-permute-start | bytes 368648 | tf_op jit(solution)/shard_map/ppermute | solution.py:404
  174.6 18.9 %all-to-all-start.3 = ((f32[32,8,128]{2,1,0:T(8,128)}), f32[32,8,128]{2,1,0:T(8,128)S(1)}, u32[]{:S(2)}, u32[]{:S(2)}) async-start(f32[32,8,128]{2,1,0:T(8,128)} %broadcast_in_dim.5), calls=%async_computation.4 | async-start | bytes 262144 | tf_op jit(solution)/shard_map/all_to_all | solution.py:409
  182.2 63.8 %all-gather.11.cloned.1.call-start = ((), (), s32[]{:S(2)}) async-start(), calls=%async_computation.8 | async-start | bytes 2654208 | tf_op jit(solution)/shard_map/all_gather | solution.py:440
  182.3 6.4 %collective-permute-start.10 = (bf16[2,48,768]{2,1,0:T(8,128)(2,1)S(1)}, bf16[2,48,768]{2,1,0:T(8,128)(2,1)S(1)}, u32[]{:S(2)}, u32[]{:S(2)}) collective-permute-start(bf16[2,48,768]{2,1,0:T(8,128)(2,1)S(1)} %get-tuple-element.23.a0), channel_id=1, source_target_pairs={{0,64},{64,128},{128,192},{192,0},{1,65},{65,129},{129,193},{193,1... | collective-permute-start | bytes 442376 | tf_op jit(solution)/shard_map/ppermute | solution.py:404
  183.8 4.9 %collective-permute-start.11 = (bf16[2,48,768]{2,1,0:T(8,128)(2,1)S(1)}, bf16[2,48,768]{2,1,0:T(8,128)(2,1)S(1)}, u32[]{:S(2)}, u32[]{:S(2)}) collective-permute-start(bf16[2,48,768]{2,1,0:T(8,128)(2,1)S(1)} %get-tuple-element.23.a0), channel_id=1, source_target_pairs={{0,192},{64,0},{128,64},{192,128},{1,193},{65,1},{129,65},{193,129... | collective-permute-start | bytes 442376 | tf_op jit(solution)/shard_map/ppermute | solution.py:404
  185.2 8.3 %collective-permute-start.12 = (bf16[2,48,768]{2,1,0:T(8,128)(2,1)S(1)}, bf16[2,48,768]{2,1,0:T(8,128)(2,1)S(1)}, u32[]{:S(2)}, u32[]{:S(2)}) collective-permute-start(bf16[2,48,768]{2,1,0:T(8,128)(2,1)S(1)} %get-tuple-element.23.a0), channel_id=1, source_target_pairs={{0,128},{64,192},{128,0},{192,64},{1,129},{65,193},{129,1},{193,65... | collective-permute-start | bytes 442376 | tf_op jit(solution)/shard_map/ppermute | solution.py:404
  203.7 1.5 copy-start
  205.7 21.0 %collective-permute-start.6 = (bf16[8,80,768]{2,1,0:T(8,128)(2,1)S(1)}, bf16[8,80,768]{2,1,0:T(8,128)(2,1)S(1)}, u32[]{:S(2)}, u32[]{:S(2)}) collective-permute-start(bf16[8,80,768]{2,1,0:T(8,128)(2,1)S(1)} %apply_b.1.b0), channel_id=1, source_target_pairs={{0,64},{64,128},{128,192},{192,0},{1,65},{65,129},{129,193},{193,1... | collective-permute-start | bytes 2949128 | tf_op jit(solution)/shard_map/ppermute | solution.py:404
  206.9 20.6 %collective-permute-start.7 = (bf16[8,80,768]{2,1,0:T(8,128)(2,1)S(1)}, bf16[8,80,768]{2,1,0:T(8,128)(2,1)S(1)}, u32[]{:S(2)}, u32[]{:S(2)}) collective-permute-start(bf16[8,80,768]{2,1,0:T(8,128)(2,1)S(1)} %apply_b.1.b0), channel_id=1, source_target_pairs={{0,192},{64,0},{128,64},{192,128},{1,193},{65,1},{129,65},{193,129... | collective-permute-start | bytes 2949128 | tf_op jit(solution)/shard_map/ppermute | solution.py:404
  227.5 9.8 %collective-permute-start.8 = (bf16[4,80,768]{2,1,0:T(8,128)(2,1)}, bf16[4,80,768]{2,1,0:T(8,128)(2,1)}, u32[]{:S(2)}, u32[]{:S(2)}) collective-permute-start(bf16[4,80,768]{2,1,0:T(8,128)(2,1)} %slice.40), channel_id=1, source_target_pairs={{0,64},{64,128},{128,192},{192,0},{1,65},{65,129},{129,193},{193,1... | collective-permute-start | bytes 1474568 | tf_op jit(solution)/shard_map/ppermute | solution.py:404
  228.3 8.9 %collective-permute-start.9 = (bf16[4,80,768]{2,1,0:T(8,128)(2,1)}, bf16[4,80,768]{2,1,0:T(8,128)(2,1)}, u32[]{:S(2)}, u32[]{:S(2)}) collective-permute-start(bf16[4,80,768]{2,1,0:T(8,128)(2,1)} %slice.41), channel_id=1, source_target_pairs={{0,192},{64,0},{128,64},{192,128},{1,193},{65,1},{129,65},{193,129... | collective-permute-start | bytes 1474568 | tf_op jit(solution)/shard_map/ppermute | solution.py:404
Sparse Core Ops, SparseCore 0:
  9.9 77.1 all-gather.6
  95.9 53.0 reduce-scatter.1
  163.4 40.2 all-gather.8
  205.3 40.6 all-gather.10

commit v9 on v8

--- a/solution.py
+++ b/solution.py
@@ -146,43 +146,46 @@
     )(packed, packed, packed, packed)
 
 
-def project(grouped, x, lo, hi, at_x, name):
-    part = hi - lo
-
-    def kernel(place, grouped_ref, x_ref, out_ref):
+def project_a_kernel(place, grouped_ref, x0, x1, out_ref):
+    for k, ref in enumerate((x0, x1)):
         rows = jnp.concatenate(
-            [x_ref[t, :, lo:hi, :].reshape(NZ * part, ROWS) for t in range(8)], axis=1
+            [ref[t, :, :PART_A, :].reshape(NZ * PART_A, ROWS) for t in range(8)], axis=1
         )
-        res = dot(rows, grouped_ref[...], 1, 0).astype(bf16)
-        out_ref[...] = res.reshape(out_ref.shape)
-
-    if at_x is None:
-        shape, block = (NX, NZ, part, COLS), (1, NZ, part, COLS)
-        out_map = lambda x, place: (x, 0, 0, 0)
-        at_x = jnp.zeros((1,), jnp.int32)
-    else:
-        shape, block = (NZ, NX, part, COLS), (NZ, 1, part, COLS)
-        out_map = lambda x, place: (0, lax.rem(x - place[0] + NX, NX), 0, 0)
-    return pl.pallas_call(
-        kernel,
+        if k == 0:
+            first = rows
+    rows = jnp.concatenate([first, rows], axis=0)
+    res = dot(rows, grouped_ref[...], 1, 0).astype(bf16).reshape(2, NZ, PART_A, COLS)
+    out_ref[:, 0] = res[0]
+    out_ref[:, 1] = res[1]
+
+
+def project_a(at_x, grouped, x):
+    def x_spec(by):
+        return pl.BlockSpec(
+            (8, NZ, ROWS, ROWS), lambda j, place: (0, lax.rem(place[0] + 2 * j + by, NX), 0, 0)
+        )
+
+    return pl.pallas_call(
+        project_a_kernel,
         grid_spec=pltpu.PrefetchScalarGridSpec(
             num_scalar_prefetch=1,
-            grid=(NX,),
+            grid=(NX // 2,),
             in_specs=[
-                pl.BlockSpec((LENGTH, COLS), lambda x, place: (0, 0)),
-                pl.BlockSpec((8, NZ, ROWS, ROWS), lambda x, place: (0, x, 0, 0)),
+                pl.BlockSpec((LENGTH, COLS), lambda j, place: (0, 0)),
+                x_spec(0),
+                x_spec(1),
             ],
-            out_specs=pl.BlockSpec(block, out_map),
-        ),
-        out_shape=jax.ShapeDtypeStruct(shape, bf16),
+            out_specs=pl.BlockSpec((NZ, 2, PART_A, COLS), lambda j, place: (0, j, 0, 0)),
+        ),
+        out_shape=jax.ShapeDtypeStruct((NZ, NX, PART_A, COLS), bf16),
         compiler_params=pltpu.CompilerParams(vmem_limit_bytes=60 << 20),
         cost_estimate=pl.CostEstimate(
-            flops=2 * LENGTH * COLS * WIDTH * part // ROWS,
+            flops=2 * LENGTH * COLS * WIDTH * PART_A // ROWS,
             bytes_accessed=12 << 20,
             transcendentals=0,
         ),
-        name=name,
-    )(at_x, grouped, x)
+        name="project_a",
+    )(at_x, grouped, x, x)
 
 
 def project_b_kernel(place, grouped_ref, x_ref, *outs):
@@ -418,7 +421,7 @@
 
     at_x = lax.axis_index("x")
     place_x = at_x.reshape(1).astype(jnp.int32)
-    part_a = project(grouped, x_full, 0, PART_A, place_x, "project_a")
+    part_a = project_a(place_x, grouped, x_full)
     part_b = project_b(place_x, grouped, x_full)
     part_a = lax.psum_scatter(part_a, "z", scatter_dimension=0, tiled=True)[0]
     part_b = fold([part_b[0]] + [shift(part_b[by], "x", NX, by) for by in range(1, NX)])

time: 258 us -> 258 us (level)
  no operation moved by 1% of the time
where the time goes in v9:
time: 258 us; the launch traced here: 255 us
  waiting for transfers between devices  130 us (50%)
  Pallas kernels  50 us (19%)
  starting transfers between devices  40.3 us (16%)
  between operations  15.3 us (6%)
  blocking collectives  10.7 us (4%)
  local copies, waits for them, and re-layouts  7.67 us (3%)
    ppermute x13, waiting for transfers between devices, shift(): lax.ppermute(value, axis, [(i, (i + by) % size) for i in range(size)])  53.4 us
    all_to_all x1, waiting for transfers between devices, body(): lax.all_to_all(packed, ('y', 'core'), 0, 0, tiled=True)  52 us
    ppermute x13, starting transfers between devices, shift(): lax.ppermute(value, axis, [(i, (i + by) % size) for i in range(size)])  18.7 us
    pallas_call x1, Pallas kernels, attention(): pl.pallas_call(attention_kernel, grid=(GROUP,), in_specs=[pl.BlockSpec((L...  13.5 us
    all_to_all x1, blocking collectives, spread(): return lax.all_to_all(wide, axes, 0, 0, tiled=True)  10.7 us
    all_gather x1, waiting for transfers between devices, body(): gathered_b = lax.all_gather(mine_b, 'z', axis=0, tiled=False)  8.89 us
    pallas_call x1, Pallas kernels, project_a(): pl.pallas_call(project_a_kernel, grid_spec=pltpu.PrefetchScalarGridSpec(n...  8.4 us
    pallas_call x1, Pallas kernels, project_b(): pl.pallas_call(project_b_kernel, grid_spec=pltpu.PrefetchScalarGridSpec(n...  7.81 us
  transfers between devices with their start and end apart: 20, of which 13 were waited for; matrix products, arithmetic and copies ran while one was open for 2% of the time, Pallas kernels for 14%

profile of v9, /device:TPU:1, one launch (start us, length us, event | category | flops | bytes accessed | tf_op | source)
XLA Modules:
  0.0 254.8 jit_solution(15314411550127964803)
XLA Ops:
  7.2 2.3 turn.1
  9.5 2.9 %pack.1 = bf16[8,128,1280]{2,1,0:T(8,128)(2,1)} custom-call(bf16[128,4096]{1,0:T(8,128)(2,1)} %bitcast.33, bf16[128,1024]{1,0:T(8,128)(2,1)} %bitcast.36, bf16[128,1024]{1,0:T(8,128)(2,1)} %bitcast.37, bf16[128,4096]{1,0:T(8,128)(2,1)} %bitcast.34), custom_call_target="tpu_custom_call" | custom-call | bytes 5242880 | tf_op jit(solution)/shard_map/pack/pallas_call | solution.py:52
  12.4 6.8 %all-to-all-start = ((bf16[8,128,1280]{2,1,0:T(8,128)(2,1)}), bf16[8,128,1280]{2,1,0:T(8,128)(2,1)S(1)}, u32[]{:S(2)}, u32[]{:S(2)}) async-start(bf16[8,128,1280]{2,1,0:T(8,128)(2,1)} %pack.1), calls=%async_computation | async-start | bytes 5242880 | tf_op jit(solution)/shard_map/all_to_all | solution.py:418
  19.2 52.0 %all-to-all-done = bf16[8,128,1280]{2,1,0:T(8,128)(2,1)S(1)} async-done(((bf16[8,128,1280]{2,1,0:T(8,128)(2,1)}), bf16[8,128,1280]{2,1,0:T(8,128)(2,1)S(1)}, u32[]{:S(2)}, u32[]{:S(2)}) %all-to-all-start) | async-done | bytes 2621472 | tf_op jit(solution)/shard_map/all_to_all | solution.py:418
  71.2 13.5 %attention_backward.1.grouped_ref = bf16[1024,768]{1,0:T(8,128)(2,1)S(1)} custom-call(bf16[1024,1280]{1,0:T(8,128)(2,1)S(1)} %bitcast.23, bf16[1024,1280]{1,0:T(8,128)(2,1)S(1)} %bitcast.24, bf16[1024,1280]{1,0:T(8,128)(2,1)S(1)} %bitcast.25, bf16[1024,1280]{1,0:T(8,128)(2,1)S(1)} %bitcast.26), custom_call_target="tpu_custom_call" | custom-call | flops 4294967296 | bytes 5242880 | tf_op jit(solution)/shard_map/attention_backward/pallas_call | solution.py:125
  87.1 8.4 %project_a.1 = bf16[8,4,80,768]{3,2,1,0:T(8,128)(2,1)} custom-call(s32[1]{0:T(128)} %bitcast.place, bf16[1024,768]{1,0:T(8,128)(2,1)} %copy-done, bf16[8,32,128,128]{3,2,1,0:T(8,128)(2,1)} %bitcast.28, bf16[8,32,128,128]{3,2,1,0:T(8,128)(2,1)} %bitcast.29), custom_call_target="tpu_custom_call" | custom-call | flops 4026531840 | bytes 12582912 | tf_op jit(solution)/shard_map/project_a/pallas_call | solution.py:168
  95.5 7.8 %project_b.1 = (bf16[8,48,768]{2,1,0:T(8,128)(2,1)}, bf16[8,48,768]{2,1,0:T(8,128)(2,1)}, bf16[8,48,768]{2,1,0:T(8,128)(2,1)}, bf16[8,48,768]{2,1,0:T(8,128)(2,1)}) custom-call(s32[1]{0:T(128)} %bitcast.place, bf16[1024,768]{1,0:T(8,128)(2,1)} %copy-done, bf16[8,32,128,128]{3,2,1,0:T(8,128)(2,1)} %bitcast.30), custom_call_target="tpu_custom_call" | custom-call | flops 2415919104 | bytes 12582912 | tf_op jit(solution)/shard_map/project_b/pallas_call | solution.py:205
  103.8 2.4 collective-permute-start.4
  107.4 11.7 %collective-permute-done.3.p1 = bf16[8,48,768]{2,1,0:T(8,128)(2,1)S(1)} collective-permute-done((bf16[8,48,768]{2,1,0:T(8,128)(2,1)}, bf16[8,48,768]{2,1,0:T(8,128)(2,1)S(1)}, u32[]{:S(2)}, u32[]{:S(2)}) %collective-permute-start.3) | collective-permute-done | bytes 589856 | tf_op jit(solution)/shard_map/ppermute | solution.py:407
  119.1 13.2 %collective-permute-done.4.p2 = bf16[8,48,768]{2,1,0:T(8,128)(2,1)S(1)} collective-permute-done((bf16[8,48,768]{2,1,0:T(8,128)(2,1)}, bf16[8,48,768]{2,1,0:T(8,128)(2,1)S(1)}, u32[]{:S(2)}, u32[]{:S(2)}) %collective-permute-start.4) | collective-permute-done | bytes 589856 | tf_op jit(solution)/shard_map/ppermute | solution.py:407
  133.3 3.7 %fold.1 = bf16[8,48,768]{2,1,0:T(8,128)(2,1)} custom-call(bf16[8,48,768]{2,1,0:T(8,128)(2,1)} %get-tuple-element.14.p0, bf16[8,48,768]{2,1,0:T(8,128)(2,1)} %copy-done.5, bf16[8,48,768]{2,1,0:T(8,128)(2,1)} %copy-done.6, bf16[8,48,768]{2,1,0:T(8,128)(2,1)} %copy-done.7), custom_call_target="tpu_custom_call" | custom-call | bytes 3145728 | tf_op jit(solution)/shard_map/fold/pallas_call | solution.py:236
  137.0 7.2 %all-to-all-start.1 = ((bf16[8,48,768]{2,1,0:T(8,128)(2,1)}), bf16[8,48,768]{2,1,0:T(8,128)(2,1)S(1)}, u32[]{:S(2)}, u32[]{:S(2)}) async-start(bf16[8,48,768]{2,1,0:T(8,128)(2,1)} %fold.1), calls=%async_computation.2 | async-start | bytes 1179648 | tf_op jit(solution)/shard_map/all_to_all | solution.py:428
  144.3 4.5 %reduce-scatter.2.cloned.1.call-done = bf16[1,4,80,768]{3,2,1,0:T(8,128)(2,1)} async-done(((bf16[8,4,80,768]{3,2,1,0:T(8,128)(2,1)}), bf16[1,4,80,768]{3,2,1,0:T(8,128)(2,1)}) %reduce-scatter.2.cloned.1.call-update) | async-done | bytes 491536 | tf_op jit(solution)/shard_map/reduce_scatter | solution.py:426
  151.1 2.4 collective-permute-start.1
  154.7 6.5 %all-to-all-done.1.gb_ref = bf16[8,48,768]{2,1,0:T(8,128)(2,1)S(1)} async-done(((bf16[8,48,768]{2,1,0:T(8,128)(2,1)}), bf16[8,48,768]{2,1,0:T(8,128)(2,1)S(1)}, u32[]{:S(2)}, u32[]{:S(2)}) %all-to-all-start.1) | async-done | bytes 589856 | tf_op jit(solution)/shard_map/all_to_all | solution.py:428
  161.2 1.7 optimizer.1
  163.0 10.7 %all_to_all.20 = f32[8,8,128]{2,1,0:T(8,128)S(1)} all-to-all(f32[8,8,128]{2,1,0:T(8,128)S(1)} %broadcast_in_dim.4), channel_id=1, replica_groups=mesh['x'=4,'z'=8,'y'=4,'core'=2] {'y','core'}, dimensions={0} | all-to-all | bytes 65536 | tf_op jit(solution)/shard_map/all_to_all | solution.py:412
  174.3 7.5 %all-to-all-start.3 = ((f32[32,8,128]{2,1,0:T(8,128)}), f32[32,8,128]{2,1,0:T(8,128)S(1)}, u32[]{:S(2)}, u32[]{:S(2)}) async-start(f32[32,8,128]{2,1,0:T(8,128)} %broadcast_in_dim.5), calls=%async_computation.4 | async-start | bytes 262144 | tf_op jit(solution)/shard_map/all_to_all | solution.py:412
  183.3 1.4 collective-permute-start.11
  184.7 1.5 collective-permute-start.12
  186.3 1.9 collective-permute-done.10.a1
  188.2 4.8 %collective-permute-done.12.a3 = bf16[2,48,768]{2,1,0:T(8,128)(2,1)S(1)} collective-permute-done((bf16[2,48,768]{2,1,0:T(8,128)(2,1)S(1)}, bf16[2,48,768]{2,1,0:T(8,128)(2,1)S(1)}, u32[]{:S(2)}, u32[]{:S(2)}) %collective-permute-start.12) | collective-permute-done | bytes 147488 | tf_op jit(solution)/shard_map/ppermute | solution.py:407
  193.0 1.4 apply_a.1
  194.5 8.9 %all-gather.9.cloned.1.call-done = bf16[16,80,768]{2,1,0:T(8,128)(2,1)} async-done(((bf16[2,80,768]{2,1,0:T(8,128)(2,1)}), bf16[16,80,768]{2,1,0:T(8,128)(2,1)}) %all-gather.9.cloned.1.call-update) | async-done | bytes 1966096 | tf_op jit(solution)/shard_map/all_gather | solution.py:439
  203.3 1.5 copy-done.1
  206.6 1.5 collective-permute-start.7
  208.1 18.2 %collective-permute-done.6.b1 = bf16[8,80,768]{2,1,0:T(8,128)(2,1)S(1)} collective-permute-done((bf16[8,80,768]{2,1,0:T(8,128)(2,1)S(1)}, bf16[8,80,768]{2,1,0:T(8,128)(2,1)S(1)}, u32[]{:S(2)}, u32[]{:S(2)}) %collective-permute-start.6) | collective-permute-done | bytes 983072 | tf_op jit(solution)/shard_map/ppermute | solution.py:407
  228.0 2.6 %collective-permute-start.9 = (bf16[4,80,768]{2,1,0:T(8,128)(2,1)}, bf16[4,80,768]{2,1,0:T(8,128)(2,1)}, u32[]{:S(2)}, u32[]{:S(2)}) collective-permute-start(bf16[4,80,768]{2,1,0:T(8,128)(2,1)} %slice.41), channel_id=1, source_target_pairs={{0,192},{64,0},{128,64},{192,128},{1,193},{65,1},{129,65},{193,129... | collective-permute-start | bytes 1474568 | tf_op jit(solution)/shard_map/ppermute | solution.py:407
  233.5 3.4 %collective-permute-done.8.b3 = bf16[4,80,768]{2,1,0:T(8,128)(2,1)} collective-permute-done((bf16[4,80,768]{2,1,0:T(8,128)(2,1)}, bf16[4,80,768]{2,1,0:T(8,128)(2,1)}, u32[]{:S(2)}, u32[]{:S(2)}) %collective-permute-start.8) | collective-permute-done | bytes 491552 | tf_op jit(solution)/shard_map/ppermute | solution.py:407
  236.9 5.2 %join_x.1.base_ref = bf16[4,8,128,768]{3,2,1,0:T(8,128)(2,1)} custom-call(s32[4]{0:T(128)S(1)} %pad_add_fusion.place_ref, bf16[8,80,768]{2,1,0:T(8,128)(2,1)S(1)} %apply_b.1.b0, bf16[8,80,768]{2,1,0:T(8,128)(2,1)S(1)} %collective-permute-done.6.b1, bf16[8,80,768]{2,1,0:T(8,128)(2,1)S(1)} %collective-permute-done.7.b2, ...), custom_call_target="tpu_custom_call" | custom-call | bytes 7340032 | tf_op jit(solution)/shard_map/join_x/pallas_call | solution.py:353
  242.2 3.5 %all-gather.11.cloned.1.call-done = bf16[32,48,768]{2,1,0:T(8,128)(2,1)} async-done(((bf16[4,48,768]{2,1,0:T(8,128)(2,1)}), bf16[32,48,768]{2,1,0:T(8,128)(2,1)}) %all-gather.11.cloned.1.call-update) | async-done | bytes 2359312 | tf_op jit(solution)/shard_map/all_gather | solution.py:443
  245.7 2.5 join_sc.1
  (50 shorter events, 15.6 us)
Async XLA Ops:
  7.2 79.9 %all-gather.7.cloned.1.call-start = ((), (), s32[]{:S(2)}) async-start(), calls=%async_computation.6 | async-start | bytes 9437184 | tf_op jit(solution)/shard_map/all_gather | solution.py:419
  12.4 58.8 %all-to-all-start = ((bf16[8,128,1280]{2,1,0:T(8,128)(2,1)}), bf16[8,128,1280]{2,1,0:T(8,128)(2,1)S(1)}, u32[]{:S(2)}, u32[]{:S(2)}) async-start(bf16[8,128,1280]{2,1,0:T(8,128)(2,1)} %pack.1), calls=%async_computation | async-start | bytes 5242880 | tf_op jit(solution)/shard_map/all_to_all | solution.py:418
  19.2 129.5 %reduce-scatter.2.cloned.1.call-start = ((), (), s32[]{:S(2)}) async-start(), calls=%async_computation.5 | async-start | bytes 4423680 | tf_op jit(solution)/shard_map/reduce_scatter | solution.py:426
  84.7 1.2 copy-start
  103.3 57.9 %copy-start.2 = (f32[128,768]{1,0:T(8,128)S(1)}, f32[128,768]{1,0:T(8,128)}, u32[]{:S(2)}) copy-start(f32[128,768]{1,0:T(8,128)} %w_ref.1) | copy-start | bytes 1179652
  103.3 57.9 %copy-start.3 = (f32[128,768]{1,0:T(8,128)S(1)}, f32[128,768]{1,0:T(8,128)}, u32[]{:S(2)}) copy-start(f32[128,768]{1,0:T(8,128)} %m_ref.1) | copy-start | bytes 1179652
  103.3 57.9 %copy-start.4 = (f32[128,768]{1,0:T(8,128)S(1)}, f32[128,768]{1,0:T(8,128)}, u32[]{:S(2)}) copy-start(f32[128,768]{1,0:T(8,128)} %v_ref.1) | copy-start | bytes 1179652
  103.3 15.8 %collective-permute-start.3 = (bf16[8,48,768]{2,1,0:T(8,128)(2,1)}, bf16[8,48,768]{2,1,0:T(8,128)(2,1)S(1)}, u32[]{:S(2)}, u32[]{:S(2)}) collective-permute-start(bf16[8,48,768]{2,1,0:T(8,128)(2,1)} %get-tuple-element.15), channel_id=1, source_target_pairs={{0,64},{64,128},{128,192},{192,0},{1,65},{65,129},{129,193},{193,1... | collective-permute-start | bytes 1769480 | tf_op jit(solution)/shard_map/ppermute | solution.py:407
  103.8 28.5 %collective-permute-start.4 = (bf16[8,48,768]{2,1,0:T(8,128)(2,1)}, bf16[8,48,768]{2,1,0:T(8,128)(2,1)S(1)}, u32[]{:S(2)}, u32[]{:S(2)}) collective-permute-start(bf16[8,48,768]{2,1,0:T(8,128)(2,1)} %get-tuple-element.16), channel_id=1, source_target_pairs={{0,128},{64,192},{128,0},{192,64},{1,129},{65,193},{129,1},{193,65... | collective-permute-start | bytes 1769480 | tf_op jit(solution)/shard_map/ppermute | solution.py:407
  106.2 26.1 %collective-permute-start.5 = (bf16[8,48,768]{2,1,0:T(8,128)(2,1)}, bf16[8,48,768]{2,1,0:T(8,128)(2,1)S(1)}, u32[]{:S(2)}, u32[]{:S(2)}) collective-permute-start(bf16[8,48,768]{2,1,0:T(8,128)(2,1)} %get-tuple-element.17), channel_id=1, source_target_pairs={{0,192},{64,0},{128,64},{192,128},{1,193},{65,1},{129,65},{193,129... | collective-permute-start | bytes 1769480 | tf_op jit(solution)/shard_map/ppermute | solution.py:407
  119.1 13.3 %copy-start.5 = (bf16[8,48,768]{2,1,0:T(8,128)(2,1)}, bf16[8,48,768]{2,1,0:T(8,128)(2,1)S(1)}, u32[]{:S(2)}) copy-start(bf16[8,48,768]{2,1,0:T(8,128)(2,1)S(1)} %collective-permute-done.3.p1) | copy-start | bytes 1769476
  132.3 0.9 copy-start.6
  132.4 0.9 copy-start.7
  137.0 24.2 %all-to-all-start.1 = ((bf16[8,48,768]{2,1,0:T(8,128)(2,1)}), bf16[8,48,768]{2,1,0:T(8,128)(2,1)S(1)}, u32[]{:S(2)}, u32[]{:S(2)}) async-start(bf16[8,48,768]{2,1,0:T(8,128)(2,1)} %fold.1), calls=%async_computation.2 | async-start | bytes 1179648 | tf_op jit(solution)/shard_map/all_to_all | solution.py:428
  144.2 59.1 %all-gather.9.cloned.1.call-start = ((), (), s32[]{:S(2)}) async-start(), calls=%async_computation.7 | async-start | bytes 2211840 | tf_op jit(solution)/shard_map/all_gather | solution.py:439
  149.8 11.3 %collective-permute-start = (bf16[80,768]{1,0:T(8,128)(2,1)S(1)}, bf16[80,768]{1,0:T(8,128)(2,1)S(1)}, u32[]{:S(2)}, u32[]{:S(2)}) collective-permute-start(bf16[80,768]{1,0:T(8,128)(2,1)S(1)} %get-tuple-element.26), channel_id=1, source_target_pairs={{0,64},{64,128},{128,192},{192,0},{1,65},{65,129},{129,193},{193,1... | collective-permute-start | bytes 368648 | tf_op jit(solution)/shard_map/ppermute | solution.py:407
  151.1 10.1 %collective-permute-start.1 = (bf16[80,768]{1,0:T(8,128)(2,1)S(1)}, bf16[80,768]{1,0:T(8,128)(2,1)S(1)}, u32[]{:S(2)}, u32[]{:S(2)}) collective-permute-start(bf16[80,768]{1,0:T(8,128)(2,1)S(1)} %get-tuple-element.25), channel_id=1, source_target_pairs={{0,128},{64,192},{128,0},{192,64},{1,129},{65,193},{129,1},{193,65... | collective-permute-start | bytes 368648 | tf_op jit(solution)/shard_map/ppermute | solution.py:407
  153.5 7.7 %collective-permute-start.2 = (bf16[80,768]{1,0:T(8,128)(2,1)S(1)}, bf16[80,768]{1,0:T(8,128)(2,1)S(1)}, u32[]{:S(2)}, u32[]{:S(2)}) collective-permute-start(bf16[80,768]{1,0:T(8,128)(2,1)S(1)} %get-tuple-element.24), channel_id=1, source_target_pairs={{0,192},{64,0},{128,64},{192,128},{1,193},{65,1},{129,65},{193,129... | collective-permute-start | bytes 368648 | tf_op jit(solution)/shard_map/ppermute | solution.py:407
  174.3 18.6 %all-to-all-start.3 = ((f32[32,8,128]{2,1,0:T(8,128)}), f32[32,8,128]{2,1,0:T(8,128)S(1)}, u32[]{:S(2)}, u32[]{:S(2)}) async-start(f32[32,8,128]{2,1,0:T(8,128)} %broadcast_in_dim.5), calls=%async_computation.4 | async-start | bytes 262144 | tf_op jit(solution)/shard_map/all_to_all | solution.py:412
  181.9 63.8 %all-gather.11.cloned.1.call-start = ((), (), s32[]{:S(2)}) async-start(), calls=%async_computation.8 | async-start | bytes 2654208 | tf_op jit(solution)/shard_map/all_gather | solution.py:443
  181.9 6.2 %collective-permute-start.10 = (bf16[2,48,768]{2,1,0:T(8,128)(2,1)S(1)}, bf16[2,48,768]{2,1,0:T(8,128)(2,1)S(1)}, u32[]{:S(2)}, u32[]{:S(2)}) collective-permute-start(bf16[2,48,768]{2,1,0:T(8,128)(2,1)S(1)} %get-tuple-element.23.a0), channel_id=1, source_target_pairs={{0,64},{64,128},{128,192},{192,0},{1,65},{65,129},{129,193},{193,1... | collective-permute-start | bytes 442376 | tf_op jit(solution)/shard_map/ppermute | solution.py:407
  183.3 4.9 %collective-permute-start.11 = (bf16[2,48,768]{2,1,0:T(8,128)(2,1)S(1)}, bf16[2,48,768]{2,1,0:T(8,128)(2,1)S(1)}, u32[]{:S(2)}, u32[]{:S(2)}) collective-permute-start(bf16[2,48,768]{2,1,0:T(8,128)(2,1)S(1)} %get-tuple-element.23.a0), channel_id=1, source_target_pairs={{0,192},{64,0},{128,64},{192,128},{1,193},{65,1},{129,65},{193,129... | collective-permute-start | bytes 442376 | tf_op jit(solution)/shard_map/ppermute | solution.py:407
  184.7 8.3 %collective-permute-start.12 = (bf16[2,48,768]{2,1,0:T(8,128)(2,1)S(1)}, bf16[2,48,768]{2,1,0:T(8,128)(2,1)S(1)}, u32[]{:S(2)}, u32[]{:S(2)}) collective-permute-start(bf16[2,48,768]{2,1,0:T(8,128)(2,1)S(1)} %get-tuple-element.23.a0), channel_id=1, source_target_pairs={{0,128},{64,192},{128,0},{192,64},{1,129},{65,193},{129,1},{193,65... | collective-permute-start | bytes 442376 | tf_op jit(solution)/shard_map/ppermute | solution.py:407
  203.3 1.5 copy-start.1
  205.3 21.0 %collective-permute-start.6 = (bf16[8,80,768]{2,1,0:T(8,128)(2,1)S(1)}, bf16[8,80,768]{2,1,0:T(8,128)(2,1)S(1)}, u32[]{:S(2)}, u32[]{:S(2)}) collective-permute-start(bf16[8,80,768]{2,1,0:T(8,128)(2,1)S(1)} %apply_b.1.b0), channel_id=1, source_target_pairs={{0,64},{64,128},{128,192},{192,0},{1,65},{65,129},{129,193},{193,1... | collective-permute-start | bytes 2949128 | tf_op jit(solution)/shard_map/ppermute | solution.py:407
  206.6 20.6 %collective-permute-start.7 = (bf16[8,80,768]{2,1,0:T(8,128)(2,1)S(1)}, bf16[8,80,768]{2,1,0:T(8,128)(2,1)S(1)}, u32[]{:S(2)}, u32[]{:S(2)}) collective-permute-start(bf16[8,80,768]{2,1,0:T(8,128)(2,1)S(1)} %apply_b.1.b0), channel_id=1, source_target_pairs={{0,192},{64,0},{128,64},{192,128},{1,193},{65,1},{129,65},{193,129... | collective-permute-start | bytes 2949128 | tf_op jit(solution)/shard_map/ppermute | solution.py:407
  227.2 9.8 %collective-permute-start.8 = (bf16[4,80,768]{2,1,0:T(8,128)(2,1)}, bf16[4,80,768]{2,1,0:T(8,128)(2,1)}, u32[]{:S(2)}, u32[]{:S(2)}) collective-permute-start(bf16[4,80,768]{2,1,0:T(8,128)(2,1)} %slice.40), channel_id=1, source_target_pairs={{0,64},{64,128},{128,192},{192,0},{1,65},{65,129},{129,193},{193,1... | collective-permute-start | bytes 1474568 | tf_op jit(solution)/shard_map/ppermute | solution.py:407
  228.0 8.9 %collective-permute-start.9 = (bf16[4,80,768]{2,1,0:T(8,128)(2,1)}, bf16[4,80,768]{2,1,0:T(8,128)(2,1)}, u32[]{:S(2)}, u32[]{:S(2)}) collective-permute-start(bf16[4,80,768]{2,1,0:T(8,128)(2,1)} %slice.41), channel_id=1, source_target_pairs={{0,192},{64,0},{128,64},{192,128},{1,193},{65,1},{129,65},{193,129... | collective-permute-start | bytes 1474568 | tf_op jit(solution)/shard_map/ppermute | solution.py:407
Sparse Core Ops, SparseCore 0:
  9.9 77.1 all-gather.6
  95.6 53.0 reduce-scatter.1
  163.1 40.1 all-gather.8
  205.0 40.6 all-gather.10
